TPU v7x, 256 devices: a whole 4x4x8 slice. The times are simulated.
256 devices in a mesh: ctx: 32 (over y, x, core), head: 8 (over z).
Axes of the slice: x: 4, y: 4, z: 8, core: 2. Of those that a mesh axis runs over, the one named last changes fastest.
Arguments:
- hits_in: bfloat16 [32768, 1024], P(('ctx', 'head')), may hold values from -32 to 32
- w_query: bfloat16 [1024, 512], replicated, may hold values from -0.25 to 0.25
- w_key: bfloat16 [1024, 512], replicated, may hold values from -0.25 to 0.25
- w_value: bfloat16 [1024, 512], replicated, may hold values from -0.1875 to 0.1875
- w_out: bfloat16 [512, 1024], replicated, may hold values from -0.5 to 0.5
- grad_y: bfloat16 [32768, 1024], P(('ctx', 'head')), may hold values from -6 to 6
- block_cell: int32 [256], replicated, may hold values from 0 to 255, each once
- cell_mask: int32 [256, 256], replicated, may hold values from 0 to 1, as said below
Outputs:
- layer_out: bfloat16 [32768, 1024], P(('ctx', 'head'))
- grad_hits: bfloat16 [32768, 1024], P(('ctx', 'head'))
Inputs may be any that keep to these rules, and one draw needn't show every extreme that they name: `cell_mask`: entries are 0 or 1; every cell may attend to itself; no row and no column holds more than 21 ones. `block_cell`: each cell is named by exactly one block.
All inputs are finite; a program needn't handle non-finite values.
Results may differ from a plain program's by a relative error of at most 0.03.
The roundings to bfloat16 on the way count: a program that leaves them out, or rounds other values in their place, can miss the bound.
Values may be sent and summed in bfloat16 or wider, within the bound.
No kernel may reach another device: no remote copies, remote signals or barrier semaphores. Data moves between devices by JAX's collectives and lax.ppermute only.
A program may use at most 192 MiB of HBM per device.

v0:
```python
import jax
import jax.numpy as jnp
from jax import lax
from jax.sharding import PartitionSpec as P

HEADS = 8
HEAD_DIM = 64
BLOCK = 128
KB_MAX = 21


def block_allowed(block_cell, cell_mask):
    amount = block_cell.shape[0]
    onehot = (block_cell[:, None] == jnp.arange(amount, dtype=jnp.int32)[None, :]).astype(
        jnp.float32
    )
    mask_table = cell_mask.astype(jnp.float32)
    picked = jnp.dot(onehot, mask_table, precision=lax.Precision.HIGHEST)
    return jnp.dot(picked, onehot.T, precision=lax.Precision.HIGHEST)


def block_lists(mask_rows):
    block_total = mask_rows.shape[1]
    is_live = mask_rows > 0.5
    slot_rank = jnp.cumsum(is_live.astype(jnp.int32), axis=1) - 1
    slot_ids = jnp.arange(KB_MAX, dtype=jnp.int32)
    matched = is_live[:, None, :] & (slot_rank[:, None, :] == slot_ids[None, :, None])
    positions = jnp.arange(block_total, dtype=jnp.int32)
    indices = jnp.sum(jnp.where(matched, positions[None, None, :], 0), axis=2)
    present = jnp.any(matched, axis=2)
    return (indices, present)


def pick_blocks(array, indices):
    block_total = array.shape[0] // BLOCK
    shaped = array.reshape((block_total, BLOCK) + array.shape[1:])
    chosen = shaped[indices]
    return chosen.reshape((indices.shape[0], indices.shape[1] * BLOCK) + array.shape[1:])


def body(hits_in, w_query, w_key, w_value, w_out, grad_y, block_cell, cell_mask):
    score_scale = HEAD_DIM ** (-0.5)
    groups = lax.axis_size("head")
    row_count = hits_in.shape[0]
    hit_dev = row_count * groups
    heads_dev = HEADS // groups
    width_dev = heads_dev * HEAD_DIM
    own_blocks = hit_dev // BLOCK
    query_rows = jnp.dot(hits_in, w_query, preferred_element_type=jnp.float32).astype(jnp.bfloat16)
    key_rows = jnp.dot(hits_in, w_key, preferred_element_type=jnp.float32).astype(jnp.bfloat16)
    value_rows = jnp.dot(hits_in, w_value, preferred_element_type=jnp.float32).astype(jnp.bfloat16)
    queries, keys, values = (
        lax.all_to_all(query_rows, "head", split_axis=1, concat_axis=0, tiled=True),
        lax.all_to_all(key_rows, "head", split_axis=1, concat_axis=0, tiled=True),
        lax.all_to_all(value_rows, "head", split_axis=1, concat_axis=0, tiled=True),
    )
    pair_rows = jnp.concatenate([keys, values], axis=1)
    gathered = lax.all_gather(pair_rows, "ctx", axis=0, tiled=True)
    allowed = block_allowed(block_cell, cell_mask)
    first_block = lax.axis_index("ctx") * own_blocks
    own_rows = lax.dynamic_slice_in_dim(allowed, first_block, own_blocks, 0)
    key_index, key_present = block_lists(own_rows)
    picked = pick_blocks(gathered, key_index)
    key_pick = picked[:, :, :width_dev].reshape(own_blocks, -1, heads_dev, HEAD_DIM)
    value_pick = picked[:, :, width_dev:].reshape(own_blocks, -1, heads_dev, HEAD_DIM)
    query_heads = queries.reshape(own_blocks, BLOCK, heads_dev, HEAD_DIM)
    visible = jnp.repeat(key_present, BLOCK, axis=1)[:, None, None, :]
    scores = (
        jnp.einsum("bqhe,bkhe->bhqk", query_heads, key_pick, preferred_element_type=jnp.float32)
        * score_scale
    )
    row_top = jnp.max(jnp.where(visible, scores, -jnp.inf), axis=3)
    norm_sum = jnp.sum(jnp.where(visible, jnp.exp(scores - row_top[..., None]), 0.0), axis=3)
    log_norm = row_top + jnp.log(norm_sum)
    probs = jnp.where(visible, jnp.exp(scores - log_norm[..., None]), 0.0)
    probs_low = probs.astype(jnp.bfloat16)
    attended = jnp.einsum(
        "bhqk,bkhe->bqhe", probs_low, value_pick, preferred_element_type=jnp.float32
    ).astype(jnp.bfloat16)
    out_rows = lax.all_to_all(
        attended.reshape(hit_dev, width_dev), "head", split_axis=0, concat_axis=1, tiled=True
    )
    layer_out = jnp.dot(out_rows, w_out, preferred_element_type=jnp.float32).astype(jnp.bfloat16)
    grad_rows = jnp.dot(grad_y, w_out.T, preferred_element_type=jnp.float32).astype(jnp.bfloat16)
    grad_flat = lax.all_to_all(grad_rows, "head", split_axis=1, concat_axis=0, tiled=True)
    grad_heads = grad_flat.reshape(own_blocks, BLOCK, heads_dev, HEAD_DIM)
    row_delta = jnp.sum(grad_heads.astype(jnp.float32) * attended.astype(jnp.float32), axis=3)
    delta_heads = row_delta.transpose(0, 2, 1)
    dprobs = jnp.einsum(
        "bqhe,bkhe->bhqk", grad_heads, value_pick, preferred_element_type=jnp.float32
    )
    dscores_low = (probs * (dprobs - delta_heads[..., None])).astype(jnp.bfloat16)
    grad_query_sum = (
        jnp.einsum("bhqk,bkhe->bqhe", dscores_low, key_pick, preferred_element_type=jnp.float32)
        * score_scale
    )
    grad_query = grad_query_sum.reshape(hit_dev, width_dev).astype(jnp.bfloat16)
    key_term = (
        jnp.einsum("bhqk,bqhe->bkhe", dscores_low, query_heads, preferred_element_type=jnp.float32)
        * score_scale
    )
    value_term = jnp.einsum(
        "bhqk,bqhe->bkhe", probs_low, grad_heads, preferred_element_type=jnp.float32
    )
    key_term = key_term.reshape(own_blocks * KB_MAX, BLOCK, width_dev)
    value_term = value_term.reshape(own_blocks * KB_MAX, BLOCK, width_dev)
    terms = jnp.concatenate([key_term, value_term], axis=2)
    block_total = gathered.shape[0] // BLOCK
    scattered = (
        jnp.zeros((block_total, BLOCK, 2 * width_dev), jnp.float32)
        .at[key_index.reshape(-1)]
        .add(terms)
    )
    own_grads = lax.psum_scatter(
        scattered.reshape(block_total * BLOCK, 2 * width_dev),
        "ctx",
        scatter_dimension=0,
        tiled=True,
    )
    grad_key = own_grads[:, :width_dev].astype(jnp.bfloat16)
    grad_value = own_grads[:, width_dev:].astype(jnp.bfloat16)
    query_back, key_back, value_back = (
        lax.all_to_all(grad_query, "head", split_axis=0, concat_axis=1, tiled=True),
        lax.all_to_all(grad_key, "head", split_axis=0, concat_axis=1, tiled=True),
        lax.all_to_all(grad_value, "head", split_axis=0, concat_axis=1, tiled=True),
    )
    grad_hits = jnp.dot(query_back, w_query.T, preferred_element_type=jnp.float32)
    grad_hits = grad_hits + jnp.dot(key_back, w_key.T, preferred_element_type=jnp.float32)
    grad_hits = grad_hits + jnp.dot(value_back, w_value.T, preferred_element_type=jnp.float32)
    return (layer_out, grad_hits.astype(jnp.bfloat16))


def solution(mesh):
    return jax.shard_map(
        body,
        mesh=mesh,
        in_specs=(P(("ctx", "head"), None), P(), P(), P(), P(), P(("ctx", "head"), None), P(), P()),
        out_specs=(P(("ctx", "head"), None), P(("ctx", "head"), None)),
        check_vma=False,
    )
```

profile of v0, /device:TPU:6, one launch (start us, length us, event | category | flops | bytes accessed | tf_op | source)
XLA Modules:
  0.0 434.1 jit_solution(17323915229542859029)
XLA Ops:
  9.7 8.5 %all-to-all-start = ((bf16[128,8,64]{0,2,1:T(8,128)(2,1)}), bf16[128,8,64]{0,2,1:T(8,128)(2,1)S(1)}, u32[]{:S(2)}, u32[]{:S(2)}) async-start(bf16[128,8,64]{0,2,1:T(8,128)(2,1)} %bitcast), calls=%async_computation | async-start | bytes 262144 | tf_op jit(solution)/shard_map/all_to_all | solution.py:54
  20.5 6.7 %all-to-all-done = bf16[128,8,64]{0,2,1:T(8,128)(2,1)S(1)} async-done(((bf16[128,8,64]{0,2,1:T(8,128)(2,1)}), bf16[128,8,64]{0,2,1:T(8,128)(2,1)S(1)}, u32[]{:S(2)}, u32[]{:S(2)}) %all-to-all-start) | async-done | bytes 131104 | tf_op jit(solution)/shard_map/all_to_all | solution.py:54
  27.2 3.4 all-to-all-start.1
  30.7 8.9 %all-to-all-done.1 = bf16[128,8,64]{0,2,1:T(8,128)(2,1)S(1)} async-done(((bf16[128,8,64]{0,2,1:T(8,128)(2,1)}), bf16[128,8,64]{0,2,1:T(8,128)(2,1)S(1)}, u32[]{:S(2)}, u32[]{:S(2)}) %all-to-all-start.1) | async-done | bytes 131104 | tf_op jit(solution)/shard_map/all_to_all | solution.py:55
  42.4 3.4 all-to-all-start.2
  53.0 41.8 %all-gather.2.cloned.1.call-done = bf16[32768,128]{0,1:T(8,128)(2,1)} async-done(((bf16[1024,128]{0,1:T(8,128)(2,1)}), bf16[32768,128]{0,1:T(8,128)(2,1)}) %all-gather.2.cloned.1.call-update) | async-done | bytes 8388624 | tf_op jit(solution)/shard_map/all_gather | solution.py:58
  94.8 11.9 %copy.71 = bf16[32768,128]{1,0:T(8,128)(2,1)} copy(bf16[32768,128]{0,1:T(8,128)(2,1)} %all-gather.2.cloned.1.call-done) | data formatting | bytes 16777216 | tf_op jit(solution)/shard_map/all_gather | solution.py:58
  106.6 11.1 %gather_fusion = bf16[168,128,128]{2,1,0:T(8,128)(2,1)} fusion(bf16[256,128,128]{2,1,0:T(8,128)(2,1)} %bitcast.116, s32[1024]{0:T(1024)S(1)} %pad_clamp_fusion), kind=kCustom, calls=%fused_computation | custom fusion | bytes 11010720 | tf_op jit(solution)/shard_map/gather | solution.py:37
  117.8 7.0 %all-to-all-start.4 = ((bf16[128,8,64]{0,2,1:T(8,128)(2,1)}), bf16[128,8,64]{0,2,1:T(8,128)(2,1)S(1)}, u32[]{:S(2)}, u32[]{:S(2)}) async-start(bf16[128,8,64]{0,2,1:T(8,128)(2,1)} %bitcast.17), calls=%async_computation.4 | async-start | bytes 262144 | tf_op jit(solution)/shard_map/all_to_all | solution.py:85
  125.0 4.0 select_reduce_fusion.1
  129.0 4.2 copy-done.1
  133.2 2.6 select_reduce_fusion
  135.7 11.2 %fusion.21 = (f32[8,128]{1,0:T(8,128)S(1)}, bf16[8,64,128]{2,1,0:T(8,128)(2,1)}) fusion(bf16[128,8,64]{0,2,1:T(8,128)(2,1)S(1)} %all-to-all-done.4, f32[8,128,2688]{2,1,0:T(8,128)} %copy-done.1, f32[8,128]{1,0:T(8,128)S(1)} %log_add_fusion, pred[8,2688]{1,0:T(8,128)(4,1)S(1)} %broadcast_bitcast_fusion, bf16[8,2688,128]{2,1,0:T(8,128)(2,1)} %bitcast.118), kind=kOutput, calls=%fused_computation.31 | convolution fusion | flops 363658240 | bytes 16806912 | tf_op jit(solution)/shard_map/bhqk,bkhe->bqhe/dot_general | solution.py:77
  147.0 8.8 %multiply_convert_fusion = bf16[8,128,2688]{2,1,0:T(8,128)(2,1)S(1)} fusion(f32[8,128,2688]{2,1,0:T(8,128)} %copy-done.1, f32[8,128]{1,0:T(8,128)S(1)} %get-tuple-element.8, f32[8,128]{1,0:T(8,128)S(1)} %log_add_fusion, pred[8,2688]{1,0:T(8,128)(4,1)S(1)} %broadcast_bitcast_fusion, bf16[8,2688,128]{2,1,0:T(8,128)(2,1)} %bitcast.119, ...), kind=kOutput, calls=%fused_computation.3 | convolution fusion | flops 368836608 | bytes 22180864 | tf_op jit(solution)/shard_map/bqhe,bkhe->bhqk/dot_general | solution.py:89
  159.1 5.6 %copy.78 = f32[8,2688,1,64]{1,0,3,2:T(8,128)} copy(f32[8,2688,1,64]{1,3,0,2:T(8,128)S(1)} %multiply_bitcast_fusion) | data formatting | bytes 11010048 | tf_op jit(solution)/shard_map/mul | solution.py:99
  164.7 6.7 %reshape.206 = f32[168,128,64]{1,0,2:T(8,128)} reshape(f32[8,2688,1,64]{1,0,3,2:T(8,128)} %copy.78) | data formatting | bytes 11010048 | tf_op jit(solution)/shard_map/reshape | solution.py:105
  171.4 5.5 %convolution_bitcast_fusion = f32[8,2688,1,64]{1,3,0,2:T(8,128)S(1)} fusion(f32[8,128,2688]{2,1,0:T(8,128)} %copy-done.1, f32[8,128]{1,0:T(8,128)S(1)} %log_add_fusion, pred[8,2688]{1,0:T(8,128)(4,1)S(1)} %broadcast_bitcast_fusion, bf16[128,8,64]{0,2,1:T(8,128)(2,1)S(1)} %all-to-all-done.4), kind=kOutput, calls=%fused_computation.9 | convolution fusion | flops 363331584 | bytes 16671744 | tf_op jit(solution)/shard_map/bhqk,bqhe->bkhe/dot_general | solution.py:102
  176.9 5.6 %copy.79 = f32[8,2688,1,64]{1,0,3,2:T(8,128)} copy(f32[8,2688,1,64]{1,3,0,2:T(8,128)S(1)} %convolution_bitcast_fusion) | data formatting | bytes 11010048 | tf_op jit(solution)/shard_map/bhqk,bqhe->bkhe/transpose | solution.py:102
  182.5 6.7 %reshape.207 = f32[168,128,64]{1,0,2:T(8,128)} reshape(f32[8,2688,1,64]{1,0,3,2:T(8,128)} %copy.79) | data formatting | bytes 11010048 | tf_op jit(solution)/shard_map/reshape | solution.py:106
  189.1 9.1 %pad_maximum_fusion = f32[168,128,128]{1,0,2:T(8,128)} fusion(f32[168,128,64]{1,0,2:T(8,128)} %reshape.207, f32[168,128,64]{1,0,2:T(8,128)} %reshape.206), kind=kLoop, calls=%fused_computation.2 | loop fusion | flops 2752512 | bytes 22020096 | tf_op jit(solution)/shard_map/concatenate | solution.py:107
  198.2 12.2 %copy.80 = f32[168,128,128]{2,1,0:T(8,128)} copy(f32[168,128,128]{1,0,2:T(8,128)} %pad_maximum_fusion) | data formatting | bytes 22020096 | tf_op jit(solution)/shard_map/concatenate | solution.py:107
  210.4 7.8 %broadcast_in_dim.59 = f32[256,128,128]{2,1,0:T(8,128)} broadcast(f32[]{:T(128)} %constant.7.clone.1), dimensions={} | broadcast | bytes 16777220 | tf_op jit(solution)/shard_map/broadcast_in_dim | solution.py:110
  218.3 36.4 %scatter_fusion = f32[256,128,128]{2,1,0:T(8,128)} fusion(f32[256,128,128]{2,1,0:T(8,128)} %broadcast_in_dim.59, s32[168]{0:T(256)S(1)} %bitcast.125, f32[168,128,128]{2,1,0:T(8,128)} %copy.80), kind=kCustom, calls=%fused_computation.1 | custom fusion | flops 2752512 | bytes 33030816 | tf_op jit(solution)/shard_map/scatter-add | solution.py:112
  254.7 17.4 %copy.81 = f32[32768,128]{0,1:T(8,128)} copy(f32[32768,128]{1,0:T(8,128)} %bitcast.115) | data formatting | bytes 33554432 | tf_op jit(solution)/shard_map/reshape | solution.py:115
  272.2 6.5 %fusion.18 = bf16[8,128,64]{1,2,0:T(8,128)(2,1)S(1)} fusion(bf16[8,128,2688]{2,1,0:T(8,128)(2,1)} %copy-done.2, bf16[8,2688,128]{2,1,0:T(8,128)(2,1)} %bitcast.120), kind=kOutput, calls=%fused_computation.28 | convolution fusion | flops 352452608 | bytes 11141120 | tf_op jit(solution)/shard_map/bhqk,bkhe->bqhe/dot_general | solution.py:94
  278.7 15.9 %all_to_all.143 = bf16[8,128,64]{1,2,0:T(8,128)(2,1)S(1)} all-to-all(bf16[8,128,64]{1,2,0:T(8,128)(2,1)S(1)} %fusion.18), channel_id=1, replica_groups=mesh['ctx'=32,'head'=8] {'head'}, dimensions={0} | all-to-all | bytes 262144 | tf_op jit(solution)/shard_map/all_to_all | solution.py:123
  294.6 3.4 all-to-all-start.3
  299.2 95.3 %reduce-scatter.2.cloned.1.call-done = f32[1024,128]{0,1:T(8,128)} async-done(((f32[32768,128]{0,1:T(8,128)}), f32[1024,128]{0,1:T(8,128)}) %reduce-scatter.2.cloned.1.call-update) | async-done | bytes 524304 | tf_op jit(solution)/shard_map/reduce_scatter | solution.py:114
  396.4 7.0 %all-to-all-start.6 = ((bf16[8,128,64]{1,2,0:T(8,128)(2,1)}), bf16[8,128,64]{1,2,0:T(8,128)(2,1)S(1)}, u32[]{:S(2)}, u32[]{:S(2)}) async-start(bf16[8,128,64]{1,2,0:T(8,128)(2,1)} %bitcast.114), calls=%async_computation.7 | async-start | bytes 262144 | tf_op jit(solution)/shard_map/all_to_all | solution.py:124
  405.1 7.4 %all-to-all-done.6 = bf16[8,128,64]{1,2,0:T(8,128)(2,1)S(1)} async-done(((bf16[8,128,64]{1,2,0:T(8,128)(2,1)}), bf16[8,128,64]{1,2,0:T(8,128)(2,1)S(1)}, u32[]{:S(2)}, u32[]{:S(2)}) %all-to-all-start.6) | async-done | bytes 131104 | tf_op jit(solution)/shard_map/all_to_all | solution.py:124
  412.4 3.4 all-to-all-start.7
  417.4 7.4 %all-to-all-done.7 = bf16[8,128,64]{1,2,0:T(8,128)(2,1)S(1)} async-done(((bf16[8,128,64]{1,2,0:T(8,128)(2,1)}), bf16[8,128,64]{1,2,0:T(8,128)(2,1)S(1)}, u32[]{:S(2)}, u32[]{:S(2)}) %all-to-all-start.7) | async-done | bytes 131104 | tf_op jit(solution)/shard_map/all_to_all | solution.py:125
  (55 shorter events, 27.2 us)
Async XLA Ops:
  7.2 33.2 %copy-start = (bf16[1024,512]{1,0:T(8,128)(2,1)S(1)}, bf16[1024,512]{1,0:T(8,128)(2,1)}, u32[]{:S(2)}) copy-start(bf16[1024,512]{1,0:T(8,128)(2,1)} %param.9) | copy-start | bytes 3145732
  9.7 17.6 %all-to-all-start = ((bf16[128,8,64]{0,2,1:T(8,128)(2,1)}), bf16[128,8,64]{0,2,1:T(8,128)(2,1)S(1)}, u32[]{:S(2)}, u32[]{:S(2)}) async-start(bf16[128,8,64]{0,2,1:T(8,128)(2,1)} %bitcast), calls=%async_computation | async-start | bytes 262144 | tf_op jit(solution)/shard_map/all_to_all | solution.py:54
  27.2 12.4 %all-to-all-start.1 = ((bf16[128,8,64]{0,2,1:T(8,128)(2,1)}), bf16[128,8,64]{0,2,1:T(8,128)(2,1)S(1)}, u32[]{:S(2)}, u32[]{:S(2)}) async-start(bf16[128,8,64]{0,2,1:T(8,128)(2,1)} %bitcast.2), calls=%async_computation.1 | async-start | bytes 262144 | tf_op jit(solution)/shard_map/all_to_all | solution.py:55
  30.6 64.2 %all-gather.2.cloned.1.call-start = ((), (), s32[]{:S(2)}) async-start(), calls=%async_computation.9 | async-start | bytes 8650752 | tf_op jit(solution)/shard_map/all_gather | solution.py:58
  42.4 75.4 %all-to-all-start.2 = ((bf16[128,8,64]{0,2,1:T(8,128)(2,1)}), bf16[128,8,64]{0,2,1:T(8,128)(2,1)S(1)}, u32[]{:S(2)}, u32[]{:S(2)}) async-start(bf16[128,8,64]{0,2,1:T(8,128)(2,1)} %bitcast.10), calls=%async_computation.2 | async-start | bytes 262144 | tf_op jit(solution)/shard_map/all_to_all | solution.py:53
  117.8 18.0 %all-to-all-start.4 = ((bf16[128,8,64]{0,2,1:T(8,128)(2,1)}), bf16[128,8,64]{0,2,1:T(8,128)(2,1)S(1)}, u32[]{:S(2)}, u32[]{:S(2)}) async-start(bf16[128,8,64]{0,2,1:T(8,128)(2,1)} %bitcast.17), calls=%async_computation.4 | async-start | bytes 262144 | tf_op jit(solution)/shard_map/all_to_all | solution.py:85
  124.8 269.8 %reduce-scatter.2.cloned.1.call-start = ((), (), s32[]{:S(2)}) async-start(), calls=%async_computation.10 | async-start | bytes 17301504 | tf_op jit(solution)/shard_map/reduce_scatter | solution.py:114
  129.0 4.2 copy-start.1
  155.8 2.5 copy-start.2
  272.1 131.2 %copy-start.3 = (bf16[512,1024]{1,0:T(8,128)(2,1)S(1)}, bf16[512,1024]{1,0:T(8,128)(2,1)}, u32[]{:S(2)}) copy-start(bf16[512,1024]{1,0:T(8,128)(2,1)} %param.12) | copy-start | bytes 3145732
  272.2 143.7 %copy-start.4 = (bf16[1024,512]{1,0:T(8,128)(2,1)S(1)}, bf16[1024,512]{1,0:T(8,128)(2,1)}, u32[]{:S(2)}) copy-start(bf16[1024,512]{1,0:T(8,128)(2,1)} %param.10) | copy-start | bytes 3145732
  294.6 101.8 %all-to-all-start.3 = ((bf16[8,128,64]{1,2,0:T(8,128)(2,1)}), bf16[8,128,64]{1,2,0:T(8,128)(2,1)S(1)}, u32[]{:S(2)}, u32[]{:S(2)}) async-start(bf16[8,128,64]{1,2,0:T(8,128)(2,1)} %bitcast.14), calls=%async_computation.3 | async-start | bytes 262144 | tf_op jit(solution)/shard_map/all_to_all | solution.py:80
  396.4 16.1 %all-to-all-start.6 = ((bf16[8,128,64]{1,2,0:T(8,128)(2,1)}), bf16[8,128,64]{1,2,0:T(8,128)(2,1)S(1)}, u32[]{:S(2)}, u32[]{:S(2)}) async-start(bf16[8,128,64]{1,2,0:T(8,128)(2,1)} %bitcast.114), calls=%async_computation.7 | async-start | bytes 262144 | tf_op jit(solution)/shard_map/all_to_all | solution.py:124
  412.4 12.4 %all-to-all-start.7 = ((bf16[8,128,64]{1,2,0:T(8,128)(2,1)}), bf16[8,128,64]{1,2,0:T(8,128)(2,1)S(1)}, u32[]{:S(2)}, u32[]{:S(2)}) async-start(bf16[8,128,64]{1,2,0:T(8,128)(2,1)} %bitcast.113), calls=%async_computation.8 | async-start | bytes 262144 | tf_op jit(solution)/shard_map/all_to_all | solution.py:125
Sparse Core Ops, SparseCore 0:
  40.5 54.2 all-gather.1
  272.3 122.2 reduce-scatter.1
where the time goes:
time: 436 us; the launch traced here: 434 us
  waiting for transfers between devices  168 us (39%)
  local copies, waits for them, and re-layouts  96.6 us (22%)
  matrix products  51.9 us (12%)
  other arithmetic  51.5 us (12%)
  starting transfers between devices  36.2 us (8%)
  blocking collectives  15.9 us (4%)
  between operations  14.3 us (3%)
    reduce_scatter x1, waiting for transfers between devices, body(): lax.psum_scatter(scattered.reshape(block_total * BLOCK, 2 * width_dev), '...  95.3 us
    all_gather x1, waiting for transfers between devices, body(): gathered = lax.all_gather(pair_rows, 'ctx', axis=0, tiled=True)  41.8 us
    scatter-add x1, other arithmetic, body(): scattered = jnp.zeros((block_total, BLOCK, 2 * width_dev), jnp.float32).a...  36.4 us
    reshape x1, local copies, waits for them, and re-layouts, body(): scattered.reshape(block_total * BLOCK, 2 * width_dev)  17.4 us
    all_to_all x1, blocking collectives, body(): lax.all_to_all(grad_query, 'head', split_axis=0, concat_axis=1, tiled=True)  15.9 us
    concatenate x1, local copies, waits for them, and re-layouts, body(): terms = jnp.concatenate([key_term, value_term], axis=2)  12.2 us
    all_gather x1, local copies, waits for them, and re-layouts, body(): gathered = lax.all_gather(pair_rows, 'ctx', axis=0, tiled=True)  11.9 us
    dot_general x1, matrix products, body(): jnp.einsum('bhqk,bkhe->bqhe', probs_low, value_pick, preferred_element_ty...  11.2 us
  transfers between devices with their start and end apart: 9, of which 6 were waited for; matrix products, arithmetic and copies ran while one was open for 12% of the time, Pallas kernels for 0%

commit v1 on v0

v1 whole, which is shorter than its diff:
```python
import functools

import jax
import jax.numpy as jnp
from jax import lax
from jax.experimental import pallas as pl
from jax.experimental.pallas import tpu as pltpu
from jax.sharding import PartitionSpec as P

HEADS = 8
HEAD_DIM = 64
BLOCK = 128
KB_MAX = 21
CHUNK = 7
SCALE = HEAD_DIM ** (-0.5)
F32 = jnp.float32
BF16 = jnp.bfloat16
VMEM_LIMIT = 56 * 1024 * 1024

VMEM = pltpu.VMEM
NT = (((1,), (1,)), ((), ()))


def low_lanes(shape):
    return lax.broadcasted_iota(jnp.int32, shape, len(shape) - 1) < HEAD_DIM


def pack_heads(left, right, out_ref):
    for h in range(HEADS):
        cols = slice(h * HEAD_DIM, (h + 1) * HEAD_DIM)
        out_ref[h] = jnp.concatenate([left[:, cols], right[:, cols]], axis=1)


def project_kv_kernel(x_ref, wk_ref, wv_ref, out_ref):
    x = x_ref[...]
    k = jnp.dot(x, wk_ref[...], preferred_element_type=F32).astype(BF16)
    v = jnp.dot(x, wv_ref[...], preferred_element_type=F32).astype(BF16)
    pack_heads(k, v, out_ref)


def project_qd_kernel(x_ref, gy_ref, wq_ref, wo_ref, out_ref):
    q = jnp.dot(x_ref[...], wq_ref[...], preferred_element_type=F32).astype(BF16)
    q = q * jnp.asarray(SCALE, BF16)
    d = lax.dot_general(gy_ref[...], wo_ref[...], NT, preferred_element_type=F32).astype(BF16)
    pack_heads(q, d, out_ref)


def local_call(kernel, out_shape, n_in, **kw):
    return pl.pallas_call(
        kernel,
        out_shape=out_shape,
        in_specs=[pl.BlockSpec(memory_space=VMEM)] * n_in,
        out_specs=jax.tree.map(lambda _: pl.BlockSpec(memory_space=VMEM), out_shape),
        compiler_params=pltpu.CompilerParams(vmem_limit_bytes=VMEM_LIMIT),
        **kw,
    )


def load_pieces(pieces, dst, sems):
    copies = []
    at = 0
    for i, piece in enumerate(pieces):
        rows = piece.shape[0]
        copies.append(pltpu.make_async_copy(piece, dst.at[pl.ds(at, rows)], sems.at[i]))
        at += rows
    for copy in copies:
        copy.start()
    for copy in copies:
        copy.wait()


def query_kernel(n_pieces, blocks, pos_ref, cnt_ref, qd_ref, *rest):
    pieces = rest[:n_pieces]
    out_ref, stat_ref, kv_all, kv_pick, sems = rest[n_pieces:]
    load_pieces(pieces, kv_all, sems)
    span = KB_MAX * BLOCK

    def one(b, carry):
        for s in range(KB_MAX):
            at = pl.multiple_of(pos_ref[b, s] * BLOCK, BLOCK)
            kv_pick[pl.ds(s * BLOCK, BLOCK), :] = kv_all[pl.ds(at, BLOCK), :]
        rows = pl.ds(pl.multiple_of(b * BLOCK, BLOCK), BLOCK)
        qd = qd_ref[rows, :]
        low = low_lanes((BLOCK, 2 * HEAD_DIM))
        zero = jnp.zeros_like(qd)
        d_part = jnp.where(low, zero, qd)
        both = jnp.concatenate([jnp.where(low, qd, zero), d_part], axis=0)
        kv = kv_pick[...]
        prod = lax.dot_general(both, kv, NT, preferred_element_type=F32)
        slot = lax.broadcasted_iota(jnp.int32, (1, span), 1) // BLOCK
        scores = jnp.where(slot < cnt_ref[b], prod[:BLOCK], -1e30)
        top = jnp.max(scores, axis=1, keepdims=True)
        raw = jnp.exp(scores - top)
        total = jnp.sum(raw, axis=1, keepdims=True)
        probs = raw * (1.0 / total)
        probs_low = probs.astype(BF16)
        att = jnp.dot(probs_low, kv, preferred_element_type=F32)
        att_low = att.astype(BF16)
        delta = jnp.sum(d_part.astype(F32) * att_low.astype(F32), axis=1, keepdims=True)
        dscores = (probs * (prod[BLOCK:] - delta)).astype(BF16)
        gq = jnp.dot(dscores, kv, preferred_element_type=F32) * SCALE
        out_ref[b] = jnp.where(low, gq, att).astype(BF16)
        log_norm = top + jnp.log(total)
        lane = lax.broadcasted_iota(jnp.int32, (BLOCK, BLOCK), 1)
        tile = jnp.where(lane == 0, log_norm, delta)
        stat_ref[b] = jnp.transpose(tile)[:8]
        return carry

    lax.fori_loop(0, blocks, one, 0)


def query_side(pos, cnt, qd, pieces, blocks):
    n = len(pieces)
    rows = sum(p.shape[0] for p in pieces)
    smem = pl.BlockSpec(memory_space=pltpu.SMEM)
    vmem = pl.BlockSpec(memory_space=VMEM)
    return pl.pallas_call(
        functools.partial(query_kernel, n, blocks),
        out_shape=(
            jax.ShapeDtypeStruct((blocks, BLOCK, 2 * HEAD_DIM), BF16),
            jax.ShapeDtypeStruct((blocks, 8, BLOCK), F32),
        ),
        in_specs=[smem, smem, vmem] + [pl.BlockSpec(memory_space=pl.ANY)] * n,
        out_specs=(vmem, vmem),
        scratch_shapes=[
            pltpu.VMEM((rows, 2 * HEAD_DIM), BF16),
            pltpu.VMEM((KB_MAX * BLOCK, 2 * HEAD_DIM), BF16),
            pltpu.SemaphoreType.DMA((n,)),
        ],
        compiler_params=pltpu.CompilerParams(vmem_limit_bytes=VMEM_LIMIT),
        name="query_side",
    )(pos, cnt, qd, *pieces)


def key_kernel(n_pieces, blocks, pos_ref, cnt_ref, kv_ref, lse_ref, delta_ref, *rest):
    pieces = rest[:n_pieces]
    out_ref, qd_all, sems = rest[n_pieces:]
    load_pieces(pieces, qd_all, sems)

    def one(b, carry):
        rows = pl.ds(pl.multiple_of(b * BLOCK, BLOCK), BLOCK)
        kv = kv_ref[rows, :]
        low = low_lanes((BLOCK, 2 * HEAD_DIM))
        zero = jnp.zeros_like(kv)
        both = jnp.concatenate([jnp.where(low, kv, zero), jnp.where(low, zero, kv)], axis=0)
        cnt = cnt_ref[b]

        def chunk(c, acc):
            qds, lses, deltas = [], [], []
            for i in range(CHUNK):
                s = c * CHUNK + i
                at = pos_ref[b, s]
                qds.append(qd_all[pl.ds(pl.multiple_of(at * BLOCK, BLOCK), BLOCK), :])
                lses.append(jnp.where(s < cnt, lse_ref[pl.ds(at, 1), :], 1e30))
                deltas.append(delta_ref[pl.ds(at, 1), :])
            qd = jnp.concatenate(qds, axis=0)
            prod = lax.dot_general(both, qd, NT, preferred_element_type=F32)
            probs = jnp.exp(prod[:BLOCK] - jnp.concatenate(lses, axis=1))
            dscores = probs * (prod[BLOCK:] - jnp.concatenate(deltas, axis=1))
            left = jnp.concatenate([probs.astype(BF16), dscores.astype(BF16)], axis=0)
            return acc + jnp.dot(left, qd, preferred_element_type=F32)

        acc = lax.fori_loop(
            0, (cnt + CHUNK - 1) // CHUNK, chunk, jnp.zeros((2 * BLOCK, 2 * HEAD_DIM), F32)
        )
        out_ref[b] = jnp.where(low, acc[BLOCK:], acc[:BLOCK]).astype(BF16)
        return carry

    lax.fori_loop(0, blocks, one, 0)


def key_side(pos, cnt, kv, lse, delta, pieces, blocks):
    n = len(pieces)
    rows = sum(p.shape[0] for p in pieces)
    smem = pl.BlockSpec(memory_space=pltpu.SMEM)
    vmem = pl.BlockSpec(memory_space=VMEM)
    return pl.pallas_call(
        functools.partial(key_kernel, n, blocks),
        out_shape=jax.ShapeDtypeStruct((blocks, BLOCK, 2 * HEAD_DIM), BF16),
        in_specs=[smem, smem, vmem, vmem, vmem] + [pl.BlockSpec(memory_space=pl.ANY)] * n,
        out_specs=vmem,
        scratch_shapes=[
            pltpu.VMEM((rows, 2 * HEAD_DIM), BF16),
            pltpu.SemaphoreType.DMA((n,)),
        ],
        compiler_params=pltpu.CompilerParams(vmem_limit_bytes=VMEM_LIMIT),
        name="key_side",
    )(pos, cnt, kv, lse, delta, *pieces)


def unpack_heads(ref, left):
    cols = slice(0, HEAD_DIM) if left else slice(HEAD_DIM, 2 * HEAD_DIM)
    return jnp.concatenate([ref[h][:, cols] for h in range(HEADS)], axis=1)


def output_kernel(og_ref, wo_ref, wq_ref, out_ref, part_ref):
    att = unpack_heads(og_ref, False)
    gq = unpack_heads(og_ref, True)
    out_ref[...] = jnp.dot(att, wo_ref[...], preferred_element_type=F32).astype(BF16)
    part_ref[...] = lax.dot_general(gq, wq_ref[...], NT, preferred_element_type=F32)


def input_grad_kernel(kv_ref, part_ref, wk_ref, wv_ref, out_ref):
    gk = unpack_heads(kv_ref, True)
    gv = unpack_heads(kv_ref, False)
    total = part_ref[...] + lax.dot_general(gk, wk_ref[...], NT, preferred_element_type=F32)
    total = total + lax.dot_general(gv, wv_ref[...], NT, preferred_element_type=F32)
    out_ref[...] = total.astype(BF16)


def allowed_blocks(block_cell, cell_mask):
    amount = block_cell.shape[0]
    onehot = (block_cell[:, None] == jnp.arange(amount, dtype=jnp.int32)[None, :]).astype(BF16)
    picked = jnp.dot(onehot, cell_mask.astype(BF16), preferred_element_type=F32).astype(BF16)
    return lax.dot_general(picked, onehot, NT, preferred_element_type=F32)


def block_lists(rows, place):
    total = rows.shape[1]
    at = jnp.arange(total, dtype=jnp.int32)
    upto = (at[:, None] <= at[None, :]).astype(BF16)
    rank = jnp.dot(rows.astype(BF16), upto, preferred_element_type=F32)
    slots = jnp.arange(1, KB_MAX + 1, dtype=jnp.int32).astype(F32)
    matched = (rows[:, None, :] > 0.5) & (rank[:, None, :] == slots[None, :, None])
    picked = jnp.sum(jnp.where(matched, place[None, None, :], 0), axis=2)
    return picked, jnp.sum(rows, axis=1).astype(jnp.int32)


def exchange(x):
    return lax.all_to_all(x, "head", split_axis=0, concat_axis=0, tiled=True)


def body(hits_in, w_query, w_key, w_value, w_out, grad_y, block_cell, cell_mask):
    rows = hits_in.shape[0]
    own_blocks = HEADS * rows // BLOCK
    wide = 2 * HEAD_DIM
    packed = jax.ShapeDtypeStruct((HEADS, rows, wide), BF16)
    kv = exchange(local_call(project_kv_kernel, packed, 3)(hits_in, w_key, w_value))
    qd = exchange(local_call(project_qd_kernel, packed, 4)(hits_in, grad_y, w_query, w_out))
    kv = kv.reshape(own_blocks * BLOCK, wide)
    qd = qd.reshape(own_blocks * BLOCK, wide)
    kv_all = lax.all_gather(kv, "ctx", axis=0, tiled=True)
    qd_all = lax.all_gather(qd, "ctx", axis=0, tiled=True)

    allowed = allowed_blocks(block_cell, cell_mask)
    first = lax.axis_index("ctx") * own_blocks
    place = jnp.arange(allowed.shape[0], dtype=jnp.int32)
    lists = jnp.concatenate(
        [
            lax.dynamic_slice_in_dim(allowed, first, own_blocks, 0),
            lax.dynamic_slice_in_dim(allowed, first, own_blocks, 1).T,
        ],
        axis=0,
    )
    pos, cnt = block_lists(lists, place)

    og, stats = query_side(pos[:own_blocks], cnt[:own_blocks], qd, [kv_all], own_blocks)
    both = jnp.concatenate([stats[:, 0], stats[:, 1]], axis=1)
    both = lax.all_gather(both, "ctx", axis=0, tiled=True)
    og = exchange(og.reshape(HEADS, rows, wide))
    layer_out, part = local_call(
        output_kernel,
        (
            jax.ShapeDtypeStruct(hits_in.shape, BF16),
            jax.ShapeDtypeStruct(hits_in.shape, F32),
        ),
        3,
    )(og, w_out, w_query)
    gkv = key_side(
        pos[own_blocks:], cnt[own_blocks:], kv, both[:, :BLOCK], both[:, BLOCK:], [qd_all], own_blocks
    )
    gkv = exchange(gkv.reshape(HEADS, rows, wide))
    grad_hits = local_call(
        input_grad_kernel, jax.ShapeDtypeStruct(hits_in.shape, BF16), 4
    )(gkv, part, w_key, w_value)
    return layer_out, grad_hits


def solution(mesh):
    row = P(("ctx", "head"), None)
    return jax.shard_map(
        body,
        mesh=mesh,
        in_specs=(row, P(), P(), P(), P(), row, P(), P()),
        out_specs=(row, row),
        check_vma=False,
    )
```

time: 436 us -> 190 us (0.44)
  waiting for transfers between devices: 168 us -> 52.3 us
  local copies, waits for them, and re-layouts: 96.6 us -> 4.42 us
  other arithmetic: 51.5 us -> 0.67 us
  matrix products: 51.9 us -> 1.48 us
  Pallas kernels: 0 us -> 43.9 us
  blocking collectives: 15.9 us -> 57.5 us
  starting transfers between devices: 36.2 us -> 14.1 us
    reduce_scatter x1 -> x0, waiting for transfers between devices: 95.3 us -> none  [body(): lax.psum_scatter(scattered.reshape(block_total * BLOCK, 2 * width_dev), '...]
    dot_general x16 -> x2, matrix products: 51.9 us -> 1.48 us  [the longest x1 1.33 us: allowed_blocks(): return lax.dot_general(picked, onehot, NT, preferred_element_type=F32)]
    pallas_call x0 -> x6, Pallas kernels: none -> 43.9 us  [the longest x1 18.1 us: query_side(): pl.pallas_call(functools.partial(query_kernel, n, blocks), out_shape=(jax...]
    scatter-add x1 -> x0, other arithmetic: 36.4 us -> none  [body(): scattered = jnp.zeros((block_total, BLOCK, 2 * width_dev), jnp.float32).a...]
    reshape x4 -> x0, local copies, waits for them, and re-layouts: 30.8 us -> none  [the longest x1 17.4 us: body(): scattered.reshape(block_total * BLOCK, 2 * width_dev)]
    all_gather x0 -> x1, blocking collectives: none -> 22.6 us  [body(): both = lax.all_gather(both, 'ctx', axis=0, tiled=True)]
    all_to_all x7 -> x2, starting transfers between devices: 36 us -> 14.1 us  [exchange(): return lax.all_to_all(x, 'head', split_axis=0, concat_axis=0, tiled=True)]
    all_to_all x7 -> x2, waiting for transfers between devices: 30.4 us -> 8.75 us  [exchange(): return lax.all_to_all(x, 'head', split_axis=0, concat_axis=0, tiled=True)]
  transfers between devices with their start and end apart: 9 -> 4, of which waited for: 6 -> 3; matrix products, arithmetic and copies ran while one was open for 12% -> 3% of each run, Pallas kernels for 0% -> 20%
where the time goes in v1:
time: 190 us; the launch traced here: 189 us
  blocking collectives  57.5 us (30%)
  waiting for transfers between devices  52.3 us (28%)
  Pallas kernels  43.9 us (23%)
  starting transfers between devices  14.1 us (7%)
  between operations  14.1 us (7%)
  local copies, waits for them, and re-layouts  4.42 us (2%)
    all_to_all x2, blocking collectives, exchange(): return lax.all_to_all(x, 'head', split_axis=0, concat_axis=0, tiled=True)  34.9 us
    all_gather x1, waiting for transfers between devices, body(): kv_all = lax.all_gather(kv, 'ctx', axis=0, tiled=True)  32.3 us
    all_gather x1, blocking collectives, body(): both = lax.all_gather(both, 'ctx', axis=0, tiled=True)  22.6 us
    pallas_call x1, Pallas kernels, query_side(): pl.pallas_call(functools.partial(query_kernel, n, blocks), out_shape=(jax...  18.1 us
    all_to_all x2, starting transfers between devices, exchange(): return lax.all_to_all(x, 'head', split_axis=0, concat_axis=0, tiled=True)  14.1 us
    pallas_call x1, Pallas kernels, key_side(): pl.pallas_call(functools.partial(key_kernel, n, blocks), out_shape=jax.Sh...  13.3 us
    all_gather x1, waiting for transfers between devices, body(): qd_all = lax.all_gather(qd, 'ctx', axis=0, tiled=True)  11.2 us
    all_to_all x2, waiting for transfers between devices, exchange(): return lax.all_to_all(x, 'head', split_axis=0, concat_axis=0, tiled=True)  8.75 us
  transfers between devices with their start and end apart: 4, of which 3 were waited for; matrix products, arithmetic and copies ran while one was open for 3% of the time, Pallas kernels for 20%

profile of v1, /device:TPU:6, one launch (start us, length us, event | category | flops | bytes accessed | tf_op | source)
XLA Modules:
  0.0 188.5 jit_solution(18349386100353388675)
XLA Ops:
  7.2 0.0 all-gather.3.cloned.1.call-start
  7.2 2.8 %shard_map.96 = bf16[8,128,128]{2,1,0:T(8,128)(2,1)} custom-call(bf16[128,1024]{1,0:T(8,128)(2,1)} %x_ref.3, bf16[1024,512]{1,0:T(8,128)(2,1)} %wk_ref.3, bf16[1024,512]{1,0:T(8,128)(2,1)} %wv_ref.3), custom_call_target="tpu_custom_call" | custom-call | tf_op jit(solution)/shard_map/pallas_call | solution.py:238
  10.1 20.4 %all_to_all.20 = bf16[8,128,128]{2,1,0:T(8,128)(2,1)} all-to-all(bf16[8,128,128]{2,1,0:T(8,128)(2,1)} %shard_map.96), channel_id=1, replica_groups=mesh['ctx'=32,'head'=8] {'head'}, dimensions={0} | all-to-all | bytes 524288 | tf_op jit(solution)/shard_map/all_to_all | solution.py:230
  30.5 0.0 all-gather.3.cloned.1.call-update
  30.5 0.0 all-gather.5.cloned.1.call-start
  30.6 3.1 %shard_map.95 = bf16[8,128,128]{2,1,0:T(8,128)(2,1)} custom-call(bf16[128,1024]{1,0:T(8,128)(2,1)} %x_ref.3, bf16[128,1024]{1,0:T(8,128)(2,1)} %gy_ref.1, bf16[1024,512]{1,0:T(8,128)(2,1)} %wq_ref.3, bf16[512,1024]{1,0:T(8,128)(2,1)} %wo_ref.3), custom_call_target="tpu_custom_call" | custom-call | tf_op jit(solution)/shard_map/pallas_call | solution.py:239
  33.7 14.5 %all_to_all.21 = bf16[8,128,128]{2,1,0:T(8,128)(2,1)} all-to-all(bf16[8,128,128]{2,1,0:T(8,128)(2,1)} %shard_map.95), channel_id=1, replica_groups=mesh['ctx'=32,'head'=8] {'head'}, dimensions={0} | all-to-all | bytes 524288 | tf_op jit(solution)/shard_map/all_to_all | solution.py:230
  48.2 0.0 all-gather.5.cloned.1.call-update
  48.2 1.3 fusion
  49.6 0.1 dynamic-slice_bitcast_fusion
  49.7 0.1 copy.17
  49.8 0.1 fusion.1
  49.9 0.5 select_reduce_fusion
  50.5 0.1 fusion.12
  50.5 0.7 copy.22.pos_ref
  51.2 0.1 fusion.6
  51.3 0.7 copy.23.pos_ref
  52.0 0.6 fusion.13
  52.6 32.3 %all-gather.3.cloned.1.call-done.rest_0_ = bf16[32768,128]{1,0:T(8,128)(2,1)} async-done(((bf16[1024,128]{1,0:T(8,128)(2,1)}), bf16[32768,128]{1,0:T(8,128)(2,1)}) %all-gather.3.cloned.1.call-update) | async-done | bytes 8388624 | tf_op jit(solution)/shard_map/all_gather | solution.py:242
  84.9 18.1 %query_side.1 = (bf16[8,128,128]{2,1,0:T(8,128)(2,1)}, f32[8,8,128]{2,1,0:T(8,128)}) custom-call(s32[8,21]{1,0:T(8,128)} %copy.22.pos_ref, s32[8]{0:T(128)} %get-tuple-element.17.cnt_ref, bf16[1024,128]{1,0:T(8,128)(2,1)} %bitcast.11, bf16[32768,128]{1,0:T(8,128)(2,1)} %all-gather.3.cloned.1.call-done.rest_0_), custom_call_target="tpu_custom_call" | custom-call | tf_op jit(solution)/shard_map/query_side/pallas_call | solution.py:117
  103.0 0.8 copy.20
  103.8 7.0 %all-to-all-start.2 = ((bf16[8,128,128]{2,1,0:T(8,128)(2,1)}), bf16[8,128,128]{2,1,0:T(8,128)(2,1)S(1)}, u32[]{:S(2)}, u32[]{:S(2)}) async-start(bf16[8,128,128]{2,1,0:T(8,128)(2,1)} %get-tuple-element.6), calls=%async_computation.2 | async-start | bytes 524288 | tf_op jit(solution)/shard_map/all_to_all | solution.py:230
  110.9 22.6 %all_gather.10 = f32[256,256]{1,0:T(8,128)S(1)} all-gather(f32[8,256]{1,0:T(8,128)S(1)} %pad_maximum_fusion.1), channel_id=1, replica_groups=mesh['ctx'=32,'head'=8] {'ctx'}, dimensions={0}, use_global_device_ids=true | all-gather | bytes 270336 | tf_op jit(solution)/shard_map/all_gather | solution.py:259
  133.5 0.7 fusion.11
  134.2 11.2 %all-gather.5.cloned.1.call-done.rest_0_ = bf16[32768,128]{1,0:T(8,128)(2,1)} async-done(((bf16[1024,128]{1,0:T(8,128)(2,1)}), bf16[32768,128]{1,0:T(8,128)(2,1)}) %all-gather.5.cloned.1.call-update) | async-done | bytes 8388624 | tf_op jit(solution)/shard_map/all_gather | solution.py:243
  145.4 13.3 %key_side.1 = bf16[8,128,128]{2,1,0:T(8,128)(2,1)} custom-call(s32[8,21]{1,0:T(8,128)} %copy.23.pos_ref, s32[8]{0:T(128)} %get-tuple-element.16.cnt_ref, bf16[1024,128]{1,0:T(8,128)(2,1)} %bitcast.9, f32[256,128]{1,0:T(8,128)} %get-tuple-element.11.lse_ref, f32[256,128]{1,0:T(8,128)} %get-tuple-element.10.delta_ref, ...), custom_call_target="tpu_custom_call" | custom-call | tf_op jit(solution)/shard_map/key_side/pallas_call | solution.py:177
  158.8 0.0 copy-start
  158.8 7.0 %all-to-all-start.3 = ((bf16[8,128,128]{2,1,0:T(8,128)(2,1)}), bf16[8,128,128]{2,1,0:T(8,128)(2,1)S(1)}, u32[]{:S(2)}, u32[]{:S(2)}) async-start(bf16[8,128,128]{2,1,0:T(8,128)(2,1)} %key_side.1), calls=%async_computation.3 | async-start | bytes 524288 | tf_op jit(solution)/shard_map/all_to_all | solution.py:230
  165.8 3.1 %shard_map.97 = (bf16[128,1024]{1,0:T(8,128)(2,1)}, f32[128,1024]{1,0:T(8,128)}) custom-call(bf16[8,128,128]{2,1,0:T(8,128)(2,1)} %copy-done, bf16[512,1024]{1,0:T(8,128)(2,1)} %wo_ref.3, bf16[1024,512]{1,0:T(8,128)(2,1)} %wq_ref.3), custom_call_target="tpu_custom_call" | custom-call | tf_op jit(solution)/shard_map/pallas_call | solution.py:261
  168.9 8.7 %all-to-all-done.3.kv_ref = bf16[8,128,128]{2,1,0:T(8,128)(2,1)S(1)} async-done(((bf16[8,128,128]{2,1,0:T(8,128)(2,1)}), bf16[8,128,128]{2,1,0:T(8,128)(2,1)S(1)}, u32[]{:S(2)}, u32[]{:S(2)}) %all-to-all-start.3) | async-done | bytes 262176 | tf_op jit(solution)/shard_map/all_to_all | solution.py:230
  177.7 0.7 copy-done.1
  178.4 3.3 %shard_map.98 = bf16[128,1024]{1,0:T(8,128)(2,1)} custom-call(bf16[8,128,128]{2,1,0:T(8,128)(2,1)} %copy-done.1, f32[128,1024]{1,0:T(8,128)} %get-tuple-element.9.part_ref, bf16[1024,512]{1,0:T(8,128)(2,1)} %wk_ref.3, bf16[1024,512]{1,0:T(8,128)(2,1)} %wv_ref.3), custom_call_target="tpu_custom_call" | custom-call | tf_op jit(solution)/shard_map/pallas_call | solution.py:273
  (9 shorter events, 0.0 us)
Async XLA Ops:
  7.2 77.7 %all-gather.3.cloned.1.call-start = ((), (), s32[]{:S(2)}) async-start(), calls=%async_computation.4 | async-start | bytes 8650752 | tf_op jit(solution)/shard_map/all_gather | solution.py:242
  30.5 114.9 %all-gather.5.cloned.1.call-start = ((), (), s32[]{:S(2)}) async-start(), calls=%async_computation.5 | async-start | bytes 8650752 | tf_op jit(solution)/shard_map/all_gather | solution.py:243
  103.8 55.0 %all-to-all-start.2 = ((bf16[8,128,128]{2,1,0:T(8,128)(2,1)}), bf16[8,128,128]{2,1,0:T(8,128)(2,1)S(1)}, u32[]{:S(2)}, u32[]{:S(2)}) async-start(bf16[8,128,128]{2,1,0:T(8,128)(2,1)} %get-tuple-element.6), calls=%async_computation.2 | async-start | bytes 524288 | tf_op jit(solution)/shard_map/all_to_all | solution.py:230
  158.8 7.0 %copy-start = (bf16[8,128,128]{2,1,0:T(8,128)(2,1)}, bf16[8,128,128]{2,1,0:T(8,128)(2,1)S(1)}, u32[]{:S(2)}) copy-start(bf16[8,128,128]{2,1,0:T(8,128)(2,1)S(1)} %all-to-all-done.2.og_ref) | copy-start | bytes 786436
  158.8 18.9 %all-to-all-start.3 = ((bf16[8,128,128]{2,1,0:T(8,128)(2,1)}), bf16[8,128,128]{2,1,0:T(8,128)(2,1)S(1)}, u32[]{:S(2)}, u32[]{:S(2)}) async-start(bf16[8,128,128]{2,1,0:T(8,128)(2,1)} %key_side.1), calls=%async_computation.3 | async-start | bytes 524288 | tf_op jit(solution)/shard_map/all_to_all | solution.py:230
  177.7 0.7 copy-start.1
Sparse Core Ops, SparseCore 0:
  30.6 54.2 all-gather.2
  87.5 57.9 all-gather.4

commit v2 on v0

v2 whole, which is shorter than its diff:
```python
import functools

import jax
import jax.numpy as jnp
from jax import lax
from jax.experimental import pallas as pl
from jax.experimental.pallas import tpu as pltpu
from jax.sharding import PartitionSpec as P

HEADS = 8
HEAD_DIM = 64
WIDE = 2 * HEAD_DIM
BLOCK = 128
KB_MAX = 21
CHUNK = 4
SLOTS = -(-KB_MAX // CHUNK) * CHUNK
LINE = 4
CORES = 2
OWN = 8
Q_BLOCKS = LINE * OWN
K_BLOCKS = LINE * CORES * OWN
HOPS = (0, 1, -1, 2)
SCALE = HEAD_DIM ** (-0.5)
FAR = -1e30
F32 = jnp.float32
BF16 = jnp.bfloat16
VMEM_LIMIT = 56 * 1024 * 1024

VMEM = pl.BlockSpec(memory_space=pltpu.VMEM)
SMEM = pl.BlockSpec(memory_space=pltpu.SMEM)
ANY = pl.BlockSpec(memory_space=pl.ANY)
NT = (((1,), (1,)), ((), ()))
TN = (((0,), (0,)), ((), ()))


def call(kernel, out_shape, in_specs, scratch=(), name=None):
    return pl.pallas_call(
        kernel,
        out_shape=out_shape,
        in_specs=in_specs,
        out_specs=jax.tree.map(lambda _: VMEM, out_shape),
        scratch_shapes=scratch,
        compiler_params=pltpu.CompilerParams(vmem_limit_bytes=VMEM_LIMIT),
        name=name,
    )


def struct(shape, dtype):
    return jax.ShapeDtypeStruct(shape, dtype)


def project_kernel(x_ref, gy_ref, wq_ref, wk_ref, wv_ref, wo_ref, out_ref):
    x = x_ref[...]
    k = jnp.dot(x, wk_ref[...], preferred_element_type=F32).astype(BF16)
    v = jnp.dot(x, wv_ref[...], preferred_element_type=F32).astype(BF16)
    q = jnp.dot(x, wq_ref[...], preferred_element_type=F32).astype(BF16)
    q = q * jnp.asarray(SCALE, BF16)
    d = lax.dot_general(gy_ref[...], wo_ref[...], NT, preferred_element_type=F32).astype(BF16)
    for h in range(HEADS):
        cols = slice(h * HEAD_DIM, (h + 1) * HEAD_DIM)
        out_ref[h, :BLOCK] = jnp.concatenate([k[:, cols], v[:, cols]], axis=1)
        out_ref[h, BLOCK:] = jnp.concatenate([q[:, cols], d[:, cols]], axis=1)


def line_of(hop, at):
    return (at - hop + LINE) % LINE


def load_lines(me_ref, kv_pieces, qd_pieces, kv_all, qd_all, sems):
    y, x, c = me_ref[0], me_ref[1], me_ref[2]
    copies = []
    rows = OWN * BLOCK
    for i, piece in enumerate(kv_pieces):
        hop, other = HOPS[i % LINE], i // LINE
        core = c if other == 0 else 1 - c
        at = pl.multiple_of((line_of(hop, x) * CORES + core) * rows, rows)
        copies.append(pltpu.make_async_copy(piece, kv_all.at[pl.ds(at, rows)], sems.at[i]))
    for i, piece in enumerate(qd_pieces):
        at = pl.multiple_of(line_of(HOPS[i], y) * rows, rows)
        copies.append(
            pltpu.make_async_copy(piece, qd_all.at[pl.ds(at, rows)], sems.at[len(kv_pieces) + i])
        )
    for copy in copies:
        copy.start()
    for copy in copies:
        copy.wait()


def query_pair(qd_all, b):
    qd = qd_all[pl.ds(pl.multiple_of(b * BLOCK, BLOCK), BLOCK), :]
    low = lax.broadcasted_iota(jnp.int32, qd.shape, 1) < HEAD_DIM
    zero = jnp.zeros_like(qd)
    return jnp.concatenate([jnp.where(low, qd, zero), jnp.where(low, zero, qd)], axis=0)


def chunk_products(pos_ref, kv_all, pair, b, c, cnt):
    kvs, far = [], []
    for i in range(CHUNK):
        s = c * CHUNK + i
        at = pl.multiple_of(pos_ref[b, s] * BLOCK, BLOCK)
        kvs.append(kv_all[pl.ds(at, BLOCK), :])
        far.append(jnp.where(s < cnt, 0.0, FAR))
    kv = jnp.concatenate(kvs, axis=0)
    prod = lax.dot_general(kv, pair, NT, preferred_element_type=F32)
    scores = jnp.concatenate(
        [prod[i * BLOCK : (i + 1) * BLOCK, :BLOCK] + far[i] for i in range(CHUNK)], axis=0
    )
    return kv, scores, prod[:, BLOCK:]


def chunks_of(cnt):
    return (cnt + CHUNK - 1) // CHUNK


def stats_kernel(me_ref, pos_ref, cnt_ref, *rest):
    kv_pieces, qd_pieces = rest[: 2 * LINE], rest[2 * LINE : 3 * LINE]
    top_ref, kv_all, qd_all, sems = rest[3 * LINE :]
    load_lines(me_ref, kv_pieces, qd_pieces, kv_all, qd_all, sems)

    def one(b, carry):
        pair = query_pair(qd_all, b)
        cnt = cnt_ref[b]

        def chunk(c, state):
            top, total, dot = state
            _, scores, dprobs = chunk_products(pos_ref, kv_all, pair, b, c, cnt)
            new = jnp.maximum(top, jnp.max(scores, axis=0, keepdims=True))
            keep = jnp.exp(top - new)
            raw = jnp.exp(scores - new)
            total = total * keep + jnp.sum(raw, axis=0, keepdims=True)
            dot = dot * keep + jnp.sum(raw * dprobs, axis=0, keepdims=True)
            return new, total, dot

        zero = jnp.zeros((1, BLOCK), F32)
        top, total, dot = lax.fori_loop(
            0, chunks_of(cnt), chunk, (jnp.full((1, BLOCK), FAR, F32), zero, zero)
        )
        top_ref[0, pl.ds(b, 1), :] = top
        top_ref[1, pl.ds(b, 1), :] = total
        top_ref[2, pl.ds(b, 1), :] = dot
        return carry

    lax.fori_loop(0, Q_BLOCKS, one, 0)


def grads_kernel(me_ref, pos_ref, cnt_ref, *rest):
    stats, rest = rest[:LINE], rest[LINE:]
    kv_pieces, qd_pieces, rest = rest[: 2 * LINE], rest[2 * LINE : 3 * LINE], rest[3 * LINE :]
    y_refs, rest = rest[:LINE], rest[LINE:]
    own_ref, other_ref, kv_all, qd_all, acc_ref, lse_ref, delta_ref, sems = rest
    load_lines(me_ref, kv_pieces, qd_pieces, kv_all, qd_all, sems)

    top = functools.reduce(jnp.maximum, [s[0] for s in stats])
    weights = [jnp.exp(s[0] - top) for s in stats]
    total = sum(s[1] * w for s, w in zip(stats, weights))
    dot = sum(s[2] * w for s, w in zip(stats, weights))
    lse_ref[...] = top + jnp.log(total)
    delta_ref[...] = dot / total
    acc_ref[...] = jnp.zeros_like(acc_ref)
    y = me_ref[0]

    def one(n, carry):
        hop_at, i = n // OWN, n % OWN
        hop = jnp.where(hop_at == 3, 2, jnp.where(hop_at == 2, -1, hop_at))
        b = (y + hop + LINE) % LINE * OWN + i
        pair = query_pair(qd_all, b)
        cnt = cnt_ref[b]
        lse = lse_ref[pl.ds(b, 1), :]
        delta = delta_ref[pl.ds(b, 1), :]

        def chunk(c, state):
            kv, scores, dprobs = chunk_products(pos_ref, kv_all, pair, b, c, cnt)
            probs = jnp.exp(scores - lse)
            dscores = probs * (dprobs - delta)
            low = jnp.concatenate([dscores.astype(BF16), probs.astype(BF16)], axis=1)
            terms = jnp.dot(low, pair, preferred_element_type=F32)
            for s in range(CHUNK):
                at = pos_ref[b, c * CHUNK + s]
                acc_ref[at] = acc_ref[at] + terms[s * BLOCK : (s + 1) * BLOCK]
            return state + lax.dot_general(kv, low, TN, preferred_element_type=F32)

        state = lax.fori_loop(0, chunks_of(cnt), chunk, jnp.zeros((WIDE, 2 * BLOCK), F32))
        out = jnp.concatenate([state[:HEAD_DIM, :BLOCK] * SCALE, state[HEAD_DIM:, BLOCK:]], axis=0)
        for k in range(LINE):

            @pl.when(hop_at == k)
            def _():
                y_refs[k][i] = out.astype(y_refs[k].dtype)

        return carry

    lax.fori_loop(0, Q_BLOCKS, one, 0)
    core = me_ref[2]

    def spread(n, carry):
        line, i = n // OWN, n % OWN
        own_ref[n] = acc_ref[(line * CORES + core) * OWN + i]
        other_ref[n] = acc_ref[(line * CORES + 1 - core) * OWN + i].astype(BF16)
        return carry

    lax.fori_loop(0, LINE * OWN, spread, 0)


def core_sum_kernel(me_ref, own_ref, other_ref, *out_refs):
    x = me_ref[1]
    for k, hop in enumerate(HOPS):
        line = (x + hop + LINE) % LINE
        rows = pl.ds(line * OWN, OWN)
        out_refs[k][...] = (own_ref[rows] + other_ref[rows].astype(F32)).astype(out_refs[k].dtype)


def line_sum_kernel(*refs):
    xs, ys, out_ref = refs[:LINE], refs[LINE : 2 * LINE], refs[2 * LINE]
    for at, parts in ((0, xs), (BLOCK, ys)):
        total = sum(p[...].astype(F32) for p in parts)
        out_ref[:, at : at + BLOCK] = total.astype(BF16)


def output_kernel(in_ref, wq_ref, wk_ref, wv_ref, wo_ref, out_ref, grad_ref):
    gk = jnp.concatenate([in_ref[h, :BLOCK, :HEAD_DIM] for h in range(HEADS)], axis=1)
    gv = jnp.concatenate([in_ref[h, :BLOCK, HEAD_DIM:] for h in range(HEADS)], axis=1)
    gq = jnp.concatenate([in_ref[h, BLOCK : BLOCK + HEAD_DIM] for h in range(HEADS)], axis=0)
    att = jnp.concatenate([in_ref[h, BLOCK + HEAD_DIM :] for h in range(HEADS)], axis=0)
    out = lax.dot_general(att, wo_ref[...], TN, preferred_element_type=F32)
    out_ref[...] = out.astype(BF16)
    total = lax.dot_general(
        gq, wq_ref[...], (((0,), (1,)), ((), ())), preferred_element_type=F32
    )
    total = total + lax.dot_general(gk, wk_ref[...], NT, preferred_element_type=F32)
    total = total + lax.dot_general(gv, wv_ref[...], NT, preferred_element_type=F32)
    grad_ref[...] = total.astype(BF16)


def ctx_shift(x, dy=0, dx=0, dc=0):
    pairs = []
    for i in range(LINE * LINE * CORES):
        y, r, c = i // (LINE * CORES), i // CORES % LINE, i % CORES
        to = ((y + dy) % LINE * LINE + (r + dx) % LINE) * CORES + (c + dc) % CORES
        pairs.append((i, to))
    return lax.ppermute(x, "ctx", pairs)


def live_lists(block_cell, cell_mask, y, xc):
    cells = jnp.arange(cell_mask.shape[0], dtype=jnp.int32)
    by_line = block_cell.reshape(LINE, LINE * CORES, OWN)
    q_cell = lax.dynamic_index_in_dim(by_line, xc, 1, keepdims=False).reshape(Q_BLOCKS)
    k_cell = lax.dynamic_slice_in_dim(block_cell, y * K_BLOCKS, K_BLOCKS, 0)
    q_hot = (q_cell[:, None] == cells[None, :]).astype(BF16)
    k_hot = (k_cell[:, None] == cells[None, :]).astype(BF16)
    picked = jnp.dot(q_hot, cell_mask.astype(BF16), preferred_element_type=F32).astype(BF16)
    live = lax.dot_general(picked, k_hot, NT, preferred_element_type=F32)
    at = jnp.arange(K_BLOCKS, dtype=jnp.int32)
    upto = (at[:, None] <= at[None, :]).astype(BF16)
    rank = jnp.dot(live.astype(BF16), upto, preferred_element_type=F32)
    slots = jnp.arange(1, SLOTS + 1, dtype=jnp.int32).astype(F32)
    matched = (live[:, None, :] > 0.5) & (rank[:, None, :] == slots[None, :, None])
    pos = jnp.sum(jnp.where(matched, at[None, None, :], 0), axis=2)
    return pos, jnp.sum(live, axis=1).astype(jnp.int32)


def exchange(x):
    return lax.all_to_all(x, "head", split_axis=0, concat_axis=0, tiled=True)


def body(hits_in, w_query, w_key, w_value, w_out, grad_y, block_cell, cell_mask):
    rows = OWN * BLOCK
    ctx = lax.axis_index("ctx")
    y, x, core = ctx // (LINE * CORES), ctx // CORES % LINE, ctx % CORES
    me = jnp.stack([y, x, core]).astype(jnp.int32)
    pos, cnt = live_lists(block_cell, cell_mask, y, ctx % (LINE * CORES))

    sent = call(project_kernel, struct((HEADS, 2 * BLOCK, WIDE), BF16), [VMEM] * 6, name="project")(
        hits_in, grad_y, w_query, w_key, w_value, w_out
    )
    got = exchange(sent)
    kv = got[:, :BLOCK].reshape(rows, WIDE)
    qd = got[:, BLOCK:].reshape(rows, WIDE)
    kvs = [kv] + [ctx_shift(kv, dx=hop) for hop in HOPS[1:]]
    kvs = kvs + [ctx_shift(piece, dc=1) for piece in kvs]
    qds = [qd] + [ctx_shift(qd, dy=hop) for hop in HOPS[1:]]

    lines = [pltpu.VMEM((K_BLOCKS * BLOCK, WIDE), BF16), pltpu.VMEM((Q_BLOCKS * BLOCK, WIDE), BF16)]
    sems = pltpu.SemaphoreType.DMA((3 * LINE,))
    stats = call(
        stats_kernel,
        struct((3, Q_BLOCKS, BLOCK), F32),
        [SMEM] * 3 + [ANY] * (3 * LINE),
        lines + [sems],
        "stats",
    )(me, pos, cnt, *kvs, *qds)
    all_stats = [stats] + [ctx_shift(stats, dy=hop) for hop in HOPS[1:]]

    tile = (OWN, BLOCK, WIDE)
    mixed = [struct(tile, F32)] + [struct(tile, BF16)] * (LINE - 1)
    *y_parts, own, other = call(
        grads_kernel,
        mixed + [struct((LINE * OWN, BLOCK, WIDE), F32), struct((LINE * OWN, BLOCK, WIDE), BF16)],
        [SMEM] * 3 + [VMEM] * LINE + [ANY] * (3 * LINE),
        lines
        + [pltpu.VMEM((K_BLOCKS, BLOCK, WIDE), F32)]
        + [pltpu.VMEM((Q_BLOCKS, BLOCK), F32)] * 2
        + [sems],
        "grads",
    )(me, pos, cnt, *all_stats, *kvs, *qds)
    y_parts = [y_parts[0]] + [ctx_shift(p, dy=hop) for p, hop in zip(y_parts[1:], HOPS[1:])]
    other = ctx_shift(other, dc=1)
    x_parts = call(core_sum_kernel, mixed, [SMEM, VMEM, VMEM], name="core_sum")(me, own, other)
    x_parts = [x_parts[0]] + [ctx_shift(p, dx=hop) for p, hop in zip(x_parts[1:], HOPS[1:])]
    summed = call(
        line_sum_kernel, struct((HEADS, 2 * BLOCK, WIDE), BF16), [VMEM] * (2 * LINE), name="line_sum"
    )(*x_parts, *y_parts)
    back = exchange(summed)
    full = struct(hits_in.shape, BF16)
    return call(output_kernel, (full, full), [VMEM] * 5, name="output")(
        back, w_query, w_key, w_value, w_out
    )


def solution(mesh):
    row = P(("ctx", "head"), None)
    return jax.shard_map(
        body,
        mesh=mesh,
        in_specs=(row, P(), P(), P(), P(), row, P(), P()),
        out_specs=(row, row),
        check_vma=False,
    )
```

time: 436 us -> 161 us (0.37)
  the two profiles are of different devices: /device:TPU:6 before, /device:TPU:32 now
where the time goes in v2:
time: 161 us; the launch traced here: 160 us
  Pallas kernels  51.8 us (32%)
  waiting for transfers between devices  40.5 us (25%)
  starting transfers between devices  35.6 us (22%)
  blocking collectives  23.7 us (15%)
  local copies, waits for them, and re-layouts  4.2 us (3%)
  other arithmetic  2.54 us (2%)
    ppermute x20, starting transfers between devices, ctx_shift(): return lax.ppermute(x, 'ctx', pairs)  26.9 us
    ppermute x20, waiting for transfers between devices, ctx_shift(): return lax.ppermute(x, 'ctx', pairs)  24.7 us
    all_to_all x1, blocking collectives, exchange(): return lax.all_to_all(x, 'head', split_axis=0, concat_axis=0, tiled=True)  23.7 us
    pallas_call x1, Pallas kernels, body(): call(grads_kernel, mixed + [struct((LINE * OWN, BLOCK, WIDE), F32), struc...  22.4 us
    all_to_all x1, waiting for transfers between devices, exchange(): return lax.all_to_all(x, 'head', split_axis=0, concat_axis=0, tiled=True)  15.8 us
    pallas_call x1, Pallas kernels, body(): call(stats_kernel, struct((3, Q_BLOCKS, BLOCK), F32), [SMEM] * 3 + [ANY]...  15.3 us
    all_to_all x1, starting transfers between devices, exchange(): return lax.all_to_all(x, 'head', split_axis=0, concat_axis=0, tiled=True)  8.7 us
    pallas_call x1, Pallas kernels, body(): call(output_kernel, (full, full), [VMEM] * 5, name='output')  4.37 us
  transfers between devices with their start and end apart: 21, of which 12 were waited for; matrix products, arithmetic and copies ran while one was open for 2% of the time, Pallas kernels for 2%

profile of v2, /device:TPU:32, one launch (start us, length us, event | category | flops | bytes accessed | tf_op | source)
XLA Modules:
  0.0 159.6 jit_solution(8539375159177017539)
XLA Ops:
  0.6 4.1 %project.1 = bf16[8,256,128]{2,1,0:T(8,128)(2,1)} custom-call(bf16[128,1024]{1,0:T(8,128)(2,1)} %x_ref.1, bf16[128,1024]{1,0:T(8,128)(2,1)} %gy_ref.1, bf16[1024,512]{1,0:T(8,128)(2,1)} %wq_ref.3, bf16[1024,512]{1,0:T(8,128)(2,1)} %wk_ref.3, bf16[1024,512]{1,0:T(8,128)(2,1)} %wv_ref.3, bf16[512,1024]{1,0:T(8,128)(2,1)} %wo_ref.3), custom_call_target="tpu_custom_call" | custom-call | tf_op jit(solution)/shard_map/project/pallas_call | solution.py:272
  4.8 8.7 %all-to-all-start = ((bf16[8,256,128]{2,1,0:T(8,128)(2,1)}), bf16[8,256,128]{2,1,0:T(8,128)(2,1)S(1)}, u32[]{:S(2)}, u32[]{:S(2)}) async-start(bf16[8,256,128]{2,1,0:T(8,128)(2,1)} %project.1), calls=%async_computation | async-start | bytes 1048576 | tf_op jit(solution)/shard_map/all_to_all | solution.py:262
  13.7 15.8 %all-to-all-done = bf16[8,256,128]{2,1,0:T(8,128)(2,1)S(1)} async-done(((bf16[8,256,128]{2,1,0:T(8,128)(2,1)}), bf16[8,256,128]{2,1,0:T(8,128)(2,1)S(1)}, u32[]{:S(2)}, u32[]{:S(2)}) %all-to-all-start) | async-done | bytes 524320 | tf_op jit(solution)/shard_map/all_to_all | solution.py:262
  29.6 3.3 %collective-permute-start.9 = (bf16[1024,128]{1,0:T(8,128)(2,1)S(1)}, bf16[1024,128]{1,0:T(8,128)(2,1)S(1)}, u32[]{:S(2)}, u32[]{:S(2)}) collective-permute-start(bf16[1024,128]{1,0:T(8,128)(2,1)S(1)} %bitcast.5), channel_id=1, source_target_pairs={{0,128},{8,136},{16,144},{24,152},{32,160},{40,168},{48,176},{56,1... | collective-permute-start | bytes 786440 | tf_op jit(solution)/shard_map/ppermute | solution.py:240
  32.9 1.1 collective-permute-start.8
  33.9 3.0 %collective-permute-start.2 = (bf16[1024,128]{1,0:T(8,128)(2,1)S(1)}, bf16[1024,128]{1,0:T(8,128)(2,1)S(1)}, u32[]{:S(2)}, u32[]{:S(2)}) collective-permute-start(bf16[1024,128]{1,0:T(8,128)(2,1)S(1)} %bitcast.10), channel_id=1, source_target_pairs={{0,32},{8,40},{16,48},{24,56},{32,0},{40,8},{48,16},{56,24},{64,96... | collective-permute-start | bytes 786440 | tf_op jit(solution)/shard_map/ppermute | solution.py:240
  36.9 1.1 collective-permute-start.1
  38.1 0.9 collective-permute-start
  39.4 1.0 collective-permute-start.7
  40.4 1.4 collective-permute-done.8.rest_10_.rest_14_
  42.3 2.9 %collective-permute-done.1.rest_2_.rest_6_ = bf16[1024,128]{1,0:T(8,128)(2,1)S(1)} collective-permute-done((bf16[1024,128]{1,0:T(8,128)(2,1)S(1)}, bf16[1024,128]{1,0:T(8,128)(2,1)S(1)}, u32[]{:S(2)}, u32[]{:S(2)}) %collective-permute-start.1) | collective-permute-done | bytes 262176 | tf_op jit(solution)/shard_map/ppermute | solution.py:240
  46.3 0.6 pad_add_fusion.me_ref
  47.0 1.3 select_reduce_fusion.pos_ref
  49.3 0.7 copy-done.11
  50.0 15.3 %stats.1.rest_0_ = f32[3,32,128]{2,1,0:T(8,128)} custom-call(s32[3]{0:T(128)} %pad_add_fusion.me_ref, s32[32,24]{1,0:T(8,128)} %select_reduce_fusion.pos_ref, s32[32]{0:T(128)} %convert_element_type.26.cnt_ref, bf16[1024,128]{1,0:T(8,128)(2,1)} %bitcast.14, bf16[1024,128]{1,0:T(8,128)(2,1)} %copy-done.6, bf16[1024,128]{1,0:T(8,128)(2,1)} %copy-done.5, ...), custom_call_target="tpu_custom_call" | custom-call | tf_op jit(solution)/shard_map/stats/pallas_call | solution.py:284
  65.2 3.8 %collective-permute-start.12 = (f32[3,32,128]{2,1,0:T(8,128)}, f32[3,32,128]{2,1,0:T(8,128)S(1)}, u32[]{:S(2)}, u32[]{:S(2)}) collective-permute-start(f32[3,32,128]{2,1,0:T(8,128)} %stats.1.rest_0_), channel_id=1, source_target_pairs={{0,128},{8,136},{16,144},{24,152},{32,160},{40,168},{48,176},{56,1... | collective-permute-start | bytes 147464 | tf_op jit(solution)/shard_map/ppermute | solution.py:240
  69.1 1.6 %collective-permute-start.11 = (f32[3,32,128]{2,1,0:T(8,128)}, f32[3,32,128]{2,1,0:T(8,128)S(1)}, u32[]{:S(2)}, u32[]{:S(2)}) collective-permute-start(f32[3,32,128]{2,1,0:T(8,128)} %stats.1.rest_0_), channel_id=1, source_target_pairs={{0,192},{8,200},{16,208},{24,216},{32,224},{40,232},{48,240},{56,2... | collective-permute-start | bytes 147464 | tf_op jit(solution)/shard_map/ppermute | solution.py:240
  71.3 2.3 %collective-permute-done.11.rest_2_ = f32[3,32,128]{2,1,0:T(8,128)S(1)} collective-permute-done((f32[3,32,128]{2,1,0:T(8,128)}, f32[3,32,128]{2,1,0:T(8,128)S(1)}, u32[]{:S(2)}, u32[]{:S(2)}) %collective-permute-start.11) | collective-permute-done | bytes 49184 | tf_op jit(solution)/shard_map/ppermute | solution.py:240
  73.7 3.0 %collective-permute-done.10.rest_1_ = f32[3,32,128]{2,1,0:T(8,128)S(1)} collective-permute-done((f32[3,32,128]{2,1,0:T(8,128)}, f32[3,32,128]{2,1,0:T(8,128)S(1)}, u32[]{:S(2)}, u32[]{:S(2)}) %collective-permute-start.10) | collective-permute-done | bytes 49184 | tf_op jit(solution)/shard_map/ppermute | solution.py:240
  77.3 22.4 %grads.1 = (f32[8,128,128]{2,1,0:T(8,128)}, bf16[8,128,128]{2,1,0:T(8,128)(2,1)}, bf16[8,128,128]{2,1,0:T(8,128)(2,1)}, bf16[8,128,128]{2,1,0:T(8,128)(2,1)}, f3...) custom-call(s32[3]{0:T(128)} %pad_add_fusion.me_ref, s32[32,24]{1,0:T(8,128)} %select_reduce_fusion.pos_ref, ...), custom_call_target="tpu_custom_call" | custom-call | tf_op jit(solution)/shard_map/grads/pallas_call | solution.py:295
  99.6 3.7 %collective-permute-start.13 = (bf16[32,128,128]{2,1,0:T(8,128)(2,1)}, bf16[32,128,128]{2,1,0:T(8,128)(2,1)S(1)}, u32[]{:S(2)}, u32[]{:S(2)}) collective-permute-start(bf16[32,128,128]{2,1,0:T(8,128)(2,1)} %get-tuple-element.13), channel_id=1, source_target_pairs={{0,8},{8,0},{16,24},{24,16},{32,40},{40,32},{48,56},{56,48},{64,72... | collective-permute-start | bytes 3145736 | tf_op jit(solution)/shard_map/ppermute | solution.py:240
  103.3 3.2 %collective-permute-start.18 = (bf16[8,128,128]{2,1,0:T(8,128)(2,1)}, bf16[8,128,128]{2,1,0:T(8,128)(2,1)S(1)}, u32[]{:S(2)}, u32[]{:S(2)}) collective-permute-start(bf16[8,128,128]{2,1,0:T(8,128)(2,1)} %get-tuple-element.20), channel_id=1, source_target_pairs={{0,192},{8,200},{16,208},{24,216},{32,224},{40,232},{48,240},{56,2... | collective-permute-start | bytes 786440 | tf_op jit(solution)/shard_map/ppermute | solution.py:240
  106.6 1.0 copy-done.12
  107.6 3.0 %core_sum.1 = (f32[8,128,128]{2,1,0:T(8,128)}, bf16[8,128,128]{2,1,0:T(8,128)(2,1)}, bf16[8,128,128]{2,1,0:T(8,128)(2,1)}, bf16[8,128,128]{2,1,0:T(8,128)(2,1)}) custom-call(s32[3]{0:T(128)} %pad_add_fusion.me_ref, f32[32,128,128]{2,1,0:T(8,128)} %get-tuple-element.12.own_ref, bf16[32,128,128]{2,1,0:T(8,128)(2,1)} %copy-done.12), custom_call_target="tpu_custom_call" | custom-call | tf_op jit(solution)/shard_map/core_sum/pallas_call | solution.py:307
  110.6 3.2 %collective-permute-start.15 = (bf16[8,128,128]{2,1,0:T(8,128)(2,1)}, bf16[8,128,128]{2,1,0:T(8,128)(2,1)S(1)}, u32[]{:S(2)}, u32[]{:S(2)}) collective-permute-start(bf16[8,128,128]{2,1,0:T(8,128)(2,1)} %get-tuple-element.16), channel_id=1, source_target_pairs={{0,48},{8,56},{16,0},{24,8},{32,16},{40,24},{48,32},{56,40},{64,11... | collective-permute-start | bytes 786440 | tf_op jit(solution)/shard_map/ppermute | solution.py:240
  113.8 5.0 %collective-permute-done.17.refs_5_ = bf16[8,128,128]{2,1,0:T(8,128)(2,1)S(1)} collective-permute-done((bf16[8,128,128]{2,1,0:T(8,128)(2,1)}, bf16[8,128,128]{2,1,0:T(8,128)(2,1)S(1)}, u32[]{:S(2)}, u32[]{:S(2)}) %collective-permute-start.17) | collective-permute-done | bytes 262176 | tf_op jit(solution)/shard_map/ppermute | solution.py:240
  120.0 5.0 %collective-permute-done.15.refs_2_ = bf16[8,128,128]{2,1,0:T(8,128)(2,1)S(1)} collective-permute-done((bf16[8,128,128]{2,1,0:T(8,128)(2,1)}, bf16[8,128,128]{2,1,0:T(8,128)(2,1)S(1)}, u32[]{:S(2)}, u32[]{:S(2)}) %collective-permute-start.15) | collective-permute-done | bytes 262176 | tf_op jit(solution)/shard_map/ppermute | solution.py:240
  124.9 3.3 %collective-permute-done.16.refs_3_ = bf16[8,128,128]{2,1,0:T(8,128)(2,1)S(1)} collective-permute-done((bf16[8,128,128]{2,1,0:T(8,128)(2,1)}, bf16[8,128,128]{2,1,0:T(8,128)(2,1)S(1)}, u32[]{:S(2)}, u32[]{:S(2)}) %collective-permute-start.16) | collective-permute-done | bytes 262176 | tf_op jit(solution)/shard_map/ppermute | solution.py:240
  128.3 0.7 copy-done.18
  128.9 2.7 %line_sum.1 = bf16[8,256,128]{2,1,0:T(8,128)(2,1)} custom-call(f32[8,128,128]{2,1,0:T(8,128)} %get-tuple-element.14.refs_0_, bf16[8,128,128]{2,1,0:T(8,128)(2,1)} %copy-done.16, bf16[8,128,128]{2,1,0:T(8,128)(2,1)} %copy-done.17, bf16[8,128,128]{2,1,0:T(8,128)(2,1)} %copy-done.18, f32[8,128,128]{2,1,0:T(8,128)} %get-tuple-element.18.refs_4_, ...), custom_call_target="tpu_custom_call" | custom-call | tf_op jit(solution)/shard_map/line_sum/pallas_call | solution.py:309
  131.6 23.7 %all_to_all.10.in_ref = bf16[8,256,128]{2,1,0:T(8,128)(2,1)} all-to-all(bf16[8,256,128]{2,1,0:T(8,128)(2,1)} %line_sum.1), channel_id=1, replica_groups=mesh['ctx'=32,'head'=8] {'head'}, dimensions={0} | all-to-all | bytes 1048576 | tf_op jit(solution)/shard_map/all_to_all | solution.py:262
  155.2 4.4 %output.1 = (bf16[128,1024]{1,0:T(8,128)(2,1)}, bf16[128,1024]{1,0:T(8,128)(2,1)}) custom-call(bf16[8,256,128]{2,1,0:T(8,128)(2,1)} %all_to_all.10.in_ref, bf16[1024,512]{1,0:T(8,128)(2,1)} %wq_ref.3, bf16[1024,512]{1,0:T(8,128)(2,1)} %wk_ref.3, bf16[1024,512]{1,0:T(8,128)(2,1)} %wv_ref.3, bf16[512,1024]{1,0:T(8,128)(2,1)} %wo_ref.3), custom_call_target="tpu_custom_call" | custom-call | tf_op jit(solution)/shard_map/output/pallas_call | solution.py:314
  (77 shorter events, 5.7 us)
Async XLA Ops:
  0.6 12.8 %copy-start.23 = (s32[256]{0:T(256)S(1)}, s32[256]{0:T(256)}, u32[]{:S(2)}) copy-start(s32[256]{0:T(256)} %param.14) | copy-start | bytes 3076
  4.8 34.2 %copy-start.19 = (s32[256,256]{1,0:T(8,128)S(1)}, s32[256,256]{1,0:T(8,128)}, u32[]{:S(2)}) copy-start(s32[256,256]{1,0:T(8,128)} %param.15) | copy-start | bytes 786436
  4.8 24.7 %all-to-all-start = ((bf16[8,256,128]{2,1,0:T(8,128)(2,1)}), bf16[8,256,128]{2,1,0:T(8,128)(2,1)S(1)}, u32[]{:S(2)}, u32[]{:S(2)}) async-start(bf16[8,256,128]{2,1,0:T(8,128)(2,1)} %project.1), calls=%async_computation | async-start | bytes 1048576 | tf_op jit(solution)/shard_map/all_to_all | solution.py:262
  29.6 18.8 %copy-start = (bf16[8,128,128]{2,1,0:T(8,128)(2,1)}, bf16[8,128,128]{2,1,0:T(8,128)(2,1)S(1)}, u32[]{:S(2)}) copy-start(bf16[8,128,128]{2,1,0:T(8,128)(2,1)S(1)} %get-tuple-element.22) | copy-start | bytes 786436
  29.6 18.8 %copy-start.1 = (bf16[8,128,128]{2,1,0:T(8,128)(2,1)}, bf16[8,128,128]{2,1,0:T(8,128)(2,1)S(1)}, u32[]{:S(2)}) copy-start(bf16[8,128,128]{2,1,0:T(8,128)(2,1)S(1)} %get-tuple-element.23) | copy-start | bytes 786436
  29.6 9.8 %collective-permute-start.9 = (bf16[1024,128]{1,0:T(8,128)(2,1)S(1)}, bf16[1024,128]{1,0:T(8,128)(2,1)S(1)}, u32[]{:S(2)}, u32[]{:S(2)}) collective-permute-start(bf16[1024,128]{1,0:T(8,128)(2,1)S(1)} %bitcast.5), channel_id=1, source_target_pairs={{0,128},{8,136},{16,144},{24,152},{32,160},{40,168},{48,176},{56,1... | collective-permute-start | bytes 786440 | tf_op jit(solution)/shard_map/ppermute | solution.py:240
  32.9 8.9 %collective-permute-start.8 = (bf16[1024,128]{1,0:T(8,128)(2,1)S(1)}, bf16[1024,128]{1,0:T(8,128)(2,1)S(1)}, u32[]{:S(2)}, u32[]{:S(2)}) collective-permute-start(bf16[1024,128]{1,0:T(8,128)(2,1)S(1)} %bitcast.6), channel_id=1, source_target_pairs={{0,192},{8,200},{16,208},{24,216},{32,224},{40,232},{48,240},{56,2... | collective-permute-start | bytes 786440 | tf_op jit(solution)/shard_map/ppermute | solution.py:240
  33.9 8.4 %collective-permute-start.2 = (bf16[1024,128]{1,0:T(8,128)(2,1)S(1)}, bf16[1024,128]{1,0:T(8,128)(2,1)S(1)}, u32[]{:S(2)}, u32[]{:S(2)}) collective-permute-start(bf16[1024,128]{1,0:T(8,128)(2,1)S(1)} %bitcast.10), channel_id=1, source_target_pairs={{0,32},{8,40},{16,48},{24,56},{32,0},{40,8},{48,16},{56,24},{64,96... | collective-permute-start | bytes 786440 | tf_op jit(solution)/shard_map/ppermute | solution.py:240
  36.9 8.3 %collective-permute-start.1 = (bf16[1024,128]{1,0:T(8,128)(2,1)S(1)}, bf16[1024,128]{1,0:T(8,128)(2,1)S(1)}, u32[]{:S(2)}, u32[]{:S(2)}) collective-permute-start(bf16[1024,128]{1,0:T(8,128)(2,1)S(1)} %bitcast.11), channel_id=1, source_target_pairs={{0,48},{8,56},{16,0},{24,8},{32,16},{40,24},{48,32},{56,40},{64,11... | collective-permute-start | bytes 786440 | tf_op jit(solution)/shard_map/ppermute | solution.py:240
  38.1 7.6 %collective-permute-start = (bf16[1024,128]{1,0:T(8,128)(2,1)S(1)}, bf16[1024,128]{1,0:T(8,128)(2,1)S(1)}, u32[]{:S(2)}, u32[]{:S(2)}) collective-permute-start(bf16[1024,128]{1,0:T(8,128)(2,1)S(1)} %bitcast.12), channel_id=1, source_target_pairs={{0,16},{8,24},{16,32},{24,40},{32,48},{40,56},{48,0},{56,8},{64,80... | collective-permute-start | bytes 786440 | tf_op jit(solution)/shard_map/ppermute | solution.py:240
  39.4 9.0 %copy-start.2 = (bf16[1024,128]{1,0:T(8,128)(2,1)}, bf16[1024,128]{1,0:T(8,128)(2,1)S(1)}, u32[]{:S(2)}) copy-start(bf16[1024,128]{1,0:T(8,128)(2,1)S(1)} %collective-permute-done.9.rest_11_.rest_15_) | copy-start | bytes 786436
  39.4 8.9 %collective-permute-start.7 = (bf16[1024,128]{1,0:T(8,128)(2,1)S(1)}, bf16[1024,128]{1,0:T(8,128)(2,1)S(1)}, u32[]{:S(2)}, u32[]{:S(2)}) collective-permute-start(bf16[1024,128]{1,0:T(8,128)(2,1)S(1)} %bitcast.7), channel_id=1, source_target_pairs={{0,64},{8,72},{16,80},{24,88},{32,96},{40,104},{48,112},{56,120},{... | collective-permute-start | bytes 786440 | tf_op jit(solution)/shard_map/ppermute | solution.py:240
  41.8 6.6 %copy-start.3 = (bf16[1024,128]{1,0:T(8,128)(2,1)}, bf16[1024,128]{1,0:T(8,128)(2,1)S(1)}, u32[]{:S(2)}) copy-start(bf16[1024,128]{1,0:T(8,128)(2,1)S(1)} %collective-permute-done.8.rest_10_.rest_14_) | copy-start | bytes 786436
  41.8 6.5 %collective-permute-start.3 = (bf16[1024,128]{1,0:T(8,128)(2,1)S(1)}, bf16[1024,128]{1,0:T(8,128)(2,1)S(1)}, u32[]{:S(2)}, u32[]{:S(2)}) collective-permute-start(bf16[1024,128]{1,0:T(8,128)(2,1)S(1)} %bitcast.13), channel_id=1, source_target_pairs={{0,8},{8,0},{16,24},{24,16},{32,40},{40,32},{48,56},{56,48},{64,72... | collective-permute-start | bytes 786440 | tf_op jit(solution)/shard_map/ppermute | solution.py:240
  42.3 6.0 %copy-start.4 = (bf16[1024,128]{1,0:T(8,128)(2,1)}, bf16[1024,128]{1,0:T(8,128)(2,1)S(1)}, u32[]{:S(2)}) copy-start(bf16[1024,128]{1,0:T(8,128)(2,1)S(1)} %collective-permute-done.2.rest_3_.rest_7_) | copy-start | bytes 786436
  42.3 6.0 %collective-permute-start.6 = (bf16[1024,128]{1,0:T(8,128)(2,1)S(1)}, bf16[1024,128]{1,0:T(8,128)(2,1)S(1)}, u32[]{:S(2)}, u32[]{:S(2)}) collective-permute-start(bf16[1024,128]{1,0:T(8,128)(2,1)S(1)} %collective-permute-done.2.rest_3_.rest_7_), channel_id=1, source_target_pairs={{0,8},{8,0},{16,24},{24,16},{32,40},{40,32},{48,56},{56,48},{64,72... | collective-permute-start | bytes 786440 | tf_op jit(solution)/shard_map/ppermute | solution.py:240
  45.2 3.1 %collective-permute-start.5 = (bf16[1024,128]{1,0:T(8,128)(2,1)S(1)}, bf16[1024,128]{1,0:T(8,128)(2,1)S(1)}, u32[]{:S(2)}, u32[]{:S(2)}) collective-permute-start(bf16[1024,128]{1,0:T(8,128)(2,1)S(1)} %collective-permute-done.1.rest_2_.rest_6_), channel_id=1, source_target_pairs={{0,8},{8,0},{16,24},{24,16},{32,40},{40,32},{48,56},{56,48},{64,72... | collective-permute-start | bytes 786440 | tf_op jit(solution)/shard_map/ppermute | solution.py:240
  45.7 2.7 %collective-permute-start.4 = (bf16[1024,128]{1,0:T(8,128)(2,1)S(1)}, bf16[1024,128]{1,0:T(8,128)(2,1)S(1)}, u32[]{:S(2)}, u32[]{:S(2)}) collective-permute-start(bf16[1024,128]{1,0:T(8,128)(2,1)S(1)} %collective-permute-done.rest_1_.rest_5_), channel_id=1, source_target_pairs={{0,8},{8,0},{16,24},{24,16},{32,40},{40,32},{48,56},{56,48},{64,72... | collective-permute-start | bytes 786440 | tf_op jit(solution)/shard_map/ppermute | solution.py:240
  65.2 6.1 %collective-permute-start.12 = (f32[3,32,128]{2,1,0:T(8,128)}, f32[3,32,128]{2,1,0:T(8,128)S(1)}, u32[]{:S(2)}, u32[]{:S(2)}) collective-permute-start(f32[3,32,128]{2,1,0:T(8,128)} %stats.1.rest_0_), channel_id=1, source_target_pairs={{0,128},{8,136},{16,144},{24,152},{32,160},{40,168},{48,176},{56,1... | collective-permute-start | bytes 147464 | tf_op jit(solution)/shard_map/ppermute | solution.py:240
  69.1 4.6 %collective-permute-start.11 = (f32[3,32,128]{2,1,0:T(8,128)}, f32[3,32,128]{2,1,0:T(8,128)S(1)}, u32[]{:S(2)}, u32[]{:S(2)}) collective-permute-start(f32[3,32,128]{2,1,0:T(8,128)} %stats.1.rest_0_), channel_id=1, source_target_pairs={{0,192},{8,200},{16,208},{24,216},{32,224},{40,232},{48,240},{56,2... | collective-permute-start | bytes 147464 | tf_op jit(solution)/shard_map/ppermute | solution.py:240
  70.7 6.0 %collective-permute-start.10 = (f32[3,32,128]{2,1,0:T(8,128)}, f32[3,32,128]{2,1,0:T(8,128)S(1)}, u32[]{:S(2)}, u32[]{:S(2)}) collective-permute-start(f32[3,32,128]{2,1,0:T(8,128)} %stats.1.rest_0_), channel_id=1, source_target_pairs={{0,64},{8,72},{16,80},{24,88},{32,96},{40,104},{48,112},{56,120},{... | collective-permute-start | bytes 147464 | tf_op jit(solution)/shard_map/ppermute | solution.py:240
  99.6 7.0 %collective-permute-start.13 = (bf16[32,128,128]{2,1,0:T(8,128)(2,1)}, bf16[32,128,128]{2,1,0:T(8,128)(2,1)S(1)}, u32[]{:S(2)}, u32[]{:S(2)}) collective-permute-start(bf16[32,128,128]{2,1,0:T(8,128)(2,1)} %get-tuple-element.13), channel_id=1, source_target_pairs={{0,8},{8,0},{16,24},{24,16},{32,40},{40,32},{48,56},{56,48},{64,72... | collective-permute-start | bytes 3145736 | tf_op jit(solution)/shard_map/ppermute | solution.py:240
  103.3 15.5 %collective-permute-start.17 = (bf16[8,128,128]{2,1,0:T(8,128)(2,1)}, bf16[8,128,128]{2,1,0:T(8,128)(2,1)S(1)}, u32[]{:S(2)}, u32[]{:S(2)}) collective-permute-start(bf16[8,128,128]{2,1,0:T(8,128)(2,1)} %get-tuple-element.19), channel_id=1, source_target_pairs={{0,64},{8,72},{16,80},{24,88},{32,96},{40,104},{48,112},{56,120},{... | collective-permute-start | bytes 786440 | tf_op jit(solution)/shard_map/ppermute | solution.py:240
  103.3 16.0 %collective-permute-start.18 = (bf16[8,128,128]{2,1,0:T(8,128)(2,1)}, bf16[8,128,128]{2,1,0:T(8,128)(2,1)S(1)}, u32[]{:S(2)}, u32[]{:S(2)}) collective-permute-start(bf16[8,128,128]{2,1,0:T(8,128)(2,1)} %get-tuple-element.20), channel_id=1, source_target_pairs={{0,192},{8,200},{16,208},{24,216},{32,224},{40,232},{48,240},{56,2... | collective-permute-start | bytes 786440 | tf_op jit(solution)/shard_map/ppermute | solution.py:240
  106.6 12.8 %collective-permute-start.19 = (bf16[8,128,128]{2,1,0:T(8,128)(2,1)}, bf16[8,128,128]{2,1,0:T(8,128)(2,1)S(1)}, u32[]{:S(2)}, u32[]{:S(2)}) collective-permute-start(bf16[8,128,128]{2,1,0:T(8,128)(2,1)} %get-tuple-element.21), channel_id=1, source_target_pairs={{0,128},{8,136},{16,144},{24,152},{32,160},{40,168},{48,176},{56,1... | collective-permute-start | bytes 786440 | tf_op jit(solution)/shard_map/ppermute | solution.py:240
  110.6 9.3 %collective-permute-start.14 = (bf16[8,128,128]{2,1,0:T(8,128)(2,1)}, bf16[8,128,128]{2,1,0:T(8,128)(2,1)S(1)}, u32[]{:S(2)}, u32[]{:S(2)}) collective-permute-start(bf16[8,128,128]{2,1,0:T(8,128)(2,1)} %get-tuple-element.15), channel_id=1, source_target_pairs={{0,16},{8,24},{16,32},{24,40},{32,48},{40,56},{48,0},{56,8},{64,80... | collective-permute-start | bytes 786440 | tf_op jit(solution)/shard_map/ppermute | solution.py:240
  110.6 14.3 %collective-permute-start.15 = (bf16[8,128,128]{2,1,0:T(8,128)(2,1)}, bf16[8,128,128]{2,1,0:T(8,128)(2,1)S(1)}, u32[]{:S(2)}, u32[]{:S(2)}) collective-permute-start(bf16[8,128,128]{2,1,0:T(8,128)(2,1)} %get-tuple-element.16), channel_id=1, source_target_pairs={{0,48},{8,56},{16,0},{24,8},{32,16},{40,24},{48,32},{56,40},{64,11... | collective-permute-start | bytes 786440 | tf_op jit(solution)/shard_map/ppermute | solution.py:240
  118.9 9.4 %copy-start.13 = (bf16[8,128,128]{2,1,0:T(8,128)(2,1)}, bf16[8,128,128]{2,1,0:T(8,128)(2,1)S(1)}, u32[]{:S(2)}) copy-start(bf16[8,128,128]{2,1,0:T(8,128)(2,1)S(1)} %collective-permute-done.17.refs_5_) | copy-start | bytes 786436
  118.9 9.4 %collective-permute-start.16 = (bf16[8,128,128]{2,1,0:T(8,128)(2,1)}, bf16[8,128,128]{2,1,0:T(8,128)(2,1)S(1)}, u32[]{:S(2)}, u32[]{:S(2)}) collective-permute-start(bf16[8,128,128]{2,1,0:T(8,128)(2,1)} %get-tuple-element.17), channel_id=1, source_target_pairs={{0,32},{8,40},{16,48},{24,56},{32,0},{40,8},{48,16},{56,24},{64,96... | collective-permute-start | bytes 786440 | tf_op jit(solution)/shard_map/ppermute | solution.py:240
  119.3 8.9 %copy-start.14 = (bf16[8,128,128]{2,1,0:T(8,128)(2,1)}, bf16[8,128,128]{2,1,0:T(8,128)(2,1)S(1)}, u32[]{:S(2)}) copy-start(bf16[8,128,128]{2,1,0:T(8,128)(2,1)S(1)} %collective-permute-done.18.refs_6_) | copy-start | bytes 786436
  119.3 8.9 %copy-start.15 = (bf16[8,128,128]{2,1,0:T(8,128)(2,1)}, bf16[8,128,128]{2,1,0:T(8,128)(2,1)S(1)}, u32[]{:S(2)}) copy-start(bf16[8,128,128]{2,1,0:T(8,128)(2,1)S(1)} %collective-permute-done.19.refs_7_) | copy-start | bytes 786436
  120.0 8.3 %copy-start.16 = (bf16[8,128,128]{2,1,0:T(8,128)(2,1)}, bf16[8,128,128]{2,1,0:T(8,128)(2,1)S(1)}, u32[]{:S(2)}) copy-start(bf16[8,128,128]{2,1,0:T(8,128)(2,1)S(1)} %collective-permute-done.14.refs_1_) | copy-start | bytes 786436
  (13 other events, 23.8 us)

commit v3 on v2

v3 whole, which is shorter than its diff:
```python
import functools

import jax
import jax.numpy as jnp
from jax import lax
from jax.experimental import pallas as pl
from jax.experimental.pallas import tpu as pltpu
from jax.sharding import PartitionSpec as P

HEADS = 8
HEAD_DIM = 64
WIDE = 2 * HEAD_DIM
BLOCK = 128
KB_MAX = 21
SLOTS = 24
STATS_ITEM = 2
GRADS_ITEM = 4
STATS_UNROLL = 8
GRADS_UNROLL = 4
LINE = 4
CORES = 2
OWN = 8
Q_BLOCKS = LINE * OWN
K_BLOCKS = LINE * CORES * OWN
HOPS = (0, 1, -1, 2)
SCALE = HEAD_DIM ** (-0.5)
FAR = -1e30
F32 = jnp.float32
BF16 = jnp.bfloat16
VMEM_LIMIT = 32 * 1024 * 1024

VMEM = pl.BlockSpec(memory_space=pltpu.VMEM)
SMEM = pl.BlockSpec(memory_space=pltpu.SMEM)
ANY = pl.BlockSpec(memory_space=pl.ANY)
NT = (((1,), (1,)), ((), ()))
TN = (((0,), (0,)), ((), ()))


def call(kernel, out_shape, in_specs, scratch=(), name=None):
    return pl.pallas_call(
        kernel,
        out_shape=out_shape,
        in_specs=in_specs,
        out_specs=jax.tree.map(lambda _: VMEM, out_shape),
        scratch_shapes=scratch,
        compiler_params=pltpu.CompilerParams(vmem_limit_bytes=VMEM_LIMIT),
        name=name,
    )


def struct(shape, dtype):
    return jax.ShapeDtypeStruct(shape, dtype)


def near(*arrays):
    return [pltpu.with_memory_space_constraint(a, pltpu.VMEM) for a in arrays]


def project_kernel(*refs):
    out_ref, bufs, sems = refs[6], refs[7:13], refs[13]
    copies = [pltpu.make_async_copy(refs[i], bufs[i], sems.at[i]) for i in range(6)]
    for copy in copies:
        copy.start()

    def arrived(i):
        copies[i].wait()
        return bufs[i][...]

    x = arrived(0)
    k = jnp.dot(x, arrived(1), preferred_element_type=F32).astype(BF16)
    v = jnp.dot(x, arrived(2), preferred_element_type=F32).astype(BF16)
    q = jnp.dot(x, arrived(3), preferred_element_type=F32).astype(BF16)
    q = q * jnp.asarray(SCALE, BF16)
    gy = arrived(4)
    d = lax.dot_general(gy, arrived(5), NT, preferred_element_type=F32).astype(BF16)
    for h in range(HEADS):
        cols = slice(h * HEAD_DIM, (h + 1) * HEAD_DIM)
        out_ref[h, :BLOCK] = jnp.concatenate([k[:, cols], v[:, cols]], axis=1)
        out_ref[h, BLOCK:] = jnp.concatenate([q[:, cols], d[:, cols]], axis=1)


def line_of(hop, at):
    return (at - hop + LINE) % LINE


def load_lines(me_ref, kv_pieces, qd_pieces, kv_all, qd_all, sems):
    y, x, c = me_ref[0], me_ref[1], me_ref[2]
    copies = []
    rows = OWN * BLOCK
    for i, piece in enumerate(kv_pieces):
        hop, other = HOPS[i % LINE], i // LINE
        core = c if other == 0 else 1 - c
        at = pl.multiple_of((line_of(hop, x) * CORES + core) * rows, rows)
        copies.append(pltpu.make_async_copy(piece, kv_all.at[pl.ds(at, rows)], sems.at[i]))
    for i, piece in enumerate(qd_pieces):
        at = pl.multiple_of(line_of(HOPS[i], y) * rows, rows)
        copies.append(
            pltpu.make_async_copy(piece, qd_all.at[pl.ds(at, rows)], sems.at[len(kv_pieces) + i])
        )
    for copy in copies:
        copy.start()
    return copies


def query_pair(qd_all, b):
    qd = qd_all[pl.ds(pl.multiple_of(b * BLOCK, BLOCK), BLOCK), :]
    low = lax.broadcasted_iota(jnp.int32, qd.shape, 1) < HEAD_DIM
    zero = jnp.zeros_like(qd)
    return jnp.concatenate([jnp.where(low, qd, zero), jnp.where(low, zero, qd)], axis=0)


def build_items(cnt_ref, item_ref, size):
    def one(b, at):
        def put(j, at):
            item_ref[at] = b * 16 + j
            return at + 1

        return lax.fori_loop(0, (cnt_ref[b] + size - 1) // size, put, at)

    return lax.fori_loop(0, Q_BLOCKS, one, 0)


def read_item(item_ref, pos_ref, cnt_ref, at, amount, size):
    code = item_ref[jnp.minimum(at, amount - 1)]
    b, j = code // 16, code % 16
    limit = jnp.where(at < amount, cnt_ref[b], 0)
    places = [pos_ref[b, size * j + s] for s in range(size)]
    far = [jnp.where(size * j + s < limit, 0.0, FAR) for s in range(size)]
    return b, places, far


def item_products(kv_all, pair, places, far):
    kv = jnp.concatenate(
        [kv_all[pl.ds(pl.multiple_of(p * BLOCK, BLOCK), BLOCK), :] for p in places], axis=0
    )
    prod = lax.dot_general(kv, pair, NT, preferred_element_type=F32)
    scores = jnp.concatenate(
        [prod[s * BLOCK : (s + 1) * BLOCK, :BLOCK] + far[s] for s in range(len(places))], axis=0
    )
    return kv, scores, prod[:, BLOCK:]


def stats_kernel(me_ref, pos_ref, cnt_ref, *rest):
    kv_pieces, qd_pieces = rest[: 2 * LINE], rest[2 * LINE : 3 * LINE]
    out_ref, kv_all, qd_all, item_ref, sems = rest[3 * LINE :]
    copies = load_lines(me_ref, kv_pieces, qd_pieces, kv_all, qd_all, sems)
    out_ref[0] = jnp.full((Q_BLOCKS, BLOCK), FAR, F32)
    out_ref[1:] = jnp.zeros((2, Q_BLOCKS, BLOCK), F32)
    amount = build_items(cnt_ref, item_ref, STATS_ITEM)
    for copy in copies:
        copy.wait()

    def step(n, carry):
        done = []
        for u in range(STATS_UNROLL):
            at = n * STATS_UNROLL + u
            b, places, far = read_item(item_ref, pos_ref, cnt_ref, at, amount, STATS_ITEM)
            _, scores, dprobs = item_products(kv_all, query_pair(qd_all, b), places, far)
            top = jnp.max(scores, axis=0, keepdims=True)
            raw = jnp.exp(scores - top)
            total = jnp.sum(raw, axis=0, keepdims=True)
            dot = jnp.sum(raw * dprobs, axis=0, keepdims=True)
            done.append((pl.ds(b, 1), top, total, dot))
        for row, top, total, dot in done:
            old = out_ref[0, row, :]
            new = jnp.maximum(old, top)
            keep, take = jnp.exp(old - new), jnp.exp(top - new)
            out_ref[0, row, :] = new
            out_ref[1, row, :] = out_ref[1, row, :] * keep + total * take
            out_ref[2, row, :] = out_ref[2, row, :] * keep + dot * take
        return carry

    lax.fori_loop(0, (amount + STATS_UNROLL - 1) // STATS_UNROLL, step, 0)


def grads_kernel(me_ref, pos_ref, cnt_ref, *rest):
    stats, rest = rest[:LINE], rest[LINE:]
    kv_pieces, qd_pieces, rest = rest[: 2 * LINE], rest[2 * LINE : 3 * LINE], rest[3 * LINE :]
    y_refs, rest = rest[:LINE], rest[LINE:]
    own_ref, other_ref, kv_all, qd_all, key_ref, query_ref, lse_ref, delta_ref, item_ref, sems = rest
    copies = load_lines(me_ref, kv_pieces, qd_pieces, kv_all, qd_all, sems)

    top = functools.reduce(jnp.maximum, [s[0] for s in stats])
    weights = [jnp.exp(s[0] - top) for s in stats]
    total = sum(s[1] * w for s, w in zip(stats, weights))
    dot = sum(s[2] * w for s, w in zip(stats, weights))
    lse_ref[...] = top + jnp.log(total)
    delta_ref[...] = dot / total
    key_ref[...] = jnp.zeros_like(key_ref)
    query_ref[...] = jnp.zeros_like(query_ref)
    amount = build_items(cnt_ref, item_ref, GRADS_ITEM)
    for copy in copies:
        copy.wait()

    def step(n, carry):
        done = []
        for u in range(GRADS_UNROLL):
            at = n * GRADS_UNROLL + u
            b, places, far = read_item(item_ref, pos_ref, cnt_ref, at, amount, GRADS_ITEM)
            pair = query_pair(qd_all, b)
            kv, scores, dprobs = item_products(kv_all, pair, places, far)
            probs = jnp.exp(scores - lse_ref[pl.ds(b, 1), :])
            dscores = probs * (dprobs - delta_ref[pl.ds(b, 1), :])
            low = jnp.concatenate([dscores.astype(BF16), probs.astype(BF16)], axis=1)
            terms = jnp.dot(low, pair, preferred_element_type=F32)
            mixed = lax.dot_general(kv, low, TN, preferred_element_type=F32)
            out = jnp.concatenate([mixed[:HEAD_DIM, :BLOCK], mixed[HEAD_DIM:, BLOCK:]], axis=0)
            done.append((b, places, terms, out))
        for b, places, terms, out in done:
            for s, p in enumerate(places):
                key_ref[p] = key_ref[p] + terms[s * BLOCK : (s + 1) * BLOCK]
            query_ref[b] = query_ref[b] + out
        return carry

    lax.fori_loop(0, (amount + GRADS_UNROLL - 1) // GRADS_UNROLL, step, 0)
    y, core = me_ref[0], me_ref[2]

    def spread(n, carry):
        line, i = n // OWN, n % OWN
        own_ref[n] = key_ref[(line * CORES + core) * OWN + i]
        other_ref[n] = key_ref[(line * CORES + 1 - core) * OWN + i].astype(BF16)
        return carry

    lax.fori_loop(0, LINE * OWN, spread, 0)
    for k, hop in enumerate(HOPS):
        line = (y + hop + LINE) % LINE * OWN

        def scaled(i, carry):
            out = query_ref[line + i]
            out = jnp.concatenate([out[:HEAD_DIM] * SCALE, out[HEAD_DIM:]], axis=0)
            y_refs[k][i] = out.astype(y_refs[k].dtype)
            return carry

        lax.fori_loop(0, OWN, scaled, 0)


def core_sum_kernel(me_ref, own_ref, other_ref, *out_refs):
    x = me_ref[1]
    for k, hop in enumerate(HOPS):
        line = (x + hop + LINE) % LINE
        rows = pl.ds(line * OWN, OWN)
        out_refs[k][...] = (own_ref[rows] + other_ref[rows].astype(F32)).astype(out_refs[k].dtype)


def line_sum_kernel(*refs):
    xs, ys, out_ref = refs[:LINE], refs[LINE : 2 * LINE], refs[2 * LINE]
    for at, parts in ((0, xs), (BLOCK, ys)):
        out_ref[:, at : at + BLOCK] = sum(p[...].astype(F32) for p in parts).astype(BF16)


def output_kernel(in_ref, wq_ref, wk_ref, wv_ref, wo_ref, out_ref, grad_ref):
    gk = jnp.concatenate([in_ref[h, :BLOCK, :HEAD_DIM] for h in range(HEADS)], axis=1)
    gv = jnp.concatenate([in_ref[h, :BLOCK, HEAD_DIM:] for h in range(HEADS)], axis=1)
    gq = jnp.concatenate([in_ref[h, BLOCK : BLOCK + HEAD_DIM] for h in range(HEADS)], axis=0)
    att = jnp.concatenate([in_ref[h, BLOCK + HEAD_DIM :] for h in range(HEADS)], axis=0)
    out = lax.dot_general(att, wo_ref[...], TN, preferred_element_type=F32)
    out_ref[...] = out.astype(BF16)
    total = lax.dot_general(
        gq, wq_ref[...], (((0,), (1,)), ((), ())), preferred_element_type=F32
    )
    total = total + lax.dot_general(gk, wk_ref[...], NT, preferred_element_type=F32)
    total = total + lax.dot_general(gv, wv_ref[...], NT, preferred_element_type=F32)
    grad_ref[...] = total.astype(BF16)


def ctx_shift(x, dy=0, dx=0, dc=0):
    pairs = []
    for i in range(LINE * LINE * CORES):
        y, r, c = i // (LINE * CORES), i // CORES % LINE, i % CORES
        to = ((y + dy) % LINE * LINE + (r + dx) % LINE) * CORES + (c + dc) % CORES
        pairs.append((i, to))
    return lax.ppermute(x, "ctx", pairs)


def live_lists(block_cell, cell_mask, y, xc):
    cells = jnp.arange(cell_mask.shape[0], dtype=jnp.int32)
    by_line = block_cell.reshape(LINE, LINE * CORES, OWN)
    q_cell = lax.dynamic_index_in_dim(by_line, xc, 1, keepdims=False).reshape(Q_BLOCKS)
    k_cell = lax.dynamic_slice_in_dim(block_cell, y * K_BLOCKS, K_BLOCKS, 0)
    q_hot = (q_cell[:, None] == cells[None, :]).astype(BF16)
    k_hot = (k_cell[:, None] == cells[None, :]).astype(BF16)
    picked = jnp.dot(q_hot, cell_mask.astype(BF16), preferred_element_type=F32).astype(BF16)
    live = lax.dot_general(picked, k_hot, NT, preferred_element_type=F32)
    at = jnp.arange(K_BLOCKS, dtype=jnp.int32)
    upto = (at[:, None] <= at[None, :]).astype(BF16)
    rank = jnp.dot(live.astype(BF16), upto, preferred_element_type=F32)
    slots = jnp.arange(1, SLOTS + 1, dtype=jnp.int32).astype(F32)
    matched = (live[:, None, :] > 0.5) & (rank[:, None, :] == slots[None, :, None])
    pos = jnp.sum(jnp.where(matched, at[None, None, :], 0), axis=2)
    return pos, jnp.sum(live, axis=1).astype(jnp.int32)


def exchange(x):
    return lax.all_to_all(x, "head", split_axis=0, concat_axis=0, tiled=True)


def scratch_lines():
    return [
        pltpu.VMEM((K_BLOCKS * BLOCK, WIDE), BF16),
        pltpu.VMEM((Q_BLOCKS * BLOCK, WIDE), BF16),
    ]


def scratch_work():
    return [pltpu.SMEM((Q_BLOCKS * SLOTS // STATS_ITEM,), jnp.int32), pltpu.SemaphoreType.DMA((3 * LINE,))]


MIXED = [struct((OWN, BLOCK, WIDE), F32)] + [struct((OWN, BLOCK, WIDE), BF16)] * (LINE - 1)


def stats_call(me, pos, cnt, kvs, qds):
    return call(
        stats_kernel,
        struct((3, Q_BLOCKS, BLOCK), F32),
        [SMEM] * 3 + [VMEM] * (3 * LINE),
        scratch_lines() + scratch_work(),
        "stats",
    )(me, pos, cnt, *near(*kvs, *qds))


def grads_call(me, pos, cnt, stats, kvs, qds):
    return call(
        grads_kernel,
        MIXED + [struct((LINE * OWN, BLOCK, WIDE), F32), struct((LINE * OWN, BLOCK, WIDE), BF16)],
        [SMEM] * 3 + [VMEM] * (4 * LINE),
        scratch_lines()
        + [pltpu.VMEM((K_BLOCKS, BLOCK, WIDE), F32), pltpu.VMEM((Q_BLOCKS, BLOCK, WIDE), F32)]
        + [pltpu.VMEM((Q_BLOCKS, BLOCK), F32)] * 2
        + scratch_work(),
        "grads",
    )(me, pos, cnt, *near(*stats, *kvs, *qds))


def body(hits_in, w_query, w_key, w_value, w_out, grad_y, block_cell, cell_mask):
    rows = OWN * BLOCK
    ctx = lax.axis_index("ctx")
    y, x, core = ctx // (LINE * CORES), ctx // CORES % LINE, ctx % CORES
    me = jnp.stack([y, x, core]).astype(jnp.int32)
    pos, cnt = live_lists(block_cell, cell_mask, y, ctx % (LINE * CORES))

    wide = (HEADS, 2 * BLOCK, WIDE)
    given = (hits_in, w_key, w_value, w_query, grad_y, w_out)
    sent = call(
        project_kernel,
        struct(wide, BF16),
        [ANY] * 6,
        [pltpu.VMEM(g.shape, BF16) for g in given] + [pltpu.SemaphoreType.DMA((6,))],
        "project",
    )(*[pltpu.with_memory_space_constraint(g, pltpu.HBM) for g in given])
    got, pos, cnt, me = lax.optimization_barrier((exchange(sent), pos, cnt, me))
    kv = got[:, :BLOCK].reshape(rows, WIDE)
    qd = got[:, BLOCK:].reshape(rows, WIDE)
    kvs = [kv] + [ctx_shift(kv, dx=hop) for hop in HOPS[1:]]
    kvs = kvs + [ctx_shift(piece, dc=1) for piece in kvs]
    qds = [qd] + [ctx_shift(qd, dy=hop) for hop in HOPS[1:]]

    stats = stats_call(me, pos, cnt, kvs, qds)
    all_stats = [stats] + [ctx_shift(stats, dy=hop) for hop in HOPS[1:]]
    *y_parts, own, other = grads_call(me, pos, cnt, all_stats, kvs, qds)
    y_parts = [y_parts[0]] + [ctx_shift(p, dy=hop) for p, hop in zip(y_parts[1:], HOPS[1:])]
    other = ctx_shift(other, dc=1)
    x_parts = call(core_sum_kernel, MIXED, [SMEM, VMEM, VMEM], name="core_sum")(me, *near(own, other))
    x_parts = [x_parts[0]] + [ctx_shift(p, dx=hop) for p, hop in zip(x_parts[1:], HOPS[1:])]
    summed = call(line_sum_kernel, struct(wide, BF16), [VMEM] * (2 * LINE), name="line_sum")(
        *near(*x_parts, *y_parts)
    )
    full = struct(hits_in.shape, BF16)
    return call(output_kernel, (full, full), [VMEM] * 5, name="output")(
        *near(exchange(summed), w_query, w_key, w_value, w_out)
    )


def solution(mesh):
    row = P(("ctx", "head"), None)
    return jax.shard_map(
        body,
        mesh=mesh,
        in_specs=(row, P(), P(), P(), P(), row, P(), P()),
        out_specs=(row, row),
        check_vma=False,
    )
```

time: 161 us -> 129 us (0.80)
  the two profiles are of different devices: /device:TPU:32 before, /device:TPU:6 now
where the time goes in v3:
time: 129 us; the launch traced here: 128 us
  waiting for transfers between devices  43.6 us (34%)
  starting transfers between devices  34.9 us (27%)
  Pallas kernels  27.3 us (21%)
  blocking collectives  19.4 us (15%)
    ppermute x20, waiting for transfers between devices, ctx_shift(): return lax.ppermute(x, 'ctx', pairs)  27.8 us
    ppermute x20, starting transfers between devices, ctx_shift(): return lax.ppermute(x, 'ctx', pairs)  26.5 us
    all_to_all x1, blocking collectives, exchange(): return lax.all_to_all(x, 'head', split_axis=0, concat_axis=0, tiled=True)  19.4 us
    all_to_all x1, waiting for transfers between devices, exchange(): return lax.all_to_all(x, 'head', split_axis=0, concat_axis=0, tiled=True)  15.9 us
    pallas_call x1, Pallas kernels, grads_call(): call(grads_kernel, MIXED + [struct((LINE * OWN, BLOCK, WIDE), F32), struc...  13.7 us
    all_to_all x1, starting transfers between devices, exchange(): return lax.all_to_all(x, 'head', split_axis=0, concat_axis=0, tiled=True)  8.48 us
    pallas_call x1, Pallas kernels, stats_call(): call(stats_kernel, struct((3, Q_BLOCKS, BLOCK), F32), [SMEM] * 3 + [VMEM]...  6.77 us
    pallas_call x1, Pallas kernels, body(): call(project_kernel, struct(wide, BF16), [ANY] * 6, [pltpu.VMEM(g.shape,...  3.78 us
  transfers between devices with their start and end apart: 21, of which 10 were waited for; matrix products, arithmetic and copies ran while one was open for 1% of the time, Pallas kernels for 1%

profile of v3, /device:TPU:6, one launch (start us, length us, event | category | flops | bytes accessed | tf_op | source)
XLA Modules:
  0.0 127.7 jit_solution(13503433232585439545)
XLA Ops:
  0.7 3.8 %project.1 = bf16[8,256,128]{2,1,0:T(8,128)(2,1)} custom-call(bf16[128,1024]{1,0:T(8,128)(2,1)} %refs_0_.1, bf16[1024,512]{1,0:T(8,128)(2,1)} %wk_ref.1, bf16[1024,512]{1,0:T(8,128)(2,1)} %wv_ref.1, bf16[1024,512]{1,0:T(8,128)(2,1)} %wq_ref.1, bf16[128,1024]{1,0:T(8,128)(2,1)} %refs_4_.1, bf16[512,1024]{1,0:T(8,128)(2,1)} %wo_ref.1), custom_call_target="tpu_custom_call" | custom-call | tf_op jit(solution)/shard_map/project/pallas_call | solution.py:343
  4.4 8.5 %all-to-all-start = ((bf16[8,256,128]{2,1,0:T(8,128)(2,1)}), bf16[8,256,128]{2,1,0:T(8,128)(2,1)S(1)}, u32[]{:S(2)}, u32[]{:S(2)}) async-start(bf16[8,256,128]{2,1,0:T(8,128)(2,1)} %project.1), calls=%async_computation | async-start | bytes 1048576 | tf_op jit(solution)/shard_map/all_to_all | solution.py:294
  13.2 0.3 broadcast_compare_fusion
  13.9 0.7 select_reduce_fusion.pos_ref
  14.6 15.9 %all-to-all-done = bf16[8,256,128]{2,1,0:T(8,128)(2,1)S(1)} async-done(((bf16[8,256,128]{2,1,0:T(8,128)(2,1)}), bf16[8,256,128]{2,1,0:T(8,128)(2,1)S(1)}, u32[]{:S(2)}, u32[]{:S(2)}) %all-to-all-start) | async-done | bytes 524320 | tf_op jit(solution)/shard_map/all_to_all | solution.py:294
  30.5 3.3 %collective-permute-start.9 = (bf16[1024,128]{1,0:T(8,128)(2,1)S(1)}, bf16[1024,128]{1,0:T(8,128)(2,1)S(1)}, u32[]{:S(2)}, u32[]{:S(2)}) collective-permute-start(bf16[1024,128]{1,0:T(8,128)(2,1)S(1)} %bitcast.5), channel_id=1, source_target_pairs={{0,128},{8,136},{16,144},{24,152},{32,160},{40,168},{48,176},{56,1... | collective-permute-start | bytes 786440 | tf_op jit(solution)/shard_map/ppermute | solution.py:272
  33.7 1.1 collective-permute-start.8
  34.8 1.4 %collective-permute-start.2 = (bf16[1024,128]{1,0:T(8,128)(2,1)S(1)}, bf16[1024,128]{1,0:T(8,128)(2,1)S(1)}, u32[]{:S(2)}, u32[]{:S(2)}) collective-permute-start(bf16[1024,128]{1,0:T(8,128)(2,1)S(1)} %bitcast.10), channel_id=1, source_target_pairs={{0,32},{8,40},{16,48},{24,56},{32,0},{40,8},{48,16},{56,24},{64,96... | collective-permute-start | bytes 786440 | tf_op jit(solution)/shard_map/ppermute | solution.py:272
  36.2 3.2 %collective-permute-start = (bf16[1024,128]{1,0:T(8,128)(2,1)S(1)}, bf16[1024,128]{1,0:T(8,128)(2,1)S(1)}, u32[]{:S(2)}, u32[]{:S(2)}) collective-permute-start(bf16[1024,128]{1,0:T(8,128)(2,1)S(1)} %bitcast.12), channel_id=1, source_target_pairs={{0,16},{8,24},{16,32},{24,40},{32,48},{40,56},{48,0},{56,8},{64,80... | collective-permute-start | bytes 786440 | tf_op jit(solution)/shard_map/ppermute | solution.py:272
  39.4 0.8 collective-permute-done.9.rest_11_.rest_15_
  40.3 2.6 %collective-permute-start.7 = (bf16[1024,128]{1,0:T(8,128)(2,1)S(1)}, bf16[1024,128]{1,0:T(8,128)(2,1)S(1)}, u32[]{:S(2)}, u32[]{:S(2)}) collective-permute-start(bf16[1024,128]{1,0:T(8,128)(2,1)S(1)} %bitcast.7), channel_id=1, source_target_pairs={{0,64},{8,72},{16,80},{24,88},{32,96},{40,104},{48,112},{56,120},{... | collective-permute-start | bytes 786440 | tf_op jit(solution)/shard_map/ppermute | solution.py:272
  42.8 3.4 %collective-permute-done.8.rest_10_.rest_14_ = bf16[1024,128]{1,0:T(8,128)(2,1)S(1)} collective-permute-done((bf16[1024,128]{1,0:T(8,128)(2,1)S(1)}, bf16[1024,128]{1,0:T(8,128)(2,1)S(1)}, u32[]{:S(2)}, u32[]{:S(2)}) %collective-permute-start.8) | collective-permute-done | bytes 262176 | tf_op jit(solution)/shard_map/ppermute | solution.py:272
  46.3 0.5 collective-permute-start.6
  46.8 2.8 %collective-permute-done.1.rest_2_.rest_6_ = bf16[1024,128]{1,0:T(8,128)(2,1)S(1)} collective-permute-done((bf16[1024,128]{1,0:T(8,128)(2,1)S(1)}, bf16[1024,128]{1,0:T(8,128)(2,1)S(1)}, u32[]{:S(2)}, u32[]{:S(2)}) %collective-permute-start.1) | collective-permute-done | bytes 262176 | tf_op jit(solution)/shard_map/ppermute | solution.py:272
  49.6 0.5 collective-permute-start.4
  50.1 1.0 collective-permute-done.5.rest_6_.rest_10_
  51.1 0.4 collective-permute-done.4.rest_5_.rest_9_
  51.5 6.8 %stats.1.rest_0_ = f32[3,32,128]{2,1,0:T(8,128)S(1)} custom-call(s32[3]{0:T(128)S(1)} %pad_add_fusion.me_ref, s32[32,24]{1,0:T(8,128)S(1)} %select_reduce_fusion.pos_ref, s32[32]{0:T(128)S(1)} %convert_element_type.26.cnt_ref, bf16[1024,128]{1,0:T(8,128)(2,1)S(1)} %bitcast.14, bf16[1024,128]{1,0:T(8,128)(2,1)S(1)} %collective-permute-done.rest_1_.rest_5_, ...), custom_call_target="tpu_custom_call" | custom-call | tf_op jit(solution)/shard_map/stats/pallas_call | solution.py:312
  58.3 1.8 %collective-permute-start.12 = (f32[3,32,128]{2,1,0:T(8,128)S(1)}, f32[3,32,128]{2,1,0:T(8,128)S(1)}, u32[]{:S(2)}, u32[]{:S(2)}) collective-permute-start(f32[3,32,128]{2,1,0:T(8,128)S(1)} %stats.1.rest_0_), channel_id=1, source_target_pairs={{0,128},{8,136},{16,144},{24,152},{32,160},{40,168},{48,176},{56,1... | collective-permute-start | bytes 147464 | tf_op jit(solution)/shard_map/ppermute | solution.py:272
  60.0 2.0 %collective-permute-start.11 = (f32[3,32,128]{2,1,0:T(8,128)S(1)}, f32[3,32,128]{2,1,0:T(8,128)S(1)}, u32[]{:S(2)}, u32[]{:S(2)}) collective-permute-start(f32[3,32,128]{2,1,0:T(8,128)S(1)} %stats.1.rest_0_), channel_id=1, source_target_pairs={{0,192},{8,200},{16,208},{24,216},{32,224},{40,232},{48,240},{56,2... | collective-permute-start | bytes 147464 | tf_op jit(solution)/shard_map/ppermute | solution.py:272
  62.1 2.4 %collective-permute-done.12.rest_3_ = f32[3,32,128]{2,1,0:T(8,128)S(1)} collective-permute-done((f32[3,32,128]{2,1,0:T(8,128)S(1)}, f32[3,32,128]{2,1,0:T(8,128)S(1)}, u32[]{:S(2)}, u32[]{:S(2)}) %collective-permute-start.12) | collective-permute-done | bytes 49184 | tf_op jit(solution)/shard_map/ppermute | solution.py:272
  64.5 2.8 %collective-permute-done.10.rest_1_ = f32[3,32,128]{2,1,0:T(8,128)S(1)} collective-permute-done((f32[3,32,128]{2,1,0:T(8,128)S(1)}, f32[3,32,128]{2,1,0:T(8,128)S(1)}, u32[]{:S(2)}, u32[]{:S(2)}) %collective-permute-start.10) | collective-permute-done | bytes 49184 | tf_op jit(solution)/shard_map/ppermute | solution.py:272
  67.3 13.7 %grads.1 = (f32[8,128,128]{2,1,0:T(8,128)S(1)}, bf16[8,128,128]{2,1,0:T(8,128)(2,1)S(1)}, bf16[8,128,128]{2,1,0:T(8,128)(2,1)S(1)}, bf16[8,128,128]{2,1,0:T(8,12...) custom-call(s32[3]{0:T(128)S(1)} %pad_add_fusion.me_ref, ...), custom_call_target="tpu_custom_call" | custom-call | tf_op jit(solution)/shard_map/grads/pallas_call | solution.py:322
  81.2 3.2 %collective-permute-start.18 = (bf16[8,128,128]{2,1,0:T(8,128)(2,1)S(1)}, bf16[8,128,128]{2,1,0:T(8,128)(2,1)S(1)}, u32[]{:S(2)}, u32[]{:S(2)}) collective-permute-start(bf16[8,128,128]{2,1,0:T(8,128)(2,1)S(1)} %get-tuple-element.28), channel_id=1, source_target_pairs={{0,192},{8,200},{16,208},{24,216},{32,224},{40,232},{48,240},{56,2... | collective-permute-start | bytes 786440 | tf_op jit(solution)/shard_map/ppermute | solution.py:272
  84.4 0.9 collective-permute-start.19
  85.3 0.8 core_sum.1
  86.2 2.6 %collective-permute-start.15 = (bf16[8,128,128]{2,1,0:T(8,128)(2,1)S(1)}, bf16[8,128,128]{2,1,0:T(8,128)(2,1)S(1)}, u32[]{:S(2)}, u32[]{:S(2)}) collective-permute-start(bf16[8,128,128]{2,1,0:T(8,128)(2,1)S(1)} %get-tuple-element.24), channel_id=1, source_target_pairs={{0,48},{8,56},{16,0},{24,8},{32,16},{40,24},{48,32},{56,40},{64,11... | collective-permute-start | bytes 786440 | tf_op jit(solution)/shard_map/ppermute | solution.py:272
  88.8 7.9 %collective-permute-done.17.refs_5_ = bf16[8,128,128]{2,1,0:T(8,128)(2,1)S(1)} collective-permute-done((bf16[8,128,128]{2,1,0:T(8,128)(2,1)S(1)}, bf16[8,128,128]{2,1,0:T(8,128)(2,1)S(1)}, u32[]{:S(2)}, u32[]{:S(2)}) %collective-permute-start.17) | collective-permute-done | bytes 262176 | tf_op jit(solution)/shard_map/ppermute | solution.py:272
  96.7 3.1 %collective-permute-start.16 = (bf16[8,128,128]{2,1,0:T(8,128)(2,1)S(1)}, bf16[8,128,128]{2,1,0:T(8,128)(2,1)S(1)}, u32[]{:S(2)}, u32[]{:S(2)}) collective-permute-start(bf16[8,128,128]{2,1,0:T(8,128)(2,1)S(1)} %get-tuple-element.25), channel_id=1, source_target_pairs={{0,32},{8,40},{16,48},{24,56},{32,0},{40,8},{48,16},{56,24},{64,96... | collective-permute-start | bytes 786440 | tf_op jit(solution)/shard_map/ppermute | solution.py:272
  99.8 6.2 %collective-permute-done.16.refs_3_ = bf16[8,128,128]{2,1,0:T(8,128)(2,1)S(1)} collective-permute-done((bf16[8,128,128]{2,1,0:T(8,128)(2,1)S(1)}, bf16[8,128,128]{2,1,0:T(8,128)(2,1)S(1)}, u32[]{:S(2)}, u32[]{:S(2)}) %collective-permute-start.16) | collective-permute-done | bytes 262176 | tf_op jit(solution)/shard_map/ppermute | solution.py:272
  106.3 19.4 %all_to_all.10.in_ref = bf16[8,256,128]{2,1,0:T(8,128)(2,1)S(1)} all-to-all(bf16[8,256,128]{2,1,0:T(8,128)(2,1)S(1)} %line_sum.1), channel_id=1, replica_groups=mesh['ctx'=32,'head'=8] {'head'}, dimensions={0} | all-to-all | bytes 1048576 | tf_op jit(solution)/shard_map/all_to_all | solution.py:294
  125.6 2.0 %output.1 = (bf16[128,1024]{1,0:T(8,128)(2,1)}, bf16[128,1024]{1,0:T(8,128)(2,1)}) custom-call(bf16[8,256,128]{2,1,0:T(8,128)(2,1)S(1)} %all_to_all.10.in_ref, bf16[1024,512]{1,0:T(8,128)(2,1)S(1)} %copy-done.2, bf16[1024,512]{1,0:T(8,128)(2,1)S(1)} %copy-done, bf16[1024,512]{1,0:T(8,128)(2,1)S(1)} %copy-done.1, bf16[512,1024]{1,0:T(8,128)(2,1)S(1)} %copy-done.3), custom_call_target="tpu_custom_call" | custom-call | tf_op jit(solution)/shard_map/output/pallas_call | solution.py:368
  (41 shorter events, 1.3 us)
Async XLA Ops:
  0.6 12.3 %copy-start.5 = (s32[256]{0:T(256)S(1)}, s32[256]{0:T(256)}, u32[]{:S(2)}) copy-start(s32[256]{0:T(256)} %param.14) | copy-start | bytes 3076
  0.6 12.6 %copy-start.4 = (s32[256,256]{1,0:T(8,128)S(1)}, s32[256,256]{1,0:T(8,128)}, u32[]{:S(2)}) copy-start(s32[256,256]{1,0:T(8,128)} %param.15) | copy-start | bytes 786436
  4.4 26.0 %all-to-all-start = ((bf16[8,256,128]{2,1,0:T(8,128)(2,1)}), bf16[8,256,128]{2,1,0:T(8,128)(2,1)S(1)}, u32[]{:S(2)}, u32[]{:S(2)}) async-start(bf16[8,256,128]{2,1,0:T(8,128)(2,1)} %project.1), calls=%async_computation | async-start | bytes 1048576 | tf_op jit(solution)/shard_map/all_to_all | solution.py:294
  30.5 9.8 %collective-permute-start.9 = (bf16[1024,128]{1,0:T(8,128)(2,1)S(1)}, bf16[1024,128]{1,0:T(8,128)(2,1)S(1)}, u32[]{:S(2)}, u32[]{:S(2)}) collective-permute-start(bf16[1024,128]{1,0:T(8,128)(2,1)S(1)} %bitcast.5), channel_id=1, source_target_pairs={{0,128},{8,136},{16,144},{24,152},{32,160},{40,168},{48,176},{56,1... | collective-permute-start | bytes 786440 | tf_op jit(solution)/shard_map/ppermute | solution.py:272
  33.7 12.5 %collective-permute-start.8 = (bf16[1024,128]{1,0:T(8,128)(2,1)S(1)}, bf16[1024,128]{1,0:T(8,128)(2,1)S(1)}, u32[]{:S(2)}, u32[]{:S(2)}) collective-permute-start(bf16[1024,128]{1,0:T(8,128)(2,1)S(1)} %bitcast.6), channel_id=1, source_target_pairs={{0,192},{8,200},{16,208},{24,216},{32,224},{40,232},{48,240},{56,2... | collective-permute-start | bytes 786440 | tf_op jit(solution)/shard_map/ppermute | solution.py:272
  34.8 11.5 %collective-permute-start.2 = (bf16[1024,128]{1,0:T(8,128)(2,1)S(1)}, bf16[1024,128]{1,0:T(8,128)(2,1)S(1)}, u32[]{:S(2)}, u32[]{:S(2)}) collective-permute-start(bf16[1024,128]{1,0:T(8,128)(2,1)S(1)} %bitcast.10), channel_id=1, source_target_pairs={{0,32},{8,40},{16,48},{24,56},{32,0},{40,8},{48,16},{56,24},{64,96... | collective-permute-start | bytes 786440 | tf_op jit(solution)/shard_map/ppermute | solution.py:272
  36.2 13.4 %collective-permute-start.1 = (bf16[1024,128]{1,0:T(8,128)(2,1)S(1)}, bf16[1024,128]{1,0:T(8,128)(2,1)S(1)}, u32[]{:S(2)}, u32[]{:S(2)}) collective-permute-start(bf16[1024,128]{1,0:T(8,128)(2,1)S(1)} %bitcast.11), channel_id=1, source_target_pairs={{0,48},{8,56},{16,0},{24,8},{32,16},{40,24},{48,32},{56,40},{64,11... | collective-permute-start | bytes 786440 | tf_op jit(solution)/shard_map/ppermute | solution.py:272
  36.2 13.4 %collective-permute-start = (bf16[1024,128]{1,0:T(8,128)(2,1)S(1)}, bf16[1024,128]{1,0:T(8,128)(2,1)S(1)}, u32[]{:S(2)}, u32[]{:S(2)}) collective-permute-start(bf16[1024,128]{1,0:T(8,128)(2,1)S(1)} %bitcast.12), channel_id=1, source_target_pairs={{0,16},{8,24},{16,32},{24,40},{32,48},{40,56},{48,0},{56,8},{64,80... | collective-permute-start | bytes 786440 | tf_op jit(solution)/shard_map/ppermute | solution.py:272
  40.3 9.8 %collective-permute-start.7 = (bf16[1024,128]{1,0:T(8,128)(2,1)S(1)}, bf16[1024,128]{1,0:T(8,128)(2,1)S(1)}, u32[]{:S(2)}, u32[]{:S(2)}) collective-permute-start(bf16[1024,128]{1,0:T(8,128)(2,1)S(1)} %bitcast.7), channel_id=1, source_target_pairs={{0,64},{8,72},{16,80},{24,88},{32,96},{40,104},{48,112},{56,120},{... | collective-permute-start | bytes 786440 | tf_op jit(solution)/shard_map/ppermute | solution.py:272
  46.3 3.8 %collective-permute-start.3 = (bf16[1024,128]{1,0:T(8,128)(2,1)S(1)}, bf16[1024,128]{1,0:T(8,128)(2,1)S(1)}, u32[]{:S(2)}, u32[]{:S(2)}) collective-permute-start(bf16[1024,128]{1,0:T(8,128)(2,1)S(1)} %bitcast.13), channel_id=1, source_target_pairs={{0,8},{8,0},{16,24},{24,16},{32,40},{40,32},{48,56},{56,48},{64,72... | collective-permute-start | bytes 786440 | tf_op jit(solution)/shard_map/ppermute | solution.py:272
  46.3 3.8 %collective-permute-start.6 = (bf16[1024,128]{1,0:T(8,128)(2,1)S(1)}, bf16[1024,128]{1,0:T(8,128)(2,1)S(1)}, u32[]{:S(2)}, u32[]{:S(2)}) collective-permute-start(bf16[1024,128]{1,0:T(8,128)(2,1)S(1)} %collective-permute-done.2.rest_3_.rest_7_), channel_id=1, source_target_pairs={{0,8},{8,0},{16,24},{24,16},{32,40},{40,32},{48,56},{56,48},{64,72... | collective-permute-start | bytes 786440 | tf_op jit(solution)/shard_map/ppermute | solution.py:272
  49.6 1.5 %collective-permute-start.5 = (bf16[1024,128]{1,0:T(8,128)(2,1)S(1)}, bf16[1024,128]{1,0:T(8,128)(2,1)S(1)}, u32[]{:S(2)}, u32[]{:S(2)}) collective-permute-start(bf16[1024,128]{1,0:T(8,128)(2,1)S(1)} %collective-permute-done.1.rest_2_.rest_6_), channel_id=1, source_target_pairs={{0,8},{8,0},{16,24},{24,16},{32,40},{40,32},{48,56},{56,48},{64,72... | collective-permute-start | bytes 786440 | tf_op jit(solution)/shard_map/ppermute | solution.py:272
  49.6 1.9 %collective-permute-start.4 = (bf16[1024,128]{1,0:T(8,128)(2,1)S(1)}, bf16[1024,128]{1,0:T(8,128)(2,1)S(1)}, u32[]{:S(2)}, u32[]{:S(2)}) collective-permute-start(bf16[1024,128]{1,0:T(8,128)(2,1)S(1)} %collective-permute-done.rest_1_.rest_5_), channel_id=1, source_target_pairs={{0,8},{8,0},{16,24},{24,16},{32,40},{40,32},{48,56},{56,48},{64,72... | collective-permute-start | bytes 786440 | tf_op jit(solution)/shard_map/ppermute | solution.py:272
  58.3 6.2 %collective-permute-start.12 = (f32[3,32,128]{2,1,0:T(8,128)S(1)}, f32[3,32,128]{2,1,0:T(8,128)S(1)}, u32[]{:S(2)}, u32[]{:S(2)}) collective-permute-start(f32[3,32,128]{2,1,0:T(8,128)S(1)} %stats.1.rest_0_), channel_id=1, source_target_pairs={{0,128},{8,136},{16,144},{24,152},{32,160},{40,168},{48,176},{56,1... | collective-permute-start | bytes 147464 | tf_op jit(solution)/shard_map/ppermute | solution.py:272
  60.0 4.5 %collective-permute-start.11 = (f32[3,32,128]{2,1,0:T(8,128)S(1)}, f32[3,32,128]{2,1,0:T(8,128)S(1)}, u32[]{:S(2)}, u32[]{:S(2)}) collective-permute-start(f32[3,32,128]{2,1,0:T(8,128)S(1)} %stats.1.rest_0_), channel_id=1, source_target_pairs={{0,192},{8,200},{16,208},{24,216},{32,224},{40,232},{48,240},{56,2... | collective-permute-start | bytes 147464 | tf_op jit(solution)/shard_map/ppermute | solution.py:272
  62.0 5.3 %collective-permute-start.10 = (f32[3,32,128]{2,1,0:T(8,128)S(1)}, f32[3,32,128]{2,1,0:T(8,128)S(1)}, u32[]{:S(2)}, u32[]{:S(2)}) collective-permute-start(f32[3,32,128]{2,1,0:T(8,128)S(1)} %stats.1.rest_0_), channel_id=1, source_target_pairs={{0,64},{8,72},{16,80},{24,88},{32,96},{40,104},{48,112},{56,120},{... | collective-permute-start | bytes 147464 | tf_op jit(solution)/shard_map/ppermute | solution.py:272
  81.0 4.3 %collective-permute-start.13 = (bf16[32,128,128]{2,1,0:T(8,128)(2,1)S(1)}, bf16[32,128,128]{2,1,0:T(8,128)(2,1)S(1)}, u32[]{:S(2)}, u32[]{:S(2)}) collective-permute-start(bf16[32,128,128]{2,1,0:T(8,128)(2,1)S(1)} %get-tuple-element.21), channel_id=1, source_target_pairs={{0,8},{8,0},{16,24},{24,16},{32,40},{40,32},{48,56},{56,48},{64,72... | collective-permute-start | bytes 3145736 | tf_op jit(solution)/shard_map/ppermute | solution.py:272
  81.1 15.6 %collective-permute-start.17 = (bf16[8,128,128]{2,1,0:T(8,128)(2,1)S(1)}, bf16[8,128,128]{2,1,0:T(8,128)(2,1)S(1)}, u32[]{:S(2)}, u32[]{:S(2)}) collective-permute-start(bf16[8,128,128]{2,1,0:T(8,128)(2,1)S(1)} %get-tuple-element.27), channel_id=1, source_target_pairs={{0,64},{8,72},{16,80},{24,88},{32,96},{40,104},{48,112},{56,120},{... | collective-permute-start | bytes 786440 | tf_op jit(solution)/shard_map/ppermute | solution.py:272
  81.2 18.6 %collective-permute-start.18 = (bf16[8,128,128]{2,1,0:T(8,128)(2,1)S(1)}, bf16[8,128,128]{2,1,0:T(8,128)(2,1)S(1)}, u32[]{:S(2)}, u32[]{:S(2)}) collective-permute-start(bf16[8,128,128]{2,1,0:T(8,128)(2,1)S(1)} %get-tuple-element.28), channel_id=1, source_target_pairs={{0,192},{8,200},{16,208},{24,216},{32,224},{40,232},{48,240},{56,2... | collective-permute-start | bytes 786440 | tf_op jit(solution)/shard_map/ppermute | solution.py:272
  84.4 15.4 %collective-permute-start.19 = (bf16[8,128,128]{2,1,0:T(8,128)(2,1)S(1)}, bf16[8,128,128]{2,1,0:T(8,128)(2,1)S(1)}, u32[]{:S(2)}, u32[]{:S(2)}) collective-permute-start(bf16[8,128,128]{2,1,0:T(8,128)(2,1)S(1)} %get-tuple-element.29), channel_id=1, source_target_pairs={{0,128},{8,136},{16,144},{24,152},{32,160},{40,168},{48,176},{56,1... | collective-permute-start | bytes 786440 | tf_op jit(solution)/shard_map/ppermute | solution.py:272
  86.1 13.7 %collective-permute-start.14 = (bf16[8,128,128]{2,1,0:T(8,128)(2,1)S(1)}, bf16[8,128,128]{2,1,0:T(8,128)(2,1)S(1)}, u32[]{:S(2)}, u32[]{:S(2)}) collective-permute-start(bf16[8,128,128]{2,1,0:T(8,128)(2,1)S(1)} %get-tuple-element.23), channel_id=1, source_target_pairs={{0,16},{8,24},{16,32},{24,40},{32,48},{40,56},{48,0},{56,8},{64,80... | collective-permute-start | bytes 786440 | tf_op jit(solution)/shard_map/ppermute | solution.py:272
  86.2 13.6 %collective-permute-start.15 = (bf16[8,128,128]{2,1,0:T(8,128)(2,1)S(1)}, bf16[8,128,128]{2,1,0:T(8,128)(2,1)S(1)}, u32[]{:S(2)}, u32[]{:S(2)}) collective-permute-start(bf16[8,128,128]{2,1,0:T(8,128)(2,1)S(1)} %get-tuple-element.24), channel_id=1, source_target_pairs={{0,48},{8,56},{16,0},{24,8},{32,16},{40,24},{48,32},{56,40},{64,11... | collective-permute-start | bytes 786440 | tf_op jit(solution)/shard_map/ppermute | solution.py:272
  96.7 9.4 %collective-permute-start.16 = (bf16[8,128,128]{2,1,0:T(8,128)(2,1)S(1)}, bf16[8,128,128]{2,1,0:T(8,128)(2,1)S(1)}, u32[]{:S(2)}, u32[]{:S(2)}) collective-permute-start(bf16[8,128,128]{2,1,0:T(8,128)(2,1)S(1)} %get-tuple-element.25), channel_id=1, source_target_pairs={{0,32},{8,40},{16,48},{24,56},{32,0},{40,8},{48,16},{56,24},{64,96... | collective-permute-start | bytes 786440 | tf_op jit(solution)/shard_map/ppermute | solution.py:272
  106.0 19.6 %copy-start = (bf16[1024,512]{1,0:T(8,128)(2,1)S(1)}, bf16[1024,512]{1,0:T(8,128)(2,1)}, u32[]{:S(2)}) copy-start(bf16[1024,512]{1,0:T(8,128)(2,1)} %wk_ref.1) | copy-start | bytes 3145732
  106.0 19.6 %copy-start.1 = (bf16[1024,512]{1,0:T(8,128)(2,1)S(1)}, bf16[1024,512]{1,0:T(8,128)(2,1)}, u32[]{:S(2)}) copy-start(bf16[1024,512]{1,0:T(8,128)(2,1)} %wv_ref.1) | copy-start | bytes 3145732
  106.0 19.6 %copy-start.2 = (bf16[1024,512]{1,0:T(8,128)(2,1)S(1)}, bf16[1024,512]{1,0:T(8,128)(2,1)}, u32[]{:S(2)}) copy-start(bf16[1024,512]{1,0:T(8,128)(2,1)} %wq_ref.1) | copy-start | bytes 3145732
  106.0 19.6 %copy-start.3 = (bf16[512,1024]{1,0:T(8,128)(2,1)S(1)}, bf16[512,1024]{1,0:T(8,128)(2,1)}, u32[]{:S(2)}) copy-start(bf16[512,1024]{1,0:T(8,128)(2,1)} %wo_ref.1) | copy-start | bytes 3145732

commit v4 on v3

--- a/solution.py
+++ b/solution.py
@@ -16,7 +16,8 @@
 STATS_ITEM = 2
 GRADS_ITEM = 4
 STATS_UNROLL = 8
-GRADS_UNROLL = 4
+WHOLE_UNROLL = 6
+HALF_UNROLL = 6
 LINE = 4
 CORES = 2
 OWN = 8
@@ -118,6 +119,26 @@
         return lax.fori_loop(0, (cnt_ref[b] + size - 1) // size, put, at)
 
     return lax.fori_loop(0, Q_BLOCKS, one, 0)
+
+
+def build_halves(cnt_ref, whole_ref, half_ref):
+    half = GRADS_ITEM // 2
+
+    def one(b, at):
+        wholes, halves = at
+        left = cnt_ref[b] % GRADS_ITEM
+        short = jnp.where((left > 0) & (left <= half), 1, 0)
+        amount = (cnt_ref[b] + half - 1) // GRADS_ITEM
+
+        def put(j, at):
+            whole_ref[at] = b * 16 + j
+            return at + 1
+
+        wholes = lax.fori_loop(0, amount, put, wholes)
+        half_ref[halves] = b * 16 + 2 * amount
+        return wholes, halves + short
+
+    return lax.fori_loop(0, Q_BLOCKS, one, (0, 0))
 
 
 def read_item(item_ref, pos_ref, cnt_ref, at, amount, size):
@@ -177,7 +198,8 @@
     stats, rest = rest[:LINE], rest[LINE:]
     kv_pieces, qd_pieces, rest = rest[: 2 * LINE], rest[2 * LINE : 3 * LINE], rest[3 * LINE :]
     y_refs, rest = rest[:LINE], rest[LINE:]
-    own_ref, other_ref, kv_all, qd_all, key_ref, query_ref, lse_ref, delta_ref, item_ref, sems = rest
+    own_ref, other_ref, kv_all, qd_all, key_ref, query_ref = rest[:6]
+    lse_ref, delta_ref, whole_ref, half_ref, sems = rest[6:]
     copies = load_lines(me_ref, kv_pieces, qd_pieces, kv_all, qd_all, sems)
 
     top = functools.reduce(jnp.maximum, [s[0] for s in stats])
@@ -188,31 +210,35 @@
     delta_ref[...] = dot / total
     key_ref[...] = jnp.zeros_like(key_ref)
     query_ref[...] = jnp.zeros_like(query_ref)
-    amount = build_items(cnt_ref, item_ref, GRADS_ITEM)
+    wholes, halves = build_halves(cnt_ref, whole_ref, half_ref)
     for copy in copies:
         copy.wait()
 
-    def step(n, carry):
-        done = []
-        for u in range(GRADS_UNROLL):
-            at = n * GRADS_UNROLL + u
-            b, places, far = read_item(item_ref, pos_ref, cnt_ref, at, amount, GRADS_ITEM)
-            pair = query_pair(qd_all, b)
-            kv, scores, dprobs = item_products(kv_all, pair, places, far)
-            probs = jnp.exp(scores - lse_ref[pl.ds(b, 1), :])
-            dscores = probs * (dprobs - delta_ref[pl.ds(b, 1), :])
-            low = jnp.concatenate([dscores.astype(BF16), probs.astype(BF16)], axis=1)
-            terms = jnp.dot(low, pair, preferred_element_type=F32)
-            mixed = lax.dot_general(kv, low, TN, preferred_element_type=F32)
-            out = jnp.concatenate([mixed[:HEAD_DIM, :BLOCK], mixed[HEAD_DIM:, BLOCK:]], axis=0)
-            done.append((b, places, terms, out))
-        for b, places, terms, out in done:
-            for s, p in enumerate(places):
-                key_ref[p] = key_ref[p] + terms[s * BLOCK : (s + 1) * BLOCK]
-            query_ref[b] = query_ref[b] + out
-        return carry
-
-    lax.fori_loop(0, (amount + GRADS_UNROLL - 1) // GRADS_UNROLL, step, 0)
+    def run(item_ref, amount, size, unroll):
+        def step(n, carry):
+            done = []
+            for u in range(unroll):
+                at = n * unroll + u
+                b, places, far = read_item(item_ref, pos_ref, cnt_ref, at, amount, size)
+                pair = query_pair(qd_all, b)
+                kv, scores, dprobs = item_products(kv_all, pair, places, far)
+                probs = jnp.exp(scores - lse_ref[pl.ds(b, 1), :])
+                dscores = probs * (dprobs - delta_ref[pl.ds(b, 1), :])
+                low = jnp.concatenate([dscores.astype(BF16), probs.astype(BF16)], axis=1)
+                terms = jnp.dot(low, pair, preferred_element_type=F32)
+                mixed = lax.dot_general(kv, low, TN, preferred_element_type=F32)
+                out = jnp.concatenate([mixed[:HEAD_DIM, :BLOCK], mixed[HEAD_DIM:, BLOCK:]], axis=0)
+                done.append((b, places, terms, out))
+            for b, places, terms, out in done:
+                for s, p in enumerate(places):
+                    key_ref[p] = key_ref[p] + terms[s * BLOCK : (s + 1) * BLOCK]
+                query_ref[b] = query_ref[b] + out
+            return carry
+
+        lax.fori_loop(0, (amount + unroll - 1) // unroll, step, 0)
+
+    run(whole_ref, wholes, GRADS_ITEM, WHOLE_UNROLL)
+    run(half_ref, halves, GRADS_ITEM // 2, HALF_UNROLL)
     y, core = me_ref[0], me_ref[2]
 
     def spread(n, carry):
@@ -301,8 +327,12 @@
     ]
 
 
-def scratch_work():
-    return [pltpu.SMEM((Q_BLOCKS * SLOTS // STATS_ITEM,), jnp.int32), pltpu.SemaphoreType.DMA((3 * LINE,))]
+def item_list(size):
+    return pltpu.SMEM((Q_BLOCKS * SLOTS // size,), jnp.int32)
+
+
+def piece_sems():
+    return pltpu.SemaphoreType.DMA((3 * LINE,))
 
 
 MIXED = [struct((OWN, BLOCK, WIDE), F32)] + [struct((OWN, BLOCK, WIDE), BF16)] * (LINE - 1)
@@ -313,7 +343,7 @@
         stats_kernel,
         struct((3, Q_BLOCKS, BLOCK), F32),
         [SMEM] * 3 + [VMEM] * (3 * LINE),
-        scratch_lines() + scratch_work(),
+        scratch_lines() + [item_list(STATS_ITEM), piece_sems()],
         "stats",
     )(me, pos, cnt, *near(*kvs, *qds))
 
@@ -326,7 +356,7 @@
         scratch_lines()
         + [pltpu.VMEM((K_BLOCKS, BLOCK, WIDE), F32), pltpu.VMEM((Q_BLOCKS, BLOCK, WIDE), F32)]
         + [pltpu.VMEM((Q_BLOCKS, BLOCK), F32)] * 2
-        + scratch_work(),
+        + [item_list(GRADS_ITEM), pltpu.SMEM((Q_BLOCKS,), jnp.int32), piece_sems()],
         "grads",
     )(me, pos, cnt, *near(*stats, *kvs, *qds))
 
@@ -351,7 +381,9 @@
     kv = got[:, :BLOCK].reshape(rows, WIDE)
     qd = got[:, BLOCK:].reshape(rows, WIDE)
     kvs = [kv] + [ctx_shift(kv, dx=hop) for hop in HOPS[1:]]
-    kvs = kvs + [ctx_shift(piece, dc=1) for piece in kvs]
+    other = ctx_shift(kv, dc=1)
+    qd, other = lax.optimization_barrier((qd, other))
+    kvs = kvs + [other] + [ctx_shift(piece, dc=1) for piece in kvs[1:]]
     qds = [qd] + [ctx_shift(qd, dy=hop) for hop in HOPS[1:]]
 
     stats = stats_call(me, pos, cnt, kvs, qds)

time: 129 us -> 128 us (level); the launches traced: 128 us -> 129 us
  starting transfers between devices: 34.9 us -> 28.9 us
  waiting for transfers between devices: 43.6 us -> 48.5 us
  Pallas kernels: 27.3 us -> 29.3 us
    ppermute x20, starting transfers between devices: 26.5 us -> 20.4 us  [ctx_shift(): return lax.ppermute(x, 'ctx', pairs)]
    ppermute x20, waiting for transfers between devices: 27.8 us -> 32.6 us  [ctx_shift(): return lax.ppermute(x, 'ctx', pairs)]
    pallas_call x1, Pallas kernels: 13.7 us -> 15.1 us  [grads_call(): call(grads_kernel, MIXED + [struct((LINE * OWN, BLOCK, WIDE), F32), struc...]
  transfers between devices with their start and end apart: 21 -> 21, of which waited for: 10 -> 9; matrix products, arithmetic and copies ran while one was open for 1% -> 1% of each run, Pallas kernels for 1% -> 1%
where the time goes in v4:
time: 128 us; the launch traced here: 129 us
  waiting for transfers between devices  48.5 us (38%)
  Pallas kernels  29.3 us (23%)
  starting transfers between devices  28.9 us (23%)
  blocking collectives  19.4 us (15%)
    ppermute x20, waiting for transfers between devices, ctx_shift(): return lax.ppermute(x, 'ctx', pairs)  32.6 us
    ppermute x20, starting transfers between devices, ctx_shift(): return lax.ppermute(x, 'ctx', pairs)  20.4 us
    all_to_all x1, blocking collectives, exchange(): return lax.all_to_all(x, 'head', split_axis=0, concat_axis=0, tiled=True)  19.4 us
    all_to_all x1, waiting for transfers between devices, exchange(): return lax.all_to_all(x, 'head', split_axis=0, concat_axis=0, tiled=True)  15.9 us
    pallas_call x1, Pallas kernels, grads_call(): call(grads_kernel, MIXED + [struct((LINE * OWN, BLOCK, WIDE), F32), struc...  15.1 us
    all_to_all x1, starting transfers between devices, exchange(): return lax.all_to_all(x, 'head', split_axis=0, concat_axis=0, tiled=True)  8.48 us
    pallas_call x1, Pallas kernels, stats_call(): call(stats_kernel, struct((3, Q_BLOCKS, BLOCK), F32), [SMEM] * 3 + [VMEM]...  7.4 us
    pallas_call x1, Pallas kernels, body(): call(project_kernel, struct(wide, BF16), [ANY] * 6, [pltpu.VMEM(g.shape,...  3.78 us
  transfers between devices with their start and end apart: 21, of which 9 were waited for; matrix products, arithmetic and copies ran while one was open for 1% of the time, Pallas kernels for 1%

profile of v4, /device:TPU:6, one launch (start us, length us, event | category | flops | bytes accessed | tf_op | source)
XLA Modules:
  0.0 128.5 jit_solution(6323305936659323554)
XLA Ops:
  0.7 3.8 %project.1 = bf16[8,256,128]{2,1,0:T(8,128)(2,1)} custom-call(bf16[128,1024]{1,0:T(8,128)(2,1)} %refs_0_.1, bf16[1024,512]{1,0:T(8,128)(2,1)} %wk_ref.1, bf16[1024,512]{1,0:T(8,128)(2,1)} %wv_ref.1, bf16[1024,512]{1,0:T(8,128)(2,1)} %wq_ref.1, bf16[128,1024]{1,0:T(8,128)(2,1)} %refs_4_.1, bf16[512,1024]{1,0:T(8,128)(2,1)} %wo_ref.1), custom_call_target="tpu_custom_call" | custom-call | tf_op jit(solution)/shard_map/project/pallas_call | solution.py:373
  4.4 8.5 %all-to-all-start = ((bf16[8,256,128]{2,1,0:T(8,128)(2,1)}), bf16[8,256,128]{2,1,0:T(8,128)(2,1)S(1)}, u32[]{:S(2)}, u32[]{:S(2)}) async-start(bf16[8,256,128]{2,1,0:T(8,128)(2,1)} %project.1), calls=%async_computation | async-start | bytes 1048576 | tf_op jit(solution)/shard_map/all_to_all | solution.py:320
  13.2 0.3 broadcast_compare_fusion
  13.7 0.1 fusion.4
  13.9 0.7 select_reduce_fusion.pos_ref
  14.6 15.9 %all-to-all-done = bf16[8,256,128]{2,1,0:T(8,128)(2,1)S(1)} async-done(((bf16[8,256,128]{2,1,0:T(8,128)(2,1)}), bf16[8,256,128]{2,1,0:T(8,128)(2,1)S(1)}, u32[]{:S(2)}, u32[]{:S(2)}) %all-to-all-start) | async-done | bytes 524320 | tf_op jit(solution)/shard_map/all_to_all | solution.py:320
  30.6 1.5 %collective-permute-start.2 = (bf16[1024,128]{1,0:T(8,128)(2,1)S(1)}, bf16[1024,128]{1,0:T(8,128)(2,1)S(1)}, u32[]{:S(2)}, u32[]{:S(2)}) collective-permute-start(bf16[1024,128]{1,0:T(8,128)(2,1)S(1)} %bitcast.11), channel_id=1, source_target_pairs={{0,32},{8,40},{16,48},{24,56},{32,0},{40,8},{48,16},{56,24},{64,96... | collective-permute-start | bytes 786440 | tf_op jit(solution)/shard_map/ppermute | solution.py:298
  32.1 3.2 %collective-permute-start = (bf16[1024,128]{1,0:T(8,128)(2,1)S(1)}, bf16[1024,128]{1,0:T(8,128)(2,1)S(1)}, u32[]{:S(2)}, u32[]{:S(2)}) collective-permute-start(bf16[1024,128]{1,0:T(8,128)(2,1)S(1)} %bitcast.13), channel_id=1, source_target_pairs={{0,16},{8,24},{16,32},{24,40},{32,48},{40,56},{48,0},{56,8},{64,80... | collective-permute-start | bytes 786440 | tf_op jit(solution)/shard_map/ppermute | solution.py:298
  35.3 3.2 %collective-permute-start.9 = (bf16[1024,128]{1,0:T(8,128)(2,1)S(1)}, bf16[1024,128]{1,0:T(8,128)(2,1)S(1)}, u32[]{:S(2)}, u32[]{:S(2)}) collective-permute-start(bf16[1024,128]{1,0:T(8,128)(2,1)S(1)} %bitcast.5), channel_id=1, source_target_pairs={{0,128},{8,136},{16,144},{24,152},{32,160},{40,168},{48,176},{56,1... | collective-permute-start | bytes 786440 | tf_op jit(solution)/shard_map/ppermute | solution.py:298
  38.5 1.1 collective-permute-start.8
  39.5 1.8 %collective-permute-done.2.rest_3_.rest_7_ = bf16[1024,128]{1,0:T(8,128)(2,1)S(1)} collective-permute-done((bf16[1024,128]{1,0:T(8,128)(2,1)S(1)}, bf16[1024,128]{1,0:T(8,128)(2,1)S(1)}, u32[]{:S(2)}, u32[]{:S(2)}) %collective-permute-start.2) | collective-permute-done | bytes 262176 | tf_op jit(solution)/shard_map/ppermute | solution.py:298
  41.3 1.6 %collective-permute-start.7 = (bf16[1024,128]{1,0:T(8,128)(2,1)S(1)}, bf16[1024,128]{1,0:T(8,128)(2,1)S(1)}, u32[]{:S(2)}, u32[]{:S(2)}) collective-permute-start(bf16[1024,128]{1,0:T(8,128)(2,1)S(1)} %bitcast.7), channel_id=1, source_target_pairs={{0,64},{8,72},{16,80},{24,88},{32,96},{40,104},{48,112},{56,120},{... | collective-permute-start | bytes 786440 | tf_op jit(solution)/shard_map/ppermute | solution.py:298
  42.9 3.5 %collective-permute-done.1.rest_2_.rest_6_ = bf16[1024,128]{1,0:T(8,128)(2,1)S(1)} collective-permute-done((bf16[1024,128]{1,0:T(8,128)(2,1)S(1)}, bf16[1024,128]{1,0:T(8,128)(2,1)S(1)}, u32[]{:S(2)}, u32[]{:S(2)}) %collective-permute-start.1) | collective-permute-done | bytes 262176 | tf_op jit(solution)/shard_map/ppermute | solution.py:298
  46.4 0.5 collective-permute-start.5
  47.0 3.6 %collective-permute-done.8.rest_10_.rest_14_ = bf16[1024,128]{1,0:T(8,128)(2,1)S(1)} collective-permute-done((bf16[1024,128]{1,0:T(8,128)(2,1)S(1)}, bf16[1024,128]{1,0:T(8,128)(2,1)S(1)}, u32[]{:S(2)}, u32[]{:S(2)}) %collective-permute-start.8) | collective-permute-done | bytes 262176 | tf_op jit(solution)/shard_map/ppermute | solution.py:298
  50.6 7.4 %stats.1.rest_0_ = f32[3,32,128]{2,1,0:T(8,128)S(1)} custom-call(s32[3]{0:T(128)S(1)} %pad_add_fusion.me_ref, s32[32,24]{1,0:T(8,128)S(1)} %select_reduce_fusion.pos_ref, s32[32]{0:T(128)S(1)} %convert_element_type.26.cnt_ref, bf16[1024,128]{1,0:T(8,128)(2,1)S(1)} %bitcast.14, bf16[1024,128]{1,0:T(8,128)(2,1)S(1)} %collective-permute-done.rest_1_.rest_5_, ...), custom_call_target="tpu_custom_call" | custom-call | tf_op jit(solution)/shard_map/stats/pallas_call | solution.py:342
  58.0 1.6 %collective-permute-start.12 = (f32[3,32,128]{2,1,0:T(8,128)S(1)}, f32[3,32,128]{2,1,0:T(8,128)S(1)}, u32[]{:S(2)}, u32[]{:S(2)}) collective-permute-start(f32[3,32,128]{2,1,0:T(8,128)S(1)} %stats.1.rest_0_), channel_id=1, source_target_pairs={{0,128},{8,136},{16,144},{24,152},{32,160},{40,168},{48,176},{56,1... | collective-permute-start | bytes 147464 | tf_op jit(solution)/shard_map/ppermute | solution.py:298
  59.7 1.8 %collective-permute-start.11 = (f32[3,32,128]{2,1,0:T(8,128)S(1)}, f32[3,32,128]{2,1,0:T(8,128)S(1)}, u32[]{:S(2)}, u32[]{:S(2)}) collective-permute-start(f32[3,32,128]{2,1,0:T(8,128)S(1)} %stats.1.rest_0_), channel_id=1, source_target_pairs={{0,192},{8,200},{16,208},{24,216},{32,224},{40,232},{48,240},{56,2... | collective-permute-start | bytes 147464 | tf_op jit(solution)/shard_map/ppermute | solution.py:298
  61.4 0.2 collective-permute-start.10
  61.7 2.0 %collective-permute-done.12.rest_3_ = f32[3,32,128]{2,1,0:T(8,128)S(1)} collective-permute-done((f32[3,32,128]{2,1,0:T(8,128)S(1)}, f32[3,32,128]{2,1,0:T(8,128)S(1)}, u32[]{:S(2)}, u32[]{:S(2)}) %collective-permute-start.12) | collective-permute-done | bytes 49184 | tf_op jit(solution)/shard_map/ppermute | solution.py:298
  63.7 0.3 collective-permute-done.11.rest_2_
  64.0 2.8 %collective-permute-done.10.rest_1_ = f32[3,32,128]{2,1,0:T(8,128)S(1)} collective-permute-done((f32[3,32,128]{2,1,0:T(8,128)S(1)}, f32[3,32,128]{2,1,0:T(8,128)S(1)}, u32[]{:S(2)}, u32[]{:S(2)}) %collective-permute-start.10) | collective-permute-done | bytes 49184 | tf_op jit(solution)/shard_map/ppermute | solution.py:298
  66.7 15.1 %grads.1 = (f32[8,128,128]{2,1,0:T(8,128)S(1)}, bf16[8,128,128]{2,1,0:T(8,128)(2,1)S(1)}, bf16[8,128,128]{2,1,0:T(8,128)(2,1)S(1)}, bf16[8,128,128]{2,1,0:T(8,12...) custom-call(s32[3]{0:T(128)S(1)} %pad_add_fusion.me_ref, ...), custom_call_target="tpu_custom_call" | custom-call | tf_op jit(solution)/shard_map/grads/pallas_call | solution.py:352
  82.0 3.2 %collective-permute-start.18 = (bf16[8,128,128]{2,1,0:T(8,128)(2,1)S(1)}, bf16[8,128,128]{2,1,0:T(8,128)(2,1)S(1)}, u32[]{:S(2)}, u32[]{:S(2)}) collective-permute-start(bf16[8,128,128]{2,1,0:T(8,128)(2,1)S(1)} %get-tuple-element.32), channel_id=1, source_target_pairs={{0,192},{8,200},{16,208},{24,216},{32,224},{40,232},{48,240},{56,2... | collective-permute-start | bytes 786440 | tf_op jit(solution)/shard_map/ppermute | solution.py:298
  85.2 0.8 core_sum.1
  86.0 0.3 collective-permute-start.14
  86.3 1.8 %collective-permute-start.15 = (bf16[8,128,128]{2,1,0:T(8,128)(2,1)S(1)}, bf16[8,128,128]{2,1,0:T(8,128)(2,1)S(1)}, u32[]{:S(2)}, u32[]{:S(2)}) collective-permute-start(bf16[8,128,128]{2,1,0:T(8,128)(2,1)S(1)} %get-tuple-element.28), channel_id=1, source_target_pairs={{0,48},{8,56},{16,0},{24,8},{32,16},{40,24},{48,32},{56,40},{64,11... | collective-permute-start | bytes 786440 | tf_op jit(solution)/shard_map/ppermute | solution.py:298
  88.1 9.4 %collective-permute-done.17.refs_5_ = bf16[8,128,128]{2,1,0:T(8,128)(2,1)S(1)} collective-permute-done((bf16[8,128,128]{2,1,0:T(8,128)(2,1)S(1)}, bf16[8,128,128]{2,1,0:T(8,128)(2,1)S(1)}, u32[]{:S(2)}, u32[]{:S(2)}) %collective-permute-start.17) | collective-permute-done | bytes 262176 | tf_op jit(solution)/shard_map/ppermute | solution.py:298
  97.5 9.3 %collective-permute-done.16.refs_3_ = bf16[8,128,128]{2,1,0:T(8,128)(2,1)S(1)} collective-permute-done((bf16[8,128,128]{2,1,0:T(8,128)(2,1)S(1)}, bf16[8,128,128]{2,1,0:T(8,128)(2,1)S(1)}, u32[]{:S(2)}, u32[]{:S(2)}) %collective-permute-start.16) | collective-permute-done | bytes 262176 | tf_op jit(solution)/shard_map/ppermute | solution.py:298
  106.8 0.2 line_sum.1
  107.1 19.4 %all_to_all.10.in_ref = bf16[8,256,128]{2,1,0:T(8,128)(2,1)S(1)} all-to-all(bf16[8,256,128]{2,1,0:T(8,128)(2,1)S(1)} %line_sum.1), channel_id=1, replica_groups=mesh['ctx'=32,'head'=8] {'head'}, dimensions={0} | all-to-all | bytes 1048576 | tf_op jit(solution)/shard_map/all_to_all | solution.py:320
  126.5 2.0 %output.1 = (bf16[128,1024]{1,0:T(8,128)(2,1)}, bf16[128,1024]{1,0:T(8,128)(2,1)}) custom-call(bf16[8,256,128]{2,1,0:T(8,128)(2,1)S(1)} %all_to_all.10.in_ref, bf16[1024,512]{1,0:T(8,128)(2,1)S(1)} %copy-done.2, bf16[1024,512]{1,0:T(8,128)(2,1)S(1)} %copy-done, bf16[1024,512]{1,0:T(8,128)(2,1)S(1)} %copy-done.1, bf16[512,1024]{1,0:T(8,128)(2,1)S(1)} %copy-done.3), custom_call_target="tpu_custom_call" | custom-call | tf_op jit(solution)/shard_map/output/pallas_call | solution.py:400
  (41 shorter events, 1.0 us)
Async XLA Ops:
  0.6 12.3 %copy-start.5 = (s32[256]{0:T(256)S(1)}, s32[256]{0:T(256)}, u32[]{:S(2)}) copy-start(s32[256]{0:T(256)} %param.14) | copy-start | bytes 3076
  0.6 12.6 %copy-start.4 = (s32[256,256]{1,0:T(8,128)S(1)}, s32[256,256]{1,0:T(8,128)}, u32[]{:S(2)}) copy-start(s32[256,256]{1,0:T(8,128)} %param.15) | copy-start | bytes 786436
  4.4 26.0 %all-to-all-start = ((bf16[8,256,128]{2,1,0:T(8,128)(2,1)}), bf16[8,256,128]{2,1,0:T(8,128)(2,1)S(1)}, u32[]{:S(2)}, u32[]{:S(2)}) async-start(bf16[8,256,128]{2,1,0:T(8,128)(2,1)} %project.1), calls=%async_computation | async-start | bytes 1048576 | tf_op jit(solution)/shard_map/all_to_all | solution.py:320
  30.5 4.8 %collective-permute-start.3 = (bf16[1024,128]{1,0:T(8,128)(2,1)S(1)}, bf16[1024,128]{1,0:T(8,128)(2,1)S(1)}, u32[]{:S(2)}, u32[]{:S(2)}) collective-permute-start(bf16[1024,128]{1,0:T(8,128)(2,1)S(1)} %bitcast.10), channel_id=1, source_target_pairs={{0,8},{8,0},{16,24},{24,16},{32,40},{40,32},{48,56},{56,48},{64,72... | collective-permute-start | bytes 786440 | tf_op jit(solution)/shard_map/ppermute | solution.py:298
  30.6 10.7 %collective-permute-start.2 = (bf16[1024,128]{1,0:T(8,128)(2,1)S(1)}, bf16[1024,128]{1,0:T(8,128)(2,1)S(1)}, u32[]{:S(2)}, u32[]{:S(2)}) collective-permute-start(bf16[1024,128]{1,0:T(8,128)(2,1)S(1)} %bitcast.11), channel_id=1, source_target_pairs={{0,32},{8,40},{16,48},{24,56},{32,0},{40,8},{48,16},{56,24},{64,96... | collective-permute-start | bytes 786440 | tf_op jit(solution)/shard_map/ppermute | solution.py:298
  32.1 14.4 %collective-permute-start.1 = (bf16[1024,128]{1,0:T(8,128)(2,1)S(1)}, bf16[1024,128]{1,0:T(8,128)(2,1)S(1)}, u32[]{:S(2)}, u32[]{:S(2)}) collective-permute-start(bf16[1024,128]{1,0:T(8,128)(2,1)S(1)} %bitcast.12), channel_id=1, source_target_pairs={{0,48},{8,56},{16,0},{24,8},{32,16},{40,24},{48,32},{56,40},{64,11... | collective-permute-start | bytes 786440 | tf_op jit(solution)/shard_map/ppermute | solution.py:298
  32.1 14.4 %collective-permute-start = (bf16[1024,128]{1,0:T(8,128)(2,1)S(1)}, bf16[1024,128]{1,0:T(8,128)(2,1)S(1)}, u32[]{:S(2)}, u32[]{:S(2)}) collective-permute-start(bf16[1024,128]{1,0:T(8,128)(2,1)S(1)} %bitcast.13), channel_id=1, source_target_pairs={{0,16},{8,24},{16,32},{24,40},{32,48},{40,56},{48,0},{56,8},{64,80... | collective-permute-start | bytes 786440 | tf_op jit(solution)/shard_map/ppermute | solution.py:298
  35.3 11.6 %collective-permute-start.9 = (bf16[1024,128]{1,0:T(8,128)(2,1)S(1)}, bf16[1024,128]{1,0:T(8,128)(2,1)S(1)}, u32[]{:S(2)}, u32[]{:S(2)}) collective-permute-start(bf16[1024,128]{1,0:T(8,128)(2,1)S(1)} %bitcast.5), channel_id=1, source_target_pairs={{0,128},{8,136},{16,144},{24,152},{32,160},{40,168},{48,176},{56,1... | collective-permute-start | bytes 786440 | tf_op jit(solution)/shard_map/ppermute | solution.py:298
  38.5 12.1 %collective-permute-start.8 = (bf16[1024,128]{1,0:T(8,128)(2,1)S(1)}, bf16[1024,128]{1,0:T(8,128)(2,1)S(1)}, u32[]{:S(2)}, u32[]{:S(2)}) collective-permute-start(bf16[1024,128]{1,0:T(8,128)(2,1)S(1)} %bitcast.6), channel_id=1, source_target_pairs={{0,192},{8,200},{16,208},{24,216},{32,224},{40,232},{48,240},{56,2... | collective-permute-start | bytes 786440 | tf_op jit(solution)/shard_map/ppermute | solution.py:298
  41.3 9.3 %collective-permute-start.7 = (bf16[1024,128]{1,0:T(8,128)(2,1)S(1)}, bf16[1024,128]{1,0:T(8,128)(2,1)S(1)}, u32[]{:S(2)}, u32[]{:S(2)}) collective-permute-start(bf16[1024,128]{1,0:T(8,128)(2,1)S(1)} %bitcast.7), channel_id=1, source_target_pairs={{0,64},{8,72},{16,80},{24,88},{32,96},{40,104},{48,112},{56,120},{... | collective-permute-start | bytes 786440 | tf_op jit(solution)/shard_map/ppermute | solution.py:298
  46.4 4.2 %collective-permute-start.6 = (bf16[1024,128]{1,0:T(8,128)(2,1)S(1)}, bf16[1024,128]{1,0:T(8,128)(2,1)S(1)}, u32[]{:S(2)}, u32[]{:S(2)}) collective-permute-start(bf16[1024,128]{1,0:T(8,128)(2,1)S(1)} %collective-permute-done.2.rest_3_.rest_7_), channel_id=1, source_target_pairs={{0,8},{8,0},{16,24},{24,16},{32,40},{40,32},{48,56},{56,48},{64,72... | collective-permute-start | bytes 786440 | tf_op jit(solution)/shard_map/ppermute | solution.py:298
  46.4 4.2 %collective-permute-start.5 = (bf16[1024,128]{1,0:T(8,128)(2,1)S(1)}, bf16[1024,128]{1,0:T(8,128)(2,1)S(1)}, u32[]{:S(2)}, u32[]{:S(2)}) collective-permute-start(bf16[1024,128]{1,0:T(8,128)(2,1)S(1)} %collective-permute-done.1.rest_2_.rest_6_), channel_id=1, source_target_pairs={{0,8},{8,0},{16,24},{24,16},{32,40},{40,32},{48,56},{56,48},{64,72... | collective-permute-start | bytes 786440 | tf_op jit(solution)/shard_map/ppermute | solution.py:298
  46.9 3.7 %collective-permute-start.4 = (bf16[1024,128]{1,0:T(8,128)(2,1)S(1)}, bf16[1024,128]{1,0:T(8,128)(2,1)S(1)}, u32[]{:S(2)}, u32[]{:S(2)}) collective-permute-start(bf16[1024,128]{1,0:T(8,128)(2,1)S(1)} %collective-permute-done.rest_1_.rest_5_), channel_id=1, source_target_pairs={{0,8},{8,0},{16,24},{24,16},{32,40},{40,32},{48,56},{56,48},{64,72... | collective-permute-start | bytes 786440 | tf_op jit(solution)/shard_map/ppermute | solution.py:298
  58.0 5.7 %collective-permute-start.12 = (f32[3,32,128]{2,1,0:T(8,128)S(1)}, f32[3,32,128]{2,1,0:T(8,128)S(1)}, u32[]{:S(2)}, u32[]{:S(2)}) collective-permute-start(f32[3,32,128]{2,1,0:T(8,128)S(1)} %stats.1.rest_0_), channel_id=1, source_target_pairs={{0,128},{8,136},{16,144},{24,152},{32,160},{40,168},{48,176},{56,1... | collective-permute-start | bytes 147464 | tf_op jit(solution)/shard_map/ppermute | solution.py:298
  59.7 4.3 %collective-permute-start.11 = (f32[3,32,128]{2,1,0:T(8,128)S(1)}, f32[3,32,128]{2,1,0:T(8,128)S(1)}, u32[]{:S(2)}, u32[]{:S(2)}) collective-permute-start(f32[3,32,128]{2,1,0:T(8,128)S(1)} %stats.1.rest_0_), channel_id=1, source_target_pairs={{0,192},{8,200},{16,208},{24,216},{32,224},{40,232},{48,240},{56,2... | collective-permute-start | bytes 147464 | tf_op jit(solution)/shard_map/ppermute | solution.py:298
  61.4 5.3 %collective-permute-start.10 = (f32[3,32,128]{2,1,0:T(8,128)S(1)}, f32[3,32,128]{2,1,0:T(8,128)S(1)}, u32[]{:S(2)}, u32[]{:S(2)}) collective-permute-start(f32[3,32,128]{2,1,0:T(8,128)S(1)} %stats.1.rest_0_), channel_id=1, source_target_pairs={{0,64},{8,72},{16,80},{24,88},{32,96},{40,104},{48,112},{56,120},{... | collective-permute-start | bytes 147464 | tf_op jit(solution)/shard_map/ppermute | solution.py:298
  81.8 3.4 %collective-permute-start.13 = (bf16[32,128,128]{2,1,0:T(8,128)(2,1)S(1)}, bf16[32,128,128]{2,1,0:T(8,128)(2,1)S(1)}, u32[]{:S(2)}, u32[]{:S(2)}) collective-permute-start(bf16[32,128,128]{2,1,0:T(8,128)(2,1)S(1)} %get-tuple-element.25), channel_id=1, source_target_pairs={{0,8},{8,0},{16,24},{24,16},{32,40},{40,32},{48,56},{56,48},{64,72... | collective-permute-start | bytes 3145736 | tf_op jit(solution)/shard_map/ppermute | solution.py:298
  81.9 15.6 %collective-permute-start.17 = (bf16[8,128,128]{2,1,0:T(8,128)(2,1)S(1)}, bf16[8,128,128]{2,1,0:T(8,128)(2,1)S(1)}, u32[]{:S(2)}, u32[]{:S(2)}) collective-permute-start(bf16[8,128,128]{2,1,0:T(8,128)(2,1)S(1)} %get-tuple-element.31), channel_id=1, source_target_pairs={{0,64},{8,72},{16,80},{24,88},{32,96},{40,104},{48,112},{56,120},{... | collective-permute-start | bytes 786440 | tf_op jit(solution)/shard_map/ppermute | solution.py:298
  82.0 15.5 %collective-permute-start.18 = (bf16[8,128,128]{2,1,0:T(8,128)(2,1)S(1)}, bf16[8,128,128]{2,1,0:T(8,128)(2,1)S(1)}, u32[]{:S(2)}, u32[]{:S(2)}) collective-permute-start(bf16[8,128,128]{2,1,0:T(8,128)(2,1)S(1)} %get-tuple-element.32), channel_id=1, source_target_pairs={{0,192},{8,200},{16,208},{24,216},{32,224},{40,232},{48,240},{56,2... | collective-permute-start | bytes 786440 | tf_op jit(solution)/shard_map/ppermute | solution.py:298
  85.2 12.2 %collective-permute-start.19 = (bf16[8,128,128]{2,1,0:T(8,128)(2,1)S(1)}, bf16[8,128,128]{2,1,0:T(8,128)(2,1)S(1)}, u32[]{:S(2)}, u32[]{:S(2)}) collective-permute-start(bf16[8,128,128]{2,1,0:T(8,128)(2,1)S(1)} %get-tuple-element.33), channel_id=1, source_target_pairs={{0,128},{8,136},{16,144},{24,152},{32,160},{40,168},{48,176},{56,1... | collective-permute-start | bytes 786440 | tf_op jit(solution)/shard_map/ppermute | solution.py:298
  86.0 11.5 %collective-permute-start.14 = (bf16[8,128,128]{2,1,0:T(8,128)(2,1)S(1)}, bf16[8,128,128]{2,1,0:T(8,128)(2,1)S(1)}, u32[]{:S(2)}, u32[]{:S(2)}) collective-permute-start(bf16[8,128,128]{2,1,0:T(8,128)(2,1)S(1)} %get-tuple-element.27), channel_id=1, source_target_pairs={{0,16},{8,24},{16,32},{24,40},{32,48},{40,56},{48,0},{56,8},{64,80... | collective-permute-start | bytes 786440 | tf_op jit(solution)/shard_map/ppermute | solution.py:298
  86.3 11.2 %collective-permute-start.15 = (bf16[8,128,128]{2,1,0:T(8,128)(2,1)S(1)}, bf16[8,128,128]{2,1,0:T(8,128)(2,1)S(1)}, u32[]{:S(2)}, u32[]{:S(2)}) collective-permute-start(bf16[8,128,128]{2,1,0:T(8,128)(2,1)S(1)} %get-tuple-element.28), channel_id=1, source_target_pairs={{0,48},{8,56},{16,0},{24,8},{32,16},{40,24},{48,32},{56,40},{64,11... | collective-permute-start | bytes 786440 | tf_op jit(solution)/shard_map/ppermute | solution.py:298
  97.5 9.4 %collective-permute-start.16 = (bf16[8,128,128]{2,1,0:T(8,128)(2,1)S(1)}, bf16[8,128,128]{2,1,0:T(8,128)(2,1)S(1)}, u32[]{:S(2)}, u32[]{:S(2)}) collective-permute-start(bf16[8,128,128]{2,1,0:T(8,128)(2,1)S(1)} %get-tuple-element.29), channel_id=1, source_target_pairs={{0,32},{8,40},{16,48},{24,56},{32,0},{40,8},{48,16},{56,24},{64,96... | collective-permute-start | bytes 786440 | tf_op jit(solution)/shard_map/ppermute | solution.py:298
  106.8 19.6 %copy-start = (bf16[1024,512]{1,0:T(8,128)(2,1)S(1)}, bf16[1024,512]{1,0:T(8,128)(2,1)}, u32[]{:S(2)}) copy-start(bf16[1024,512]{1,0:T(8,128)(2,1)} %wk_ref.1) | copy-start | bytes 3145732
  106.8 19.6 %copy-start.1 = (bf16[1024,512]{1,0:T(8,128)(2,1)S(1)}, bf16[1024,512]{1,0:T(8,128)(2,1)}, u32[]{:S(2)}) copy-start(bf16[1024,512]{1,0:T(8,128)(2,1)} %wv_ref.1) | copy-start | bytes 3145732
  106.8 19.6 %copy-start.2 = (bf16[1024,512]{1,0:T(8,128)(2,1)S(1)}, bf16[1024,512]{1,0:T(8,128)(2,1)}, u32[]{:S(2)}) copy-start(bf16[1024,512]{1,0:T(8,128)(2,1)} %wq_ref.1) | copy-start | bytes 3145732
  106.8 19.6 %copy-start.3 = (bf16[512,1024]{1,0:T(8,128)(2,1)S(1)}, bf16[512,1024]{1,0:T(8,128)(2,1)}, u32[]{:S(2)}) copy-start(bf16[512,1024]{1,0:T(8,128)(2,1)} %wo_ref.1) | copy-start | bytes 3145732

commit v5 on v4

--- a/solution.py
+++ b/solution.py
@@ -13,6 +13,8 @@
 BLOCK = 128
 KB_MAX = 21
 SLOTS = 24
+STATS_MOST = 11
+GRADS_MOST = 6
 STATS_ITEM = 2
 GRADS_ITEM = 4
 STATS_UNROLL = 8
@@ -110,39 +112,8 @@
     return jnp.concatenate([jnp.where(low, qd, zero), jnp.where(low, zero, qd)], axis=0)
 
 
-def build_items(cnt_ref, item_ref, size):
-    def one(b, at):
-        def put(j, at):
-            item_ref[at] = b * 16 + j
-            return at + 1
-
-        return lax.fori_loop(0, (cnt_ref[b] + size - 1) // size, put, at)
-
-    return lax.fori_loop(0, Q_BLOCKS, one, 0)
-
-
-def build_halves(cnt_ref, whole_ref, half_ref):
-    half = GRADS_ITEM // 2
-
-    def one(b, at):
-        wholes, halves = at
-        left = cnt_ref[b] % GRADS_ITEM
-        short = jnp.where((left > 0) & (left <= half), 1, 0)
-        amount = (cnt_ref[b] + half - 1) // GRADS_ITEM
-
-        def put(j, at):
-            whole_ref[at] = b * 16 + j
-            return at + 1
-
-        wholes = lax.fori_loop(0, amount, put, wholes)
-        half_ref[halves] = b * 16 + 2 * amount
-        return wholes, halves + short
-
-    return lax.fori_loop(0, Q_BLOCKS, one, (0, 0))
-
-
-def read_item(item_ref, pos_ref, cnt_ref, at, amount, size):
-    code = item_ref[jnp.minimum(at, amount - 1)]
+def read_item(item_ref, base, pos_ref, cnt_ref, at, amount, size):
+    code = item_ref[base + jnp.minimum(at, amount - 1)]
     b, j = code // 16, code % 16
     limit = jnp.where(at < amount, cnt_ref[b], 0)
     places = [pos_ref[b, size * j + s] for s in range(size)]
@@ -161,13 +132,13 @@
     return kv, scores, prod[:, BLOCK:]
 
 
-def stats_kernel(me_ref, pos_ref, cnt_ref, *rest):
+def stats_kernel(me_ref, pos_ref, cnt_ref, item_ref, *rest):
     kv_pieces, qd_pieces = rest[: 2 * LINE], rest[2 * LINE : 3 * LINE]
-    out_ref, kv_all, qd_all, item_ref, sems = rest[3 * LINE :]
+    out_ref, kv_all, qd_all, sems = rest[3 * LINE :]
     copies = load_lines(me_ref, kv_pieces, qd_pieces, kv_all, qd_all, sems)
     out_ref[0] = jnp.full((Q_BLOCKS, BLOCK), FAR, F32)
     out_ref[1:] = jnp.zeros((2, Q_BLOCKS, BLOCK), F32)
-    amount = build_items(cnt_ref, item_ref, STATS_ITEM)
+    amount = item_ref[Q_BLOCKS * STATS_MOST]
     for copy in copies:
         copy.wait()
 
@@ -175,7 +146,7 @@
         done = []
         for u in range(STATS_UNROLL):
             at = n * STATS_UNROLL + u
-            b, places, far = read_item(item_ref, pos_ref, cnt_ref, at, amount, STATS_ITEM)
+            b, places, far = read_item(item_ref, 0, pos_ref, cnt_ref, at, amount, STATS_ITEM)
             _, scores, dprobs = item_products(kv_all, query_pair(qd_all, b), places, far)
             top = jnp.max(scores, axis=0, keepdims=True)
             raw = jnp.exp(scores - top)
@@ -194,12 +165,12 @@
     lax.fori_loop(0, (amount + STATS_UNROLL - 1) // STATS_UNROLL, step, 0)
 
 
-def grads_kernel(me_ref, pos_ref, cnt_ref, *rest):
+def grads_kernel(me_ref, pos_ref, cnt_ref, item_ref, *rest):
     stats, rest = rest[:LINE], rest[LINE:]
     kv_pieces, qd_pieces, rest = rest[: 2 * LINE], rest[2 * LINE : 3 * LINE], rest[3 * LINE :]
     y_refs, rest = rest[:LINE], rest[LINE:]
     own_ref, other_ref, kv_all, qd_all, key_ref, query_ref = rest[:6]
-    lse_ref, delta_ref, whole_ref, half_ref, sems = rest[6:]
+    lse_ref, delta_ref, sems = rest[6:]
     copies = load_lines(me_ref, kv_pieces, qd_pieces, kv_all, qd_all, sems)
 
     top = functools.reduce(jnp.maximum, [s[0] for s in stats])
@@ -210,16 +181,17 @@
     delta_ref[...] = dot / total
     key_ref[...] = jnp.zeros_like(key_ref)
     query_ref[...] = jnp.zeros_like(query_ref)
-    wholes, halves = build_halves(cnt_ref, whole_ref, half_ref)
+    whole_end = Q_BLOCKS * GRADS_MOST
+    half_end = whole_end + 1 + Q_BLOCKS
     for copy in copies:
         copy.wait()
 
-    def run(item_ref, amount, size, unroll):
+    def run(base, amount, size, unroll):
         def step(n, carry):
             done = []
             for u in range(unroll):
                 at = n * unroll + u
-                b, places, far = read_item(item_ref, pos_ref, cnt_ref, at, amount, size)
+                b, places, far = read_item(item_ref, base, pos_ref, cnt_ref, at, amount, size)
                 pair = query_pair(qd_all, b)
                 kv, scores, dprobs = item_products(kv_all, pair, places, far)
                 probs = jnp.exp(scores - lse_ref[pl.ds(b, 1), :])
@@ -237,8 +209,8 @@
 
         lax.fori_loop(0, (amount + unroll - 1) // unroll, step, 0)
 
-    run(whole_ref, wholes, GRADS_ITEM, WHOLE_UNROLL)
-    run(half_ref, halves, GRADS_ITEM // 2, HALF_UNROLL)
+    run(0, item_ref[whole_end], GRADS_ITEM, WHOLE_UNROLL)
+    run(whole_end + 1, item_ref[half_end], GRADS_ITEM // 2, HALF_UNROLL)
     y, core = me_ref[0], me_ref[2]
 
     def spread(n, carry):
@@ -316,6 +288,29 @@
     return pos, jnp.sum(live, axis=1).astype(jnp.int32)
 
 
+def item_table(amounts, first, most):
+    b = jnp.arange(Q_BLOCKS, dtype=jnp.int32)
+    j = jnp.arange(most, dtype=jnp.int32)
+    start = jnp.sum(jnp.where(b[None, :] < b[:, None], amounts[None, :], 0), axis=1)
+    at = jnp.where(j[None, :] < amounts[:, None], start[:, None] + j[None, :], -1)
+    code = (b * 16 + first)[:, None] + j[None, :]
+    slot = jnp.arange(Q_BLOCKS * most, dtype=jnp.int32)
+    hit = at[None] == slot[:, None, None]
+    return jnp.sum(jnp.where(hit, code[None], 0), axis=(1, 2)), jnp.sum(amounts)[None]
+
+
+def item_tables(cnt):
+    half = GRADS_ITEM // 2
+    none = jnp.zeros_like(cnt)
+    whole = (cnt + half - 1) // GRADS_ITEM
+    left = cnt % GRADS_ITEM
+    short = ((left > 0) & (left <= half)).astype(jnp.int32)
+    stats = item_table((cnt + STATS_ITEM - 1) // STATS_ITEM, none, STATS_MOST)
+    wholes = item_table(whole, none, GRADS_MOST)
+    halves = item_table(short, 2 * whole, 1)
+    return jnp.concatenate(stats), jnp.concatenate(wholes + halves)
+
+
 def exchange(x):
     return lax.all_to_all(x, "head", split_axis=0, concat_axis=0, tiled=True)
 
@@ -327,10 +322,6 @@
     ]
 
 
-def item_list(size):
-    return pltpu.SMEM((Q_BLOCKS * SLOTS // size,), jnp.int32)
-
-
 def piece_sems():
     return pltpu.SemaphoreType.DMA((3 * LINE,))
 
@@ -338,27 +329,27 @@
 MIXED = [struct((OWN, BLOCK, WIDE), F32)] + [struct((OWN, BLOCK, WIDE), BF16)] * (LINE - 1)
 
 
-def stats_call(me, pos, cnt, kvs, qds):
+def stats_call(lists, kvs, qds):
     return call(
         stats_kernel,
         struct((3, Q_BLOCKS, BLOCK), F32),
-        [SMEM] * 3 + [VMEM] * (3 * LINE),
-        scratch_lines() + [item_list(STATS_ITEM), piece_sems()],
+        [SMEM] * 4 + [VMEM] * (3 * LINE),
+        scratch_lines() + [piece_sems()],
         "stats",
-    )(me, pos, cnt, *near(*kvs, *qds))
-
-
-def grads_call(me, pos, cnt, stats, kvs, qds):
+    )(*lists, *near(*kvs, *qds))
+
+
+def grads_call(lists, stats, kvs, qds):
     return call(
         grads_kernel,
         MIXED + [struct((LINE * OWN, BLOCK, WIDE), F32), struct((LINE * OWN, BLOCK, WIDE), BF16)],
-        [SMEM] * 3 + [VMEM] * (4 * LINE),
+        [SMEM] * 4 + [VMEM] * (4 * LINE),
         scratch_lines()
         + [pltpu.VMEM((K_BLOCKS, BLOCK, WIDE), F32), pltpu.VMEM((Q_BLOCKS, BLOCK, WIDE), F32)]
         + [pltpu.VMEM((Q_BLOCKS, BLOCK), F32)] * 2
-        + [item_list(GRADS_ITEM), pltpu.SMEM((Q_BLOCKS,), jnp.int32), piece_sems()],
+        + [piece_sems()],
         "grads",
-    )(me, pos, cnt, *near(*stats, *kvs, *qds))
+    )(*lists, *near(*stats, *kvs, *qds))
 
 
 def body(hits_in, w_query, w_key, w_value, w_out, grad_y, block_cell, cell_mask):
@@ -377,7 +368,8 @@
         [pltpu.VMEM(g.shape, BF16) for g in given] + [pltpu.SemaphoreType.DMA((6,))],
         "project",
     )(*[pltpu.with_memory_space_constraint(g, pltpu.HBM) for g in given])
-    got, pos, cnt, me = lax.optimization_barrier((exchange(sent), pos, cnt, me))
+    tables = item_tables(cnt)
+    got, me, pos, cnt, tables = lax.optimization_barrier((exchange(sent), me, pos, cnt, tables))
     kv = got[:, :BLOCK].reshape(rows, WIDE)
     qd = got[:, BLOCK:].reshape(rows, WIDE)
     kvs = [kv] + [ctx_shift(kv, dx=hop) for hop in HOPS[1:]]
@@ -386,9 +378,9 @@
     kvs = kvs + [other] + [ctx_shift(piece, dc=1) for piece in kvs[1:]]
     qds = [qd] + [ctx_shift(qd, dy=hop) for hop in HOPS[1:]]
 
-    stats = stats_call(me, pos, cnt, kvs, qds)
+    stats = stats_call((me, pos, cnt, tables[0]), kvs, qds)
     all_stats = [stats] + [ctx_shift(stats, dy=hop) for hop in HOPS[1:]]
-    *y_parts, own, other = grads_call(me, pos, cnt, all_stats, kvs, qds)
+    *y_parts, own, other = grads_call((me, pos, cnt, tables[1]), all_stats, kvs, qds)
     y_parts = [y_parts[0]] + [ctx_shift(p, dy=hop) for p, hop in zip(y_parts[1:], HOPS[1:])]
     other = ctx_shift(other, dc=1)
     x_parts = call(core_sum_kernel, MIXED, [SMEM, VMEM, VMEM], name="core_sum")(me, *near(own, other))

time: 128 us -> 126 us (0.984); the launches traced: 129 us -> 125 us
  waiting for transfers between devices: 48.5 us -> 41.8 us
  Pallas kernels: 29.3 us -> 25.5 us
  other arithmetic: 0.9 us -> 4.24 us
  starting transfers between devices: 28.9 us -> 32.2 us
    all_to_all x1, waiting for transfers between devices: 15.9 us -> 12.5 us  [exchange(): return lax.all_to_all(x, 'head', split_axis=0, concat_axis=0, tiled=True)]
    ppermute x20, starting transfers between devices: 20.4 us -> 23.8 us  [ctx_shift(): return lax.ppermute(x, 'ctx', pairs)]
    ppermute x20, waiting for transfers between devices: 32.6 us -> 29.4 us  [ctx_shift(): return lax.ppermute(x, 'ctx', pairs)]
    pallas_call x1, Pallas kernels: 15.1 us -> 12.8 us  [grads_call(): call(grads_kernel, MIXED + [struct((LINE * OWN, BLOCK, WIDE), F32), struc...]
    concatenate x0 -> x2, other arithmetic: none -> 1.96 us  [item_tables(): return (jnp.concatenate(stats), jnp.concatenate(wholes + halves))]
    pallas_call x1, Pallas kernels: 7.4 us -> 5.92 us  [stats_call(): call(stats_kernel, struct((3, Q_BLOCKS, BLOCK), F32), [SMEM] * 4 + [VMEM]...]
    reduce_sum x0 -> x6, other arithmetic: none -> 1.36 us  [the longest x1 0.72 us: item_table(): jnp.sum(amounts)[None]]
  transfers between devices with their start and end apart: 21 -> 21, of which waited for: 9 -> 9; matrix products, arithmetic and copies ran while one was open for 1% -> 4% of each run, Pallas kernels for 1% -> 1%
where the time goes in v5:
time: 126 us; the launch traced here: 125 us
  waiting for transfers between devices  41.8 us (33%)
  starting transfers between devices  32.2 us (26%)
  Pallas kernels  25.5 us (20%)
  blocking collectives  19.4 us (15%)
  other arithmetic  4.24 us (3%)
    ppermute x20, waiting for transfers between devices, ctx_shift(): return lax.ppermute(x, 'ctx', pairs)  29.4 us
    ppermute x20, starting transfers between devices, ctx_shift(): return lax.ppermute(x, 'ctx', pairs)  23.8 us
    all_to_all x1, blocking collectives, exchange(): return lax.all_to_all(x, 'head', split_axis=0, concat_axis=0, tiled=True)  19.4 us
    pallas_call x1, Pallas kernels, grads_call(): call(grads_kernel, MIXED + [struct((LINE * OWN, BLOCK, WIDE), F32), struc...  12.8 us
    all_to_all x1, waiting for transfers between devices, exchange(): return lax.all_to_all(x, 'head', split_axis=0, concat_axis=0, tiled=True)  12.5 us
    all_to_all x1, starting transfers between devices, exchange(): return lax.all_to_all(x, 'head', split_axis=0, concat_axis=0, tiled=True)  8.48 us
    pallas_call x1, Pallas kernels, stats_call(): call(stats_kernel, struct((3, Q_BLOCKS, BLOCK), F32), [SMEM] * 4 + [VMEM]...  5.92 us
    pallas_call x1, Pallas kernels, body(): call(project_kernel, struct(wide, BF16), [ANY] * 6, [pltpu.VMEM(g.shape,...  3.77 us
  transfers between devices with their start and end apart: 21, of which 9 were waited for; matrix products, arithmetic and copies ran while one was open for 4% of the time, Pallas kernels for 1%

profile of v5, /device:TPU:6, one launch (start us, length us, event | category | flops | bytes accessed | tf_op | source)
XLA Modules:
  0.0 124.8 jit_solution(17371164888483464320)
XLA Ops:
  0.7 3.8 %project.1 = bf16[8,256,128]{2,1,0:T(8,128)(2,1)} custom-call(bf16[128,1024]{1,0:T(8,128)(2,1)} %refs_0_.1, bf16[1024,512]{1,0:T(8,128)(2,1)} %wk_ref.1, bf16[1024,512]{1,0:T(8,128)(2,1)} %wv_ref.1, bf16[1024,512]{1,0:T(8,128)(2,1)} %wq_ref.1, bf16[128,1024]{1,0:T(8,128)(2,1)} %refs_4_.1, bf16[512,1024]{1,0:T(8,128)(2,1)} %wo_ref.1), custom_call_target="tpu_custom_call" | custom-call | tf_op jit(solution)/shard_map/project/pallas_call | solution.py:364
  4.4 8.5 %all-to-all-start = ((bf16[8,256,128]{2,1,0:T(8,128)(2,1)}), bf16[8,256,128]{2,1,0:T(8,128)(2,1)S(1)}, u32[]{:S(2)}, u32[]{:S(2)}) async-start(bf16[8,256,128]{2,1,0:T(8,128)(2,1)} %project.1), calls=%async_computation | async-start | bytes 1048576 | tf_op jit(solution)/shard_map/all_to_all | solution.py:315
  13.2 0.3 broadcast_compare_fusion
  13.7 0.7 fusion.9
  14.9 1.3 %pad_add_fusion.1.item_ref = s32[226]{0:T(256)S(1)} fusion(s32[1]{0:T(128)} %bitcast.5, s32[32]{0:T(128)S(1)} %select_reduce_fusion.3, s32[1]{0:T(128)} %bitcast.4, s32[192]{0:T(256)S(1)} %select_reduce_fusion.2), kind=kLoop, calls=%fused_computation.37 | loop fusion | flops 678 | bytes 1808 | tf_op jit(solution)/shard_map/concatenate | solution.py:311
  16.5 0.6 pad_add_fusion.item_ref
  17.3 0.7 select_reduce_fusion.1.pos_ref
  17.9 12.5 %all-to-all-done = bf16[8,256,128]{2,1,0:T(8,128)(2,1)S(1)} async-done(((bf16[8,256,128]{2,1,0:T(8,128)(2,1)}), bf16[8,256,128]{2,1,0:T(8,128)(2,1)S(1)}, u32[]{:S(2)}, u32[]{:S(2)}) %all-to-all-start) | async-done | bytes 524320 | tf_op jit(solution)/shard_map/all_to_all | solution.py:315
  30.5 1.5 %collective-permute-start.2 = (bf16[1024,128]{1,0:T(8,128)(2,1)S(1)}, bf16[1024,128]{1,0:T(8,128)(2,1)S(1)}, u32[]{:S(2)}, u32[]{:S(2)}) collective-permute-start(bf16[1024,128]{1,0:T(8,128)(2,1)S(1)} %bitcast.14), channel_id=1, source_target_pairs={{0,32},{8,40},{16,48},{24,56},{32,0},{40,8},{48,16},{56,24},{64,96... | collective-permute-start | bytes 786440 | tf_op jit(solution)/shard_map/ppermute | solution.py:270
  32.0 3.2 %collective-permute-start = (bf16[1024,128]{1,0:T(8,128)(2,1)S(1)}, bf16[1024,128]{1,0:T(8,128)(2,1)S(1)}, u32[]{:S(2)}, u32[]{:S(2)}) collective-permute-start(bf16[1024,128]{1,0:T(8,128)(2,1)S(1)} %bitcast.16), channel_id=1, source_target_pairs={{0,16},{8,24},{16,32},{24,40},{32,48},{40,56},{48,0},{56,8},{64,80... | collective-permute-start | bytes 786440 | tf_op jit(solution)/shard_map/ppermute | solution.py:270
  35.3 3.2 %collective-permute-start.9 = (bf16[1024,128]{1,0:T(8,128)(2,1)S(1)}, bf16[1024,128]{1,0:T(8,128)(2,1)S(1)}, u32[]{:S(2)}, u32[]{:S(2)}) collective-permute-start(bf16[1024,128]{1,0:T(8,128)(2,1)S(1)} %bitcast.8), channel_id=1, source_target_pairs={{0,128},{8,136},{16,144},{24,152},{32,160},{40,168},{48,176},{56,1... | collective-permute-start | bytes 786440 | tf_op jit(solution)/shard_map/ppermute | solution.py:270
  38.5 1.1 collective-permute-start.8
  39.5 1.8 %collective-permute-done.2.rest_3_.rest_7_ = bf16[1024,128]{1,0:T(8,128)(2,1)S(1)} collective-permute-done((bf16[1024,128]{1,0:T(8,128)(2,1)S(1)}, bf16[1024,128]{1,0:T(8,128)(2,1)S(1)}, u32[]{:S(2)}, u32[]{:S(2)}) %collective-permute-start.2) | collective-permute-done | bytes 262176 | tf_op jit(solution)/shard_map/ppermute | solution.py:270
  41.3 1.6 %collective-permute-start.7 = (bf16[1024,128]{1,0:T(8,128)(2,1)S(1)}, bf16[1024,128]{1,0:T(8,128)(2,1)S(1)}, u32[]{:S(2)}, u32[]{:S(2)}) collective-permute-start(bf16[1024,128]{1,0:T(8,128)(2,1)S(1)} %bitcast.10), channel_id=1, source_target_pairs={{0,64},{8,72},{16,80},{24,88},{32,96},{40,104},{48,112},{56,120},{... | collective-permute-start | bytes 786440 | tf_op jit(solution)/shard_map/ppermute | solution.py:270
  42.9 3.5 %collective-permute-done.1.rest_2_.rest_6_ = bf16[1024,128]{1,0:T(8,128)(2,1)S(1)} collective-permute-done((bf16[1024,128]{1,0:T(8,128)(2,1)S(1)}, bf16[1024,128]{1,0:T(8,128)(2,1)S(1)}, u32[]{:S(2)}, u32[]{:S(2)}) %collective-permute-start.1) | collective-permute-done | bytes 262176 | tf_op jit(solution)/shard_map/ppermute | solution.py:270
  46.4 0.5 collective-permute-start.5
  47.0 3.6 %collective-permute-done.8.rest_10_.rest_14_ = bf16[1024,128]{1,0:T(8,128)(2,1)S(1)} collective-permute-done((bf16[1024,128]{1,0:T(8,128)(2,1)S(1)}, bf16[1024,128]{1,0:T(8,128)(2,1)S(1)}, u32[]{:S(2)}, u32[]{:S(2)}) %collective-permute-start.8) | collective-permute-done | bytes 262176 | tf_op jit(solution)/shard_map/ppermute | solution.py:270
  50.6 5.9 %stats.1.rest_0_ = f32[3,32,128]{2,1,0:T(8,128)S(1)} custom-call(s32[3]{0:T(128)S(1)} %pad_add_fusion.2.me_ref, s32[32,24]{1,0:T(8,128)S(1)} %select_reduce_fusion.1.pos_ref, s32[32]{0:T(128)S(1)} %convert_element_type.63.cnt_ref, s32[353]{0:T(512)S(1)} %pad_add_fusion.item_ref, bf16[1024,128]{1,0:T(8,128)(2,1)S(1)} %bitcast.17, ...), custom_call_target="tpu_custom_call" | custom-call | tf_op jit(solution)/shard_map/stats/pallas_call | solution.py:333
  56.5 3.5 %collective-permute-start.12 = (f32[3,32,128]{2,1,0:T(8,128)S(1)}, f32[3,32,128]{2,1,0:T(8,128)S(1)}, u32[]{:S(2)}, u32[]{:S(2)}) collective-permute-start(f32[3,32,128]{2,1,0:T(8,128)S(1)} %stats.1.rest_0_), channel_id=1, source_target_pairs={{0,128},{8,136},{16,144},{24,152},{32,160},{40,168},{48,176},{56,1... | collective-permute-start | bytes 147464 | tf_op jit(solution)/shard_map/ppermute | solution.py:270
  60.0 2.0 %collective-permute-start.10 = (f32[3,32,128]{2,1,0:T(8,128)S(1)}, f32[3,32,128]{2,1,0:T(8,128)S(1)}, u32[]{:S(2)}, u32[]{:S(2)}) collective-permute-start(f32[3,32,128]{2,1,0:T(8,128)S(1)} %stats.1.rest_0_), channel_id=1, source_target_pairs={{0,64},{8,72},{16,80},{24,88},{32,96},{40,104},{48,112},{56,120},{... | collective-permute-start | bytes 147464 | tf_op jit(solution)/shard_map/ppermute | solution.py:270
  62.2 1.9 %collective-permute-done.11.rest_2_ = f32[3,32,128]{2,1,0:T(8,128)S(1)} collective-permute-done((f32[3,32,128]{2,1,0:T(8,128)S(1)}, f32[3,32,128]{2,1,0:T(8,128)S(1)}, u32[]{:S(2)}, u32[]{:S(2)}) %collective-permute-start.11) | collective-permute-done | bytes 49184 | tf_op jit(solution)/shard_map/ppermute | solution.py:270
  64.1 1.2 collective-permute-done.10.rest_1_
  65.3 12.8 %grads.1 = (f32[8,128,128]{2,1,0:T(8,128)S(1)}, bf16[8,128,128]{2,1,0:T(8,128)(2,1)S(1)}, bf16[8,128,128]{2,1,0:T(8,128)(2,1)S(1)}, bf16[8,128,128]{2,1,0:T(8,12...) custom-call(s32[3]{0:T(128)S(1)} %pad_add_fusion.2.me_ref, ...), custom_call_target="tpu_custom_call" | custom-call | tf_op jit(solution)/shard_map/grads/pallas_call | solution.py:343
  78.3 3.2 %collective-permute-start.18 = (bf16[8,128,128]{2,1,0:T(8,128)(2,1)S(1)}, bf16[8,128,128]{2,1,0:T(8,128)(2,1)S(1)}, u32[]{:S(2)}, u32[]{:S(2)}) collective-permute-start(bf16[8,128,128]{2,1,0:T(8,128)(2,1)S(1)} %get-tuple-element.36), channel_id=1, source_target_pairs={{0,192},{8,200},{16,208},{24,216},{32,224},{40,232},{48,240},{56,2... | collective-permute-start | bytes 786440 | tf_op jit(solution)/shard_map/ppermute | solution.py:270
  81.5 0.8 core_sum.1
  82.3 1.9 %collective-permute-start.14 = (bf16[8,128,128]{2,1,0:T(8,128)(2,1)S(1)}, bf16[8,128,128]{2,1,0:T(8,128)(2,1)S(1)}, u32[]{:S(2)}, u32[]{:S(2)}) collective-permute-start(bf16[8,128,128]{2,1,0:T(8,128)(2,1)S(1)} %get-tuple-element.31), channel_id=1, source_target_pairs={{0,16},{8,24},{16,32},{24,40},{32,48},{40,56},{48,0},{56,8},{64,80... | collective-permute-start | bytes 786440 | tf_op jit(solution)/shard_map/ppermute | solution.py:270
  84.1 0.3 collective-permute-start.15
  84.4 9.3 %collective-permute-done.17.refs_5_ = bf16[8,128,128]{2,1,0:T(8,128)(2,1)S(1)} collective-permute-done((bf16[8,128,128]{2,1,0:T(8,128)(2,1)S(1)}, bf16[8,128,128]{2,1,0:T(8,128)(2,1)S(1)}, u32[]{:S(2)}, u32[]{:S(2)}) %collective-permute-start.17) | collective-permute-done | bytes 262176 | tf_op jit(solution)/shard_map/ppermute | solution.py:270
  93.7 1.5 %collective-permute-start.16 = (bf16[8,128,128]{2,1,0:T(8,128)(2,1)S(1)}, bf16[8,128,128]{2,1,0:T(8,128)(2,1)S(1)}, u32[]{:S(2)}, u32[]{:S(2)}) collective-permute-start(bf16[8,128,128]{2,1,0:T(8,128)(2,1)S(1)} %get-tuple-element.33), channel_id=1, source_target_pairs={{0,32},{8,40},{16,48},{24,56},{32,0},{40,8},{48,16},{56,24},{64,96... | collective-permute-start | bytes 786440 | tf_op jit(solution)/shard_map/ppermute | solution.py:270
  95.3 7.8 %collective-permute-done.16.refs_3_ = bf16[8,128,128]{2,1,0:T(8,128)(2,1)S(1)} collective-permute-done((bf16[8,128,128]{2,1,0:T(8,128)(2,1)S(1)}, bf16[8,128,128]{2,1,0:T(8,128)(2,1)S(1)}, u32[]{:S(2)}, u32[]{:S(2)}) %collective-permute-start.16) | collective-permute-done | bytes 262176 | tf_op jit(solution)/shard_map/ppermute | solution.py:270
  103.4 19.4 %all_to_all.10.in_ref = bf16[8,256,128]{2,1,0:T(8,128)(2,1)S(1)} all-to-all(bf16[8,256,128]{2,1,0:T(8,128)(2,1)S(1)} %line_sum.1), channel_id=1, replica_groups=mesh['ctx'=32,'head'=8] {'head'}, dimensions={0} | all-to-all | bytes 1048576 | tf_op jit(solution)/shard_map/all_to_all | solution.py:315
  122.7 2.0 %output.1 = (bf16[128,1024]{1,0:T(8,128)(2,1)}, bf16[128,1024]{1,0:T(8,128)(2,1)}) custom-call(bf16[8,256,128]{2,1,0:T(8,128)(2,1)S(1)} %all_to_all.10.in_ref, bf16[1024,512]{1,0:T(8,128)(2,1)S(1)} %copy-done.2, bf16[1024,512]{1,0:T(8,128)(2,1)S(1)} %copy-done, bf16[1024,512]{1,0:T(8,128)(2,1)S(1)} %copy-done.1, bf16[512,1024]{1,0:T(8,128)(2,1)S(1)} %copy-done.3), custom_call_target="tpu_custom_call" | custom-call | tf_op jit(solution)/shard_map/output/pallas_call | solution.py:392
  (55 shorter events, 2.2 us)
Async XLA Ops:
  0.6 12.3 %copy-start.5 = (s32[256]{0:T(256)S(1)}, s32[256]{0:T(256)}, u32[]{:S(2)}) copy-start(s32[256]{0:T(256)} %param.14) | copy-start | bytes 3076
  0.6 12.6 %copy-start.4 = (s32[256,256]{1,0:T(8,128)S(1)}, s32[256,256]{1,0:T(8,128)}, u32[]{:S(2)}) copy-start(s32[256,256]{1,0:T(8,128)} %param.15) | copy-start | bytes 786436
  4.4 26.0 %all-to-all-start = ((bf16[8,256,128]{2,1,0:T(8,128)(2,1)}), bf16[8,256,128]{2,1,0:T(8,128)(2,1)S(1)}, u32[]{:S(2)}, u32[]{:S(2)}) async-start(bf16[8,256,128]{2,1,0:T(8,128)(2,1)} %project.1), calls=%async_computation | async-start | bytes 1048576 | tf_op jit(solution)/shard_map/all_to_all | solution.py:315
  30.4 4.8 %collective-permute-start.3 = (bf16[1024,128]{1,0:T(8,128)(2,1)S(1)}, bf16[1024,128]{1,0:T(8,128)(2,1)S(1)}, u32[]{:S(2)}, u32[]{:S(2)}) collective-permute-start(bf16[1024,128]{1,0:T(8,128)(2,1)S(1)} %bitcast.13), channel_id=1, source_target_pairs={{0,8},{8,0},{16,24},{24,16},{32,40},{40,32},{48,56},{56,48},{64,72... | collective-permute-start | bytes 786440 | tf_op jit(solution)/shard_map/ppermute | solution.py:270
  30.5 10.7 %collective-permute-start.2 = (bf16[1024,128]{1,0:T(8,128)(2,1)S(1)}, bf16[1024,128]{1,0:T(8,128)(2,1)S(1)}, u32[]{:S(2)}, u32[]{:S(2)}) collective-permute-start(bf16[1024,128]{1,0:T(8,128)(2,1)S(1)} %bitcast.14), channel_id=1, source_target_pairs={{0,32},{8,40},{16,48},{24,56},{32,0},{40,8},{48,16},{56,24},{64,96... | collective-permute-start | bytes 786440 | tf_op jit(solution)/shard_map/ppermute | solution.py:270
  32.0 14.4 %collective-permute-start.1 = (bf16[1024,128]{1,0:T(8,128)(2,1)S(1)}, bf16[1024,128]{1,0:T(8,128)(2,1)S(1)}, u32[]{:S(2)}, u32[]{:S(2)}) collective-permute-start(bf16[1024,128]{1,0:T(8,128)(2,1)S(1)} %bitcast.15), channel_id=1, source_target_pairs={{0,48},{8,56},{16,0},{24,8},{32,16},{40,24},{48,32},{56,40},{64,11... | collective-permute-start | bytes 786440 | tf_op jit(solution)/shard_map/ppermute | solution.py:270
  32.0 14.4 %collective-permute-start = (bf16[1024,128]{1,0:T(8,128)(2,1)S(1)}, bf16[1024,128]{1,0:T(8,128)(2,1)S(1)}, u32[]{:S(2)}, u32[]{:S(2)}) collective-permute-start(bf16[1024,128]{1,0:T(8,128)(2,1)S(1)} %bitcast.16), channel_id=1, source_target_pairs={{0,16},{8,24},{16,32},{24,40},{32,48},{40,56},{48,0},{56,8},{64,80... | collective-permute-start | bytes 786440 | tf_op jit(solution)/shard_map/ppermute | solution.py:270
  35.3 11.6 %collective-permute-start.9 = (bf16[1024,128]{1,0:T(8,128)(2,1)S(1)}, bf16[1024,128]{1,0:T(8,128)(2,1)S(1)}, u32[]{:S(2)}, u32[]{:S(2)}) collective-permute-start(bf16[1024,128]{1,0:T(8,128)(2,1)S(1)} %bitcast.8), channel_id=1, source_target_pairs={{0,128},{8,136},{16,144},{24,152},{32,160},{40,168},{48,176},{56,1... | collective-permute-start | bytes 786440 | tf_op jit(solution)/shard_map/ppermute | solution.py:270
  38.5 12.1 %collective-permute-start.8 = (bf16[1024,128]{1,0:T(8,128)(2,1)S(1)}, bf16[1024,128]{1,0:T(8,128)(2,1)S(1)}, u32[]{:S(2)}, u32[]{:S(2)}) collective-permute-start(bf16[1024,128]{1,0:T(8,128)(2,1)S(1)} %bitcast.9), channel_id=1, source_target_pairs={{0,192},{8,200},{16,208},{24,216},{32,224},{40,232},{48,240},{56,2... | collective-permute-start | bytes 786440 | tf_op jit(solution)/shard_map/ppermute | solution.py:270
  41.3 9.3 %collective-permute-start.7 = (bf16[1024,128]{1,0:T(8,128)(2,1)S(1)}, bf16[1024,128]{1,0:T(8,128)(2,1)S(1)}, u32[]{:S(2)}, u32[]{:S(2)}) collective-permute-start(bf16[1024,128]{1,0:T(8,128)(2,1)S(1)} %bitcast.10), channel_id=1, source_target_pairs={{0,64},{8,72},{16,80},{24,88},{32,96},{40,104},{48,112},{56,120},{... | collective-permute-start | bytes 786440 | tf_op jit(solution)/shard_map/ppermute | solution.py:270
  46.4 4.2 %collective-permute-start.6 = (bf16[1024,128]{1,0:T(8,128)(2,1)S(1)}, bf16[1024,128]{1,0:T(8,128)(2,1)S(1)}, u32[]{:S(2)}, u32[]{:S(2)}) collective-permute-start(bf16[1024,128]{1,0:T(8,128)(2,1)S(1)} %collective-permute-done.2.rest_3_.rest_7_), channel_id=1, source_target_pairs={{0,8},{8,0},{16,24},{24,16},{32,40},{40,32},{48,56},{56,48},{64,72... | collective-permute-start | bytes 786440 | tf_op jit(solution)/shard_map/ppermute | solution.py:270
  46.4 4.2 %collective-permute-start.5 = (bf16[1024,128]{1,0:T(8,128)(2,1)S(1)}, bf16[1024,128]{1,0:T(8,128)(2,1)S(1)}, u32[]{:S(2)}, u32[]{:S(2)}) collective-permute-start(bf16[1024,128]{1,0:T(8,128)(2,1)S(1)} %collective-permute-done.1.rest_2_.rest_6_), channel_id=1, source_target_pairs={{0,8},{8,0},{16,24},{24,16},{32,40},{40,32},{48,56},{56,48},{64,72... | collective-permute-start | bytes 786440 | tf_op jit(solution)/shard_map/ppermute | solution.py:270
  46.9 3.7 %collective-permute-start.4 = (bf16[1024,128]{1,0:T(8,128)(2,1)S(1)}, bf16[1024,128]{1,0:T(8,128)(2,1)S(1)}, u32[]{:S(2)}, u32[]{:S(2)}) collective-permute-start(bf16[1024,128]{1,0:T(8,128)(2,1)S(1)} %collective-permute-done.rest_1_.rest_5_), channel_id=1, source_target_pairs={{0,8},{8,0},{16,24},{24,16},{32,40},{40,32},{48,56},{56,48},{64,72... | collective-permute-start | bytes 786440 | tf_op jit(solution)/shard_map/ppermute | solution.py:270
  56.5 5.7 %collective-permute-start.12 = (f32[3,32,128]{2,1,0:T(8,128)S(1)}, f32[3,32,128]{2,1,0:T(8,128)S(1)}, u32[]{:S(2)}, u32[]{:S(2)}) collective-permute-start(f32[3,32,128]{2,1,0:T(8,128)S(1)} %stats.1.rest_0_), channel_id=1, source_target_pairs={{0,128},{8,136},{16,144},{24,152},{32,160},{40,168},{48,176},{56,1... | collective-permute-start | bytes 147464 | tf_op jit(solution)/shard_map/ppermute | solution.py:270
  60.0 4.1 %collective-permute-start.11 = (f32[3,32,128]{2,1,0:T(8,128)S(1)}, f32[3,32,128]{2,1,0:T(8,128)S(1)}, u32[]{:S(2)}, u32[]{:S(2)}) collective-permute-start(f32[3,32,128]{2,1,0:T(8,128)S(1)} %stats.1.rest_0_), channel_id=1, source_target_pairs={{0,192},{8,200},{16,208},{24,216},{32,224},{40,232},{48,240},{56,2... | collective-permute-start | bytes 147464 | tf_op jit(solution)/shard_map/ppermute | solution.py:270
  60.0 5.3 %collective-permute-start.10 = (f32[3,32,128]{2,1,0:T(8,128)S(1)}, f32[3,32,128]{2,1,0:T(8,128)S(1)}, u32[]{:S(2)}, u32[]{:S(2)}) collective-permute-start(f32[3,32,128]{2,1,0:T(8,128)S(1)} %stats.1.rest_0_), channel_id=1, source_target_pairs={{0,64},{8,72},{16,80},{24,88},{32,96},{40,104},{48,112},{56,120},{... | collective-permute-start | bytes 147464 | tf_op jit(solution)/shard_map/ppermute | solution.py:270
  78.1 3.4 %collective-permute-start.13 = (bf16[32,128,128]{2,1,0:T(8,128)(2,1)S(1)}, bf16[32,128,128]{2,1,0:T(8,128)(2,1)S(1)}, u32[]{:S(2)}, u32[]{:S(2)}) collective-permute-start(bf16[32,128,128]{2,1,0:T(8,128)(2,1)S(1)} %get-tuple-element.29), channel_id=1, source_target_pairs={{0,8},{8,0},{16,24},{24,16},{32,40},{40,32},{48,56},{56,48},{64,72... | collective-permute-start | bytes 3145736 | tf_op jit(solution)/shard_map/ppermute | solution.py:270
  78.2 15.6 %collective-permute-start.17 = (bf16[8,128,128]{2,1,0:T(8,128)(2,1)S(1)}, bf16[8,128,128]{2,1,0:T(8,128)(2,1)S(1)}, u32[]{:S(2)}, u32[]{:S(2)}) collective-permute-start(bf16[8,128,128]{2,1,0:T(8,128)(2,1)S(1)} %get-tuple-element.35), channel_id=1, source_target_pairs={{0,64},{8,72},{16,80},{24,88},{32,96},{40,104},{48,112},{56,120},{... | collective-permute-start | bytes 786440 | tf_op jit(solution)/shard_map/ppermute | solution.py:270
  78.3 17.0 %collective-permute-start.18 = (bf16[8,128,128]{2,1,0:T(8,128)(2,1)S(1)}, bf16[8,128,128]{2,1,0:T(8,128)(2,1)S(1)}, u32[]{:S(2)}, u32[]{:S(2)}) collective-permute-start(bf16[8,128,128]{2,1,0:T(8,128)(2,1)S(1)} %get-tuple-element.36), channel_id=1, source_target_pairs={{0,192},{8,200},{16,208},{24,216},{32,224},{40,232},{48,240},{56,2... | collective-permute-start | bytes 786440 | tf_op jit(solution)/shard_map/ppermute | solution.py:270
  81.5 13.7 %collective-permute-start.19 = (bf16[8,128,128]{2,1,0:T(8,128)(2,1)S(1)}, bf16[8,128,128]{2,1,0:T(8,128)(2,1)S(1)}, u32[]{:S(2)}, u32[]{:S(2)}) collective-permute-start(bf16[8,128,128]{2,1,0:T(8,128)(2,1)S(1)} %get-tuple-element.37), channel_id=1, source_target_pairs={{0,128},{8,136},{16,144},{24,152},{32,160},{40,168},{48,176},{56,1... | collective-permute-start | bytes 786440 | tf_op jit(solution)/shard_map/ppermute | solution.py:270
  82.3 13.0 %collective-permute-start.14 = (bf16[8,128,128]{2,1,0:T(8,128)(2,1)S(1)}, bf16[8,128,128]{2,1,0:T(8,128)(2,1)S(1)}, u32[]{:S(2)}, u32[]{:S(2)}) collective-permute-start(bf16[8,128,128]{2,1,0:T(8,128)(2,1)S(1)} %get-tuple-element.31), channel_id=1, source_target_pairs={{0,16},{8,24},{16,32},{24,40},{32,48},{40,56},{48,0},{56,8},{64,80... | collective-permute-start | bytes 786440 | tf_op jit(solution)/shard_map/ppermute | solution.py:270
  84.1 11.1 %collective-permute-start.15 = (bf16[8,128,128]{2,1,0:T(8,128)(2,1)S(1)}, bf16[8,128,128]{2,1,0:T(8,128)(2,1)S(1)}, u32[]{:S(2)}, u32[]{:S(2)}) collective-permute-start(bf16[8,128,128]{2,1,0:T(8,128)(2,1)S(1)} %get-tuple-element.32), channel_id=1, source_target_pairs={{0,48},{8,56},{16,0},{24,8},{32,16},{40,24},{48,32},{56,40},{64,11... | collective-permute-start | bytes 786440 | tf_op jit(solution)/shard_map/ppermute | solution.py:270
  93.7 9.4 %collective-permute-start.16 = (bf16[8,128,128]{2,1,0:T(8,128)(2,1)S(1)}, bf16[8,128,128]{2,1,0:T(8,128)(2,1)S(1)}, u32[]{:S(2)}, u32[]{:S(2)}) collective-permute-start(bf16[8,128,128]{2,1,0:T(8,128)(2,1)S(1)} %get-tuple-element.33), channel_id=1, source_target_pairs={{0,32},{8,40},{16,48},{24,56},{32,0},{40,8},{48,16},{56,24},{64,96... | collective-permute-start | bytes 786440 | tf_op jit(solution)/shard_map/ppermute | solution.py:270
  103.1 19.6 %copy-start = (bf16[1024,512]{1,0:T(8,128)(2,1)S(1)}, bf16[1024,512]{1,0:T(8,128)(2,1)}, u32[]{:S(2)}) copy-start(bf16[1024,512]{1,0:T(8,128)(2,1)} %wk_ref.1) | copy-start | bytes 3145732
  103.1 19.6 %copy-start.1 = (bf16[1024,512]{1,0:T(8,128)(2,1)S(1)}, bf16[1024,512]{1,0:T(8,128)(2,1)}, u32[]{:S(2)}) copy-start(bf16[1024,512]{1,0:T(8,128)(2,1)} %wv_ref.1) | copy-start | bytes 3145732
  103.1 19.6 %copy-start.2 = (bf16[1024,512]{1,0:T(8,128)(2,1)S(1)}, bf16[1024,512]{1,0:T(8,128)(2,1)}, u32[]{:S(2)}) copy-start(bf16[1024,512]{1,0:T(8,128)(2,1)} %wq_ref.1) | copy-start | bytes 3145732
  103.1 19.6 %copy-start.3 = (bf16[512,1024]{1,0:T(8,128)(2,1)S(1)}, bf16[512,1024]{1,0:T(8,128)(2,1)}, u32[]{:S(2)}) copy-start(bf16[512,1024]{1,0:T(8,128)(2,1)} %wo_ref.1) | copy-start | bytes 3145732

commit v6 on v5

--- a/solution.py
+++ b/solution.py
@@ -167,11 +167,9 @@
 
 def grads_kernel(me_ref, pos_ref, cnt_ref, item_ref, *rest):
     stats, rest = rest[:LINE], rest[LINE:]
-    kv_pieces, qd_pieces, rest = rest[: 2 * LINE], rest[2 * LINE : 3 * LINE], rest[3 * LINE :]
+    kv_all, qd_all, rest = rest[0], rest[1], rest[2:]
     y_refs, rest = rest[:LINE], rest[LINE:]
-    own_ref, other_ref, kv_all, qd_all, key_ref, query_ref = rest[:6]
-    lse_ref, delta_ref, sems = rest[6:]
-    copies = load_lines(me_ref, kv_pieces, qd_pieces, kv_all, qd_all, sems)
+    own_ref, other_ref, key_ref, query_ref, lse_ref, delta_ref = rest
 
     top = functools.reduce(jnp.maximum, [s[0] for s in stats])
     weights = [jnp.exp(s[0] - top) for s in stats]
@@ -183,8 +181,6 @@
     query_ref[...] = jnp.zeros_like(query_ref)
     whole_end = Q_BLOCKS * GRADS_MOST
     half_end = whole_end + 1 + Q_BLOCKS
-    for copy in copies:
-        copy.wait()
 
     def run(base, amount, size, unroll):
         def step(n, carry):
@@ -315,11 +311,7 @@
     return lax.all_to_all(x, "head", split_axis=0, concat_axis=0, tiled=True)
 
 
-def scratch_lines():
-    return [
-        pltpu.VMEM((K_BLOCKS * BLOCK, WIDE), BF16),
-        pltpu.VMEM((Q_BLOCKS * BLOCK, WIDE), BF16),
-    ]
+LINES = (struct((K_BLOCKS * BLOCK, WIDE), BF16), struct((Q_BLOCKS * BLOCK, WIDE), BF16))
 
 
 def piece_sems():
@@ -332,24 +324,22 @@
 def stats_call(lists, kvs, qds):
     return call(
         stats_kernel,
-        struct((3, Q_BLOCKS, BLOCK), F32),
+        (struct((3, Q_BLOCKS, BLOCK), F32),) + LINES,
         [SMEM] * 4 + [VMEM] * (3 * LINE),
-        scratch_lines() + [piece_sems()],
+        [piece_sems()],
         "stats",
     )(*lists, *near(*kvs, *qds))
 
 
-def grads_call(lists, stats, kvs, qds):
+def grads_call(lists, stats, kv, qd):
     return call(
         grads_kernel,
         MIXED + [struct((LINE * OWN, BLOCK, WIDE), F32), struct((LINE * OWN, BLOCK, WIDE), BF16)],
-        [SMEM] * 4 + [VMEM] * (4 * LINE),
-        scratch_lines()
-        + [pltpu.VMEM((K_BLOCKS, BLOCK, WIDE), F32), pltpu.VMEM((Q_BLOCKS, BLOCK, WIDE), F32)]
-        + [pltpu.VMEM((Q_BLOCKS, BLOCK), F32)] * 2
-        + [piece_sems()],
+        [SMEM] * 4 + [VMEM] * (LINE + 2),
+        [pltpu.VMEM((K_BLOCKS, BLOCK, WIDE), F32), pltpu.VMEM((Q_BLOCKS, BLOCK, WIDE), F32)]
+        + [pltpu.VMEM((Q_BLOCKS, BLOCK), F32)] * 2,
         "grads",
-    )(*lists, *near(*stats, *kvs, *qds))
+    )(*lists, *near(*stats, kv, qd))
 
 
 def body(hits_in, w_query, w_key, w_value, w_out, grad_y, block_cell, cell_mask):
@@ -378,12 +368,18 @@
     kvs = kvs + [other] + [ctx_shift(piece, dc=1) for piece in kvs[1:]]
     qds = [qd] + [ctx_shift(qd, dy=hop) for hop in HOPS[1:]]
 
-    stats = stats_call((me, pos, cnt, tables[0]), kvs, qds)
+    stats, kv_lines, qd_lines = stats_call((me, pos, cnt, tables[0]), kvs, qds)
     all_stats = [stats] + [ctx_shift(stats, dy=hop) for hop in HOPS[1:]]
-    *y_parts, own, other = grads_call((me, pos, cnt, tables[1]), all_stats, kvs, qds)
+    *y_parts, own, other = grads_call(
+        (me, pos, cnt, tables[1]), all_stats, kv_lines, qd_lines
+    )
+    other = ctx_shift(other, dc=1)
+    x_parts = call(core_sum_kernel, MIXED, [SMEM, VMEM, VMEM], name="core_sum")(
+        me, *near(own, other)
+    )
+    x_parts = list(x_parts)
+    y_parts[3], x_parts[3] = lax.optimization_barrier((y_parts[3], x_parts[3]))
     y_parts = [y_parts[0]] + [ctx_shift(p, dy=hop) for p, hop in zip(y_parts[1:], HOPS[1:])]
-    other = ctx_shift(other, dc=1)
-    x_parts = call(core_sum_kernel, MIXED, [SMEM, VMEM, VMEM], name="core_sum")(me, *near(own, other))
     x_parts = [x_parts[0]] + [ctx_shift(p, dx=hop) for p, hop in zip(x_parts[1:], HOPS[1:])]
     summed = call(line_sum_kernel, struct(wide, BF16), [VMEM] * (2 * LINE), name="line_sum")(
         *near(*x_parts, *y_parts)

time: 126 us -> 124 us (0.984); the launches traced: 125 us -> 125 us
  waiting for transfers between devices: 41.8 us -> 43.3 us
    ppermute x20, waiting for transfers between devices: 29.4 us -> 30.9 us  [ctx_shift(): return lax.ppermute(x, 'ctx', pairs)]
  transfers between devices with their start and end apart: 21 -> 21, of which waited for: 9 -> 10; matrix products, arithmetic and copies ran while one was open for 4% -> 4% of each run, Pallas kernels for 1% -> 1%
where the time goes in v6:
time: 124 us; the launch traced here: 125 us
  waiting for transfers between devices  43.3 us (35%)
  starting transfers between devices  31.7 us (26%)
  Pallas kernels  24.6 us (20%)
  blocking collectives  19.4 us (16%)
  other arithmetic  4.27 us (3%)
    ppermute x20, waiting for transfers between devices, ctx_shift(): return lax.ppermute(x, 'ctx', pairs)  30.9 us
    ppermute x20, starting transfers between devices, ctx_shift(): return lax.ppermute(x, 'ctx', pairs)  23.2 us
    all_to_all x1, blocking collectives, exchange(): return lax.all_to_all(x, 'head', split_axis=0, concat_axis=0, tiled=True)  19.4 us
    all_to_all x1, waiting for transfers between devices, exchange(): return lax.all_to_all(x, 'head', split_axis=0, concat_axis=0, tiled=True)  12.4 us
    pallas_call x1, Pallas kernels, grads_call(): call(grads_kernel, MIXED + [struct((LINE * OWN, BLOCK, WIDE), F32), struc...  12.4 us
    all_to_all x1, starting transfers between devices, exchange(): return lax.all_to_all(x, 'head', split_axis=0, concat_axis=0, tiled=True)  8.48 us
    pallas_call x1, Pallas kernels, stats_call(): call(stats_kernel, (struct((3, Q_BLOCKS, BLOCK), F32),) + LINES, [SMEM] *...  5.35 us
    pallas_call x1, Pallas kernels, body(): call(project_kernel, struct(wide, BF16), [ANY] * 6, [pltpu.VMEM(g.shape,...  3.77 us
  transfers between devices with their start and end apart: 21, of which 10 were waited for; matrix products, arithmetic and copies ran while one was open for 4% of the time, Pallas kernels for 1%

profile of v6, /device:TPU:6, one launch (start us, length us, event | category | flops | bytes accessed | tf_op | source)
XLA Modules:
  0.0 124.8 jit_solution(15792202417077154235)
XLA Ops:
  0.7 3.8 %project.1 = bf16[8,256,128]{2,1,0:T(8,128)(2,1)} custom-call(bf16[128,1024]{1,0:T(8,128)(2,1)} %refs_0_.1, bf16[1024,512]{1,0:T(8,128)(2,1)} %wk_ref.1, bf16[1024,512]{1,0:T(8,128)(2,1)} %wv_ref.1, bf16[1024,512]{1,0:T(8,128)(2,1)} %wq_ref.1, bf16[128,1024]{1,0:T(8,128)(2,1)} %refs_4_.1, bf16[512,1024]{1,0:T(8,128)(2,1)} %wo_ref.1), custom_call_target="tpu_custom_call" | custom-call | tf_op jit(solution)/shard_map/project/pallas_call | solution.py:354
  4.4 8.5 %all-to-all-start = ((bf16[8,256,128]{2,1,0:T(8,128)(2,1)}), bf16[8,256,128]{2,1,0:T(8,128)(2,1)S(1)}, u32[]{:S(2)}, u32[]{:S(2)}) async-start(bf16[8,256,128]{2,1,0:T(8,128)(2,1)} %project.1), calls=%async_computation | async-start | bytes 1048576 | tf_op jit(solution)/shard_map/all_to_all | solution.py:311
  13.7 0.8 fusion.9
  14.9 1.2 pad_add_fusion.1.item_ref
  16.4 0.7 pad_add_fusion.item_ref
  17.3 0.7 select_reduce_fusion.1.pos_ref
  18.0 12.4 %all-to-all-done = bf16[8,256,128]{2,1,0:T(8,128)(2,1)S(1)} async-done(((bf16[8,256,128]{2,1,0:T(8,128)(2,1)}), bf16[8,256,128]{2,1,0:T(8,128)(2,1)S(1)}, u32[]{:S(2)}, u32[]{:S(2)}) %all-to-all-start) | async-done | bytes 524320 | tf_op jit(solution)/shard_map/all_to_all | solution.py:311
  30.5 1.5 %collective-permute-start.2 = (bf16[1024,128]{1,0:T(8,128)(2,1)S(1)}, bf16[1024,128]{1,0:T(8,128)(2,1)S(1)}, u32[]{:S(2)}, u32[]{:S(2)}) collective-permute-start(bf16[1024,128]{1,0:T(8,128)(2,1)S(1)} %bitcast.13), channel_id=1, source_target_pairs={{0,32},{8,40},{16,48},{24,56},{32,0},{40,8},{48,16},{56,24},{64,96... | collective-permute-start | bytes 786440 | tf_op jit(solution)/shard_map/ppermute | solution.py:266
  32.0 3.2 %collective-permute-start = (bf16[1024,128]{1,0:T(8,128)(2,1)S(1)}, bf16[1024,128]{1,0:T(8,128)(2,1)S(1)}, u32[]{:S(2)}, u32[]{:S(2)}) collective-permute-start(bf16[1024,128]{1,0:T(8,128)(2,1)S(1)} %bitcast.15), channel_id=1, source_target_pairs={{0,16},{8,24},{16,32},{24,40},{32,48},{40,56},{48,0},{56,8},{64,80... | collective-permute-start | bytes 786440 | tf_op jit(solution)/shard_map/ppermute | solution.py:266
  35.3 3.2 %collective-permute-start.9 = (bf16[1024,128]{1,0:T(8,128)(2,1)S(1)}, bf16[1024,128]{1,0:T(8,128)(2,1)S(1)}, u32[]{:S(2)}, u32[]{:S(2)}) collective-permute-start(bf16[1024,128]{1,0:T(8,128)(2,1)S(1)} %bitcast.8), channel_id=1, source_target_pairs={{0,128},{8,136},{16,144},{24,152},{32,160},{40,168},{48,176},{56,1... | collective-permute-start | bytes 786440 | tf_op jit(solution)/shard_map/ppermute | solution.py:266
  38.5 1.1 collective-permute-start.8
  39.5 1.8 %collective-permute-done.2.rest_3_ = bf16[1024,128]{1,0:T(8,128)(2,1)S(1)} collective-permute-done((bf16[1024,128]{1,0:T(8,128)(2,1)S(1)}, bf16[1024,128]{1,0:T(8,128)(2,1)S(1)}, u32[]{:S(2)}, u32[]{:S(2)}) %collective-permute-start.2) | collective-permute-done | bytes 262176 | tf_op jit(solution)/shard_map/ppermute | solution.py:266
  41.3 1.6 %collective-permute-start.7 = (bf16[1024,128]{1,0:T(8,128)(2,1)S(1)}, bf16[1024,128]{1,0:T(8,128)(2,1)S(1)}, u32[]{:S(2)}, u32[]{:S(2)}) collective-permute-start(bf16[1024,128]{1,0:T(8,128)(2,1)S(1)} %bitcast.10), channel_id=1, source_target_pairs={{0,64},{8,72},{16,80},{24,88},{32,96},{40,104},{48,112},{56,120},{... | collective-permute-start | bytes 786440 | tf_op jit(solution)/shard_map/ppermute | solution.py:266
  42.9 3.5 %collective-permute-done.1.rest_2_ = bf16[1024,128]{1,0:T(8,128)(2,1)S(1)} collective-permute-done((bf16[1024,128]{1,0:T(8,128)(2,1)S(1)}, bf16[1024,128]{1,0:T(8,128)(2,1)S(1)}, u32[]{:S(2)}, u32[]{:S(2)}) %collective-permute-start.1) | collective-permute-done | bytes 262176 | tf_op jit(solution)/shard_map/ppermute | solution.py:266
  47.0 3.6 %collective-permute-done.8.rest_10_ = bf16[1024,128]{1,0:T(8,128)(2,1)S(1)} collective-permute-done((bf16[1024,128]{1,0:T(8,128)(2,1)S(1)}, bf16[1024,128]{1,0:T(8,128)(2,1)S(1)}, u32[]{:S(2)}, u32[]{:S(2)}) %collective-permute-start.8) | collective-permute-done | bytes 262176 | tf_op jit(solution)/shard_map/ppermute | solution.py:266
  50.6 5.3 %stats.1 = (f32[3,32,128]{2,1,0:T(8,128)S(1)}, bf16[8192,128]{1,0:T(8,128)(2,1)S(1)}, bf16[4096,128]{1,0:T(8,128)(2,1)S(1)}) custom-call(s32[3]{0:T(128)S(1)} %pad_add_fusion.2.me_ref, s32[32,24]{1,0:T(8,128)S(1)} %select_reduce_fusion.1.pos_ref, s32[32]{0:T(128)S(1)} %convert_element_type.63.cnt_ref, s32[353]{0:T(512)S(1)} %pad_add_fusion.item_ref, ...), custom_call_target="tpu_custom_call" | custom-call | tf_op jit(solution)/shard_map/stats/pallas_call | solution.py:325
  56.0 3.5 %collective-permute-start.12 = (f32[3,32,128]{2,1,0:T(8,128)S(1)}, f32[3,32,128]{2,1,0:T(8,128)S(1)}, u32[]{:S(2)}, u32[]{:S(2)}) collective-permute-start(f32[3,32,128]{2,1,0:T(8,128)S(1)} %get-tuple-element.33.rest_0_), channel_id=1, source_target_pairs={{0,128},{8,136},{16,144},{24,152},{32,160},{40,168},{48,176},{56,1... | collective-permute-start | bytes 147464 | tf_op jit(solution)/shard_map/ppermute | solution.py:266
  59.4 1.2 collective-permute-start.11
  60.6 0.9 collective-permute-start.10
  61.6 1.9 %collective-permute-done.11.rest_2_ = f32[3,32,128]{2,1,0:T(8,128)S(1)} collective-permute-done((f32[3,32,128]{2,1,0:T(8,128)S(1)}, f32[3,32,128]{2,1,0:T(8,128)S(1)}, u32[]{:S(2)}, u32[]{:S(2)}) %collective-permute-start.11) | collective-permute-done | bytes 49184 | tf_op jit(solution)/shard_map/ppermute | solution.py:266
  63.5 2.5 %collective-permute-done.10.rest_1_ = f32[3,32,128]{2,1,0:T(8,128)S(1)} collective-permute-done((f32[3,32,128]{2,1,0:T(8,128)S(1)}, f32[3,32,128]{2,1,0:T(8,128)S(1)}, u32[]{:S(2)}, u32[]{:S(2)}) %collective-permute-start.10) | collective-permute-done | bytes 49184 | tf_op jit(solution)/shard_map/ppermute | solution.py:266
  66.0 12.4 %grads.1 = (f32[8,128,128]{2,1,0:T(8,128)S(1)}, bf16[8,128,128]{2,1,0:T(8,128)(2,1)S(1)}, bf16[8,128,128]{2,1,0:T(8,128)(2,1)S(1)}, bf16[8,128,128]{2,1,0:T(8,12...) custom-call(s32[3]{0:T(128)S(1)} %pad_add_fusion.2.me_ref, ...), custom_call_target="tpu_custom_call" | custom-call | tf_op jit(solution)/shard_map/grads/pallas_call | solution.py:335
  78.5 0.9 collective-permute-start.17
  79.4 2.4 %collective-permute-start.18 = (bf16[8,128,128]{2,1,0:T(8,128)(2,1)S(1)}, bf16[8,128,128]{2,1,0:T(8,128)(2,1)S(1)}, u32[]{:S(2)}, u32[]{:S(2)}) collective-permute-start(bf16[8,128,128]{2,1,0:T(8,128)(2,1)S(1)} %get-tuple-element.46), channel_id=1, source_target_pairs={{0,192},{8,200},{16,208},{24,216},{32,224},{40,232},{48,240},{56,2... | collective-permute-start | bytes 786440 | tf_op jit(solution)/shard_map/ppermute | solution.py:266
  81.8 0.8 core_sum.1
  82.6 0.9 collective-permute-start.16
  83.7 1.8 %collective-permute-start.14 = (bf16[8,128,128]{2,1,0:T(8,128)(2,1)S(1)}, bf16[8,128,128]{2,1,0:T(8,128)(2,1)S(1)}, u32[]{:S(2)}, u32[]{:S(2)}) collective-permute-start(bf16[8,128,128]{2,1,0:T(8,128)(2,1)S(1)} %get-tuple-element.39), channel_id=1, source_target_pairs={{0,16},{8,24},{16,32},{24,40},{32,48},{40,56},{48,0},{56,8},{64,80... | collective-permute-start | bytes 786440 | tf_op jit(solution)/shard_map/ppermute | solution.py:266
  85.5 8.6 %collective-permute-done.17.refs_5_ = bf16[8,128,128]{2,1,0:T(8,128)(2,1)S(1)} collective-permute-done((bf16[8,128,128]{2,1,0:T(8,128)(2,1)S(1)}, bf16[8,128,128]{2,1,0:T(8,128)(2,1)S(1)}, u32[]{:S(2)}, u32[]{:S(2)}) %collective-permute-start.17) | collective-permute-done | bytes 262176 | tf_op jit(solution)/shard_map/ppermute | solution.py:266
  94.2 1.9 %collective-permute-done.14.refs_1_ = bf16[8,128,128]{2,1,0:T(8,128)(2,1)S(1)} collective-permute-done((bf16[8,128,128]{2,1,0:T(8,128)(2,1)S(1)}, bf16[8,128,128]{2,1,0:T(8,128)(2,1)S(1)}, u32[]{:S(2)}, u32[]{:S(2)}) %collective-permute-start.14) | collective-permute-done | bytes 262176 | tf_op jit(solution)/shard_map/ppermute | solution.py:266
  96.0 7.1 %collective-permute-done.15.refs_2_ = bf16[8,128,128]{2,1,0:T(8,128)(2,1)S(1)} collective-permute-done((bf16[8,128,128]{2,1,0:T(8,128)(2,1)S(1)}, bf16[8,128,128]{2,1,0:T(8,128)(2,1)S(1)}, u32[]{:S(2)}, u32[]{:S(2)}) %collective-permute-start.15) | collective-permute-done | bytes 262176 | tf_op jit(solution)/shard_map/ppermute | solution.py:266
  103.4 19.4 %all_to_all.10.in_ref = bf16[8,256,128]{2,1,0:T(8,128)(2,1)S(1)} all-to-all(bf16[8,256,128]{2,1,0:T(8,128)(2,1)S(1)} %line_sum.1), channel_id=1, replica_groups=mesh['ctx'=32,'head'=8] {'head'}, dimensions={0} | all-to-all | bytes 1048576 | tf_op jit(solution)/shard_map/all_to_all | solution.py:311
  122.7 2.0 %output.1 = (bf16[128,1024]{1,0:T(8,128)(2,1)}, bf16[128,1024]{1,0:T(8,128)(2,1)}) custom-call(bf16[8,256,128]{2,1,0:T(8,128)(2,1)S(1)} %all_to_all.10.in_ref, bf16[1024,512]{1,0:T(8,128)(2,1)S(1)} %copy-done.2, bf16[1024,512]{1,0:T(8,128)(2,1)S(1)} %copy-done, bf16[1024,512]{1,0:T(8,128)(2,1)S(1)} %copy-done.1, bf16[512,1024]{1,0:T(8,128)(2,1)S(1)} %copy-done.3), custom_call_target="tpu_custom_call" | custom-call | tf_op jit(solution)/shard_map/output/pallas_call | solution.py:388
  (55 shorter events, 3.2 us)
Async XLA Ops:
  0.6 12.3 %copy-start.5 = (s32[256]{0:T(256)S(1)}, s32[256]{0:T(256)}, u32[]{:S(2)}) copy-start(s32[256]{0:T(256)} %param.14) | copy-start | bytes 3076
  0.6 12.6 %copy-start.4 = (s32[256,256]{1,0:T(8,128)S(1)}, s32[256,256]{1,0:T(8,128)}, u32[]{:S(2)}) copy-start(s32[256,256]{1,0:T(8,128)} %param.15) | copy-start | bytes 786436
  4.4 26.0 %all-to-all-start = ((bf16[8,256,128]{2,1,0:T(8,128)(2,1)}), bf16[8,256,128]{2,1,0:T(8,128)(2,1)S(1)}, u32[]{:S(2)}, u32[]{:S(2)}) async-start(bf16[8,256,128]{2,1,0:T(8,128)(2,1)} %project.1), calls=%async_computation | async-start | bytes 1048576 | tf_op jit(solution)/shard_map/all_to_all | solution.py:311
  30.4 4.8 %collective-permute-start.3 = (bf16[1024,128]{1,0:T(8,128)(2,1)S(1)}, bf16[1024,128]{1,0:T(8,128)(2,1)S(1)}, u32[]{:S(2)}, u32[]{:S(2)}) collective-permute-start(bf16[1024,128]{1,0:T(8,128)(2,1)S(1)} %bitcast.12), channel_id=1, source_target_pairs={{0,8},{8,0},{16,24},{24,16},{32,40},{40,32},{48,56},{56,48},{64,72... | collective-permute-start | bytes 786440 | tf_op jit(solution)/shard_map/ppermute | solution.py:266
  30.5 10.7 %collective-permute-start.2 = (bf16[1024,128]{1,0:T(8,128)(2,1)S(1)}, bf16[1024,128]{1,0:T(8,128)(2,1)S(1)}, u32[]{:S(2)}, u32[]{:S(2)}) collective-permute-start(bf16[1024,128]{1,0:T(8,128)(2,1)S(1)} %bitcast.13), channel_id=1, source_target_pairs={{0,32},{8,40},{16,48},{24,56},{32,0},{40,8},{48,16},{56,24},{64,96... | collective-permute-start | bytes 786440 | tf_op jit(solution)/shard_map/ppermute | solution.py:266
  32.0 14.4 %collective-permute-start.1 = (bf16[1024,128]{1,0:T(8,128)(2,1)S(1)}, bf16[1024,128]{1,0:T(8,128)(2,1)S(1)}, u32[]{:S(2)}, u32[]{:S(2)}) collective-permute-start(bf16[1024,128]{1,0:T(8,128)(2,1)S(1)} %bitcast.14), channel_id=1, source_target_pairs={{0,48},{8,56},{16,0},{24,8},{32,16},{40,24},{48,32},{56,40},{64,11... | collective-permute-start | bytes 786440 | tf_op jit(solution)/shard_map/ppermute | solution.py:266
  32.0 14.4 %collective-permute-start = (bf16[1024,128]{1,0:T(8,128)(2,1)S(1)}, bf16[1024,128]{1,0:T(8,128)(2,1)S(1)}, u32[]{:S(2)}, u32[]{:S(2)}) collective-permute-start(bf16[1024,128]{1,0:T(8,128)(2,1)S(1)} %bitcast.15), channel_id=1, source_target_pairs={{0,16},{8,24},{16,32},{24,40},{32,48},{40,56},{48,0},{56,8},{64,80... | collective-permute-start | bytes 786440 | tf_op jit(solution)/shard_map/ppermute | solution.py:266
  35.3 11.6 %collective-permute-start.9 = (bf16[1024,128]{1,0:T(8,128)(2,1)S(1)}, bf16[1024,128]{1,0:T(8,128)(2,1)S(1)}, u32[]{:S(2)}, u32[]{:S(2)}) collective-permute-start(bf16[1024,128]{1,0:T(8,128)(2,1)S(1)} %bitcast.8), channel_id=1, source_target_pairs={{0,128},{8,136},{16,144},{24,152},{32,160},{40,168},{48,176},{56,1... | collective-permute-start | bytes 786440 | tf_op jit(solution)/shard_map/ppermute | solution.py:266
  38.5 12.1 %collective-permute-start.8 = (bf16[1024,128]{1,0:T(8,128)(2,1)S(1)}, bf16[1024,128]{1,0:T(8,128)(2,1)S(1)}, u32[]{:S(2)}, u32[]{:S(2)}) collective-permute-start(bf16[1024,128]{1,0:T(8,128)(2,1)S(1)} %bitcast.9), channel_id=1, source_target_pairs={{0,192},{8,200},{16,208},{24,216},{32,224},{40,232},{48,240},{56,2... | collective-permute-start | bytes 786440 | tf_op jit(solution)/shard_map/ppermute | solution.py:266
  41.3 9.3 %collective-permute-start.7 = (bf16[1024,128]{1,0:T(8,128)(2,1)S(1)}, bf16[1024,128]{1,0:T(8,128)(2,1)S(1)}, u32[]{:S(2)}, u32[]{:S(2)}) collective-permute-start(bf16[1024,128]{1,0:T(8,128)(2,1)S(1)} %bitcast.10), channel_id=1, source_target_pairs={{0,64},{8,72},{16,80},{24,88},{32,96},{40,104},{48,112},{56,120},{... | collective-permute-start | bytes 786440 | tf_op jit(solution)/shard_map/ppermute | solution.py:266
  46.4 4.2 %collective-permute-start.6 = (bf16[1024,128]{1,0:T(8,128)(2,1)S(1)}, bf16[1024,128]{1,0:T(8,128)(2,1)S(1)}, u32[]{:S(2)}, u32[]{:S(2)}) collective-permute-start(bf16[1024,128]{1,0:T(8,128)(2,1)S(1)} %collective-permute-done.2.rest_3_), channel_id=1, source_target_pairs={{0,8},{8,0},{16,24},{24,16},{32,40},{40,32},{48,56},{56,48},{64,72... | collective-permute-start | bytes 786440 | tf_op jit(solution)/shard_map/ppermute | solution.py:266
  46.4 4.2 %collective-permute-start.5 = (bf16[1024,128]{1,0:T(8,128)(2,1)S(1)}, bf16[1024,128]{1,0:T(8,128)(2,1)S(1)}, u32[]{:S(2)}, u32[]{:S(2)}) collective-permute-start(bf16[1024,128]{1,0:T(8,128)(2,1)S(1)} %collective-permute-done.1.rest_2_), channel_id=1, source_target_pairs={{0,8},{8,0},{16,24},{24,16},{32,40},{40,32},{48,56},{56,48},{64,72... | collective-permute-start | bytes 786440 | tf_op jit(solution)/shard_map/ppermute | solution.py:266
  46.9 3.7 %collective-permute-start.4 = (bf16[1024,128]{1,0:T(8,128)(2,1)S(1)}, bf16[1024,128]{1,0:T(8,128)(2,1)S(1)}, u32[]{:S(2)}, u32[]{:S(2)}) collective-permute-start(bf16[1024,128]{1,0:T(8,128)(2,1)S(1)} %collective-permute-done.rest_1_), channel_id=1, source_target_pairs={{0,8},{8,0},{16,24},{24,16},{32,40},{40,32},{48,56},{56,48},{64,72... | collective-permute-start | bytes 786440 | tf_op jit(solution)/shard_map/ppermute | solution.py:266
  56.0 5.7 %collective-permute-start.12 = (f32[3,32,128]{2,1,0:T(8,128)S(1)}, f32[3,32,128]{2,1,0:T(8,128)S(1)}, u32[]{:S(2)}, u32[]{:S(2)}) collective-permute-start(f32[3,32,128]{2,1,0:T(8,128)S(1)} %get-tuple-element.33.rest_0_), channel_id=1, source_target_pairs={{0,128},{8,136},{16,144},{24,152},{32,160},{40,168},{48,176},{56,1... | collective-permute-start | bytes 147464 | tf_op jit(solution)/shard_map/ppermute | solution.py:266
  59.4 4.1 %collective-permute-start.11 = (f32[3,32,128]{2,1,0:T(8,128)S(1)}, f32[3,32,128]{2,1,0:T(8,128)S(1)}, u32[]{:S(2)}, u32[]{:S(2)}) collective-permute-start(f32[3,32,128]{2,1,0:T(8,128)S(1)} %get-tuple-element.33.rest_0_), channel_id=1, source_target_pairs={{0,192},{8,200},{16,208},{24,216},{32,224},{40,232},{48,240},{56,2... | collective-permute-start | bytes 147464 | tf_op jit(solution)/shard_map/ppermute | solution.py:266
  60.6 5.4 %collective-permute-start.10 = (f32[3,32,128]{2,1,0:T(8,128)S(1)}, f32[3,32,128]{2,1,0:T(8,128)S(1)}, u32[]{:S(2)}, u32[]{:S(2)}) collective-permute-start(f32[3,32,128]{2,1,0:T(8,128)S(1)} %get-tuple-element.33.rest_0_), channel_id=1, source_target_pairs={{0,64},{8,72},{16,80},{24,88},{32,96},{40,104},{48,112},{56,120},{... | collective-permute-start | bytes 147464 | tf_op jit(solution)/shard_map/ppermute | solution.py:266
  78.4 3.4 %collective-permute-start.13 = (bf16[32,128,128]{2,1,0:T(8,128)(2,1)S(1)}, bf16[32,128,128]{2,1,0:T(8,128)(2,1)S(1)}, u32[]{:S(2)}, u32[]{:S(2)}) collective-permute-start(bf16[32,128,128]{2,1,0:T(8,128)(2,1)S(1)} %get-tuple-element.37), channel_id=1, source_target_pairs={{0,8},{8,0},{16,24},{24,16},{32,40},{40,32},{48,56},{56,48},{64,72... | collective-permute-start | bytes 3145736 | tf_op jit(solution)/shard_map/ppermute | solution.py:266
  78.5 15.6 %collective-permute-start.17 = (bf16[8,128,128]{2,1,0:T(8,128)(2,1)S(1)}, bf16[8,128,128]{2,1,0:T(8,128)(2,1)S(1)}, u32[]{:S(2)}, u32[]{:S(2)}) collective-permute-start(bf16[8,128,128]{2,1,0:T(8,128)(2,1)S(1)} %get-tuple-element.45), channel_id=1, source_target_pairs={{0,64},{8,72},{16,80},{24,88},{32,96},{40,104},{48,112},{56,120},{... | collective-permute-start | bytes 786440 | tf_op jit(solution)/shard_map/ppermute | solution.py:266
  79.4 14.8 %collective-permute-start.18 = (bf16[8,128,128]{2,1,0:T(8,128)(2,1)S(1)}, bf16[8,128,128]{2,1,0:T(8,128)(2,1)S(1)}, u32[]{:S(2)}, u32[]{:S(2)}) collective-permute-start(bf16[8,128,128]{2,1,0:T(8,128)(2,1)S(1)} %get-tuple-element.46), channel_id=1, source_target_pairs={{0,192},{8,200},{16,208},{24,216},{32,224},{40,232},{48,240},{56,2... | collective-permute-start | bytes 786440 | tf_op jit(solution)/shard_map/ppermute | solution.py:266
  82.6 11.6 %collective-permute-start.16 = (bf16[8,128,128]{2,1,0:T(8,128)(2,1)S(1)}, bf16[8,128,128]{2,1,0:T(8,128)(2,1)S(1)}, u32[]{:S(2)}, u32[]{:S(2)}) collective-permute-start(bf16[8,128,128]{2,1,0:T(8,128)(2,1)S(1)} %get-tuple-element.43), channel_id=1, source_target_pairs={{0,32},{8,40},{16,48},{24,56},{32,0},{40,8},{48,16},{56,24},{64,96... | collective-permute-start | bytes 786440 | tf_op jit(solution)/shard_map/ppermute | solution.py:266
  83.5 10.7 %collective-permute-start.19 = (bf16[8,128,128]{2,1,0:T(8,128)(2,1)S(1)}, bf16[8,128,128]{2,1,0:T(8,128)(2,1)S(1)}, u32[]{:S(2)}, u32[]{:S(2)}) collective-permute-start(bf16[8,128,128]{2,1,0:T(8,128)(2,1)S(1)} %get-tuple-element.47), channel_id=1, source_target_pairs={{0,128},{8,136},{16,144},{24,152},{32,160},{40,168},{48,176},{56,1... | collective-permute-start | bytes 786440 | tf_op jit(solution)/shard_map/ppermute | solution.py:266
  83.7 12.4 %collective-permute-start.14 = (bf16[8,128,128]{2,1,0:T(8,128)(2,1)S(1)}, bf16[8,128,128]{2,1,0:T(8,128)(2,1)S(1)}, u32[]{:S(2)}, u32[]{:S(2)}) collective-permute-start(bf16[8,128,128]{2,1,0:T(8,128)(2,1)S(1)} %get-tuple-element.39), channel_id=1, source_target_pairs={{0,16},{8,24},{16,32},{24,40},{32,48},{40,56},{48,0},{56,8},{64,80... | collective-permute-start | bytes 786440 | tf_op jit(solution)/shard_map/ppermute | solution.py:266
  94.0 9.1 %collective-permute-start.15 = (bf16[8,128,128]{2,1,0:T(8,128)(2,1)S(1)}, bf16[8,128,128]{2,1,0:T(8,128)(2,1)S(1)}, u32[]{:S(2)}, u32[]{:S(2)}) collective-permute-start(bf16[8,128,128]{2,1,0:T(8,128)(2,1)S(1)} %get-tuple-element.40), channel_id=1, source_target_pairs={{0,48},{8,56},{16,0},{24,8},{32,16},{40,24},{48,32},{56,40},{64,11... | collective-permute-start | bytes 786440 | tf_op jit(solution)/shard_map/ppermute | solution.py:266
  103.1 19.6 %copy-start = (bf16[1024,512]{1,0:T(8,128)(2,1)S(1)}, bf16[1024,512]{1,0:T(8,128)(2,1)}, u32[]{:S(2)}) copy-start(bf16[1024,512]{1,0:T(8,128)(2,1)} %wk_ref.1) | copy-start | bytes 3145732
  103.1 19.6 %copy-start.1 = (bf16[1024,512]{1,0:T(8,128)(2,1)S(1)}, bf16[1024,512]{1,0:T(8,128)(2,1)}, u32[]{:S(2)}) copy-start(bf16[1024,512]{1,0:T(8,128)(2,1)} %wv_ref.1) | copy-start | bytes 3145732
  103.1 19.6 %copy-start.2 = (bf16[1024,512]{1,0:T(8,128)(2,1)S(1)}, bf16[1024,512]{1,0:T(8,128)(2,1)}, u32[]{:S(2)}) copy-start(bf16[1024,512]{1,0:T(8,128)(2,1)} %wq_ref.1) | copy-start | bytes 3145732
  103.1 19.6 %copy-start.3 = (bf16[512,1024]{1,0:T(8,128)(2,1)S(1)}, bf16[512,1024]{1,0:T(8,128)(2,1)}, u32[]{:S(2)}) copy-start(bf16[512,1024]{1,0:T(8,128)(2,1)} %wo_ref.1) | copy-start | bytes 3145732
